TPU v7x, 128 devices: a whole 4x4x4 slice. The times are simulated.
128 devices in a mesh: member: 8 (over y, core), lat: 16 (over x, z).
Axes of the slice: x: 4, y: 4, z: 4, core: 2. Of those that a mesh axis runs over, the one named last changes fastest.
Arguments:
- ensemble: float32 [640, 64, 1024], P('member', 'lat'), may hold values from -6 to 6
- obs_cell: int32 [128, 128], P(('member', 'lat')), may hold values from 0 to 511
- obs_value: float32 [128, 128], P(('member', 'lat')), may hold values from -8 to 8
- obs_var: float32 [128, 128], P(('member', 'lat')), may hold values from 0.5 to 8
- patch_rows: int32 [128, 2], P(('member', 'lat')), may hold values from 1 to 48, 64 in all within a row
Outputs:
- analysis: float32 [640, 64, 1024], P('member', 'lat')
Inputs may be any that keep to these rules, and one draw needn't show every extreme that they name: `patch_rows`: each server's 2 patch lengths sum to 64.
All inputs are finite; a program needn't handle non-finite values. Where the computation divides by a largest or mean magnitude, that divisor is 1e-20 or more.
Results may differ from a plain program's by a relative error of at most 0.0003.
Values sent between devices are 32-bit elements; how exact they have to be, the bound alone decides.
No kernel may reach another device: no remote copies, remote signals or barrier semaphores. Data moves between devices by JAX's collectives and lax.ppermute only.
A program may use at most 64 MiB of HBM per device.

v0:
```python
import jax
import jax.numpy as jnp
from jax import lax
from jax.sharding import PartitionSpec as P

NS_ITERS = 3
STEPS = 4


lat_coeff = 0.4
lon_coeff = 0.05
advect_coeff = 0.1


def with_halo(value, sides, width, wrap):
    for axis, dim in sides:
        size, length = (lax.axis_size(axis), value.shape[dim])
        up = [(i, (i + 1) % size) for i in range(size if wrap else size - 1)]
        down = [(j, i) for i, j in up]
        last = lax.slice_in_dim(value, length - width, length, axis=dim)
        initial = lax.slice_in_dim(value, 0, width, axis=dim)
        before = lax.ppermute(last, axis, up)
        after = lax.ppermute(initial, axis, down)
        value = jnp.concatenate([before, value, after], axis=dim)
    return value


def cut_along(value, dim, length):
    shape = value.shape
    parts = value.reshape(*shape[:dim], length, shape[dim] // length, *shape[dim + 1 :])
    return jnp.moveaxis(parts, dim, 0)


def in_order(parts, dim):
    shape = list(parts.shape[1:])
    shape[dim] *= parts.shape[0]
    return jnp.moveaxis(parts, 0, dim).reshape(shape)


def joined_exchange(value, axis, axes, splits, concats):
    sizes = [lax.axis_size(a) for a in axes]
    parts = cut_along(value, splits[0], sizes[0])
    parts = jnp.moveaxis(cut_along(parts, splits[1] + 1, sizes[1]), 0, 1)
    inside = parts.shape[2:]
    parts = parts.reshape(-1, *inside)
    parts = lax.all_to_all(parts, axis, split_axis=0, concat_axis=0, tiled=True)
    parts = in_order(parts.reshape(*sizes, *inside), concats[0] + 1)
    return in_order(parts, concats[1])


def matmul(left, right):
    return jnp.dot(left, right, precision=lax.Precision.HIGHEST, preferred_element_type=jnp.float32)


def advance(padded):
    centre = padded[:, 1:-1]
    northern = padded[:, :-2]
    southern = padded[:, 2:]
    eastern = jnp.roll(centre, -1, axis=2)
    western = jnp.roll(centre, 1, axis=2)
    return (
        centre
        + lat_coeff * (northern + southern - 2.0 * centre)
        + lon_coeff * (eastern + western - 2.0 * centre)
        - advect_coeff * centre * (eastern - western)
    )


def observe(states, cell_index, values):
    observed = jnp.take(states, cell_index, axis=1)
    obs_mean = jnp.mean(observed, axis=0)
    return (observed - obs_mean, values - obs_mean)


def localize(obs_rows, rel_cols, first_row, row_count, lat_scale, width_cols):
    lower = first_row.astype(jnp.float32)
    upper = lower + row_count.astype(jnp.float32) - 1.0
    lat_gap = jnp.maximum(jnp.maximum(lower - obs_rows, obs_rows - upper), 0.0) / lat_scale
    lon_gap = jnp.maximum(jnp.maximum(-rel_cols, rel_cols - (width_cols - 1.0)), 0.0) / width_cols
    return jnp.exp(-lat_gap * lat_gap - lon_gap * lon_gap)


def inverse_root(gram_matrix):
    bound = jnp.max(jnp.sum(jnp.abs(gram_matrix), axis=1))
    identity = jnp.eye(gram_matrix.shape[0], dtype=jnp.float32)
    iterate = gram_matrix / bound
    result = identity
    for turn_index in range(NS_ITERS):
        middle = 1.5 * identity - 0.5 * matmul(result, iterate)
        result = matmul(middle, result)
        if turn_index + 1 < NS_ITERS:
            iterate = matmul(iterate, middle)
    return result / jnp.sqrt(bound)


def analyse(states, spread, obs_meta, lengths, width_cols):
    members = states.shape[0]
    cell_total = states.shape[1]
    lat_total = cell_total // width_cols
    state_mean = jnp.mean(states, axis=0)
    anomaly = states - state_mean
    starts = jnp.cumsum(lengths) - lengths
    cell_rows = jnp.arange(cell_total, dtype=jnp.int32) // width_cols
    identity = jnp.eye(members, dtype=jnp.float32)
    result = jnp.broadcast_to(state_mean, states.shape)
    for patch in range(lengths.shape[0]):
        weights = (
            localize(
                obs_meta[2],
                obs_meta[3],
                starts[patch],
                lengths[patch],
                lat_total / 4.0,
                float(width_cols),
            )
            / obs_meta[1]
        )
        weighted = spread * weights
        gram_matrix = (members - 1.0) * identity + matmul(weighted, spread.T)
        root = inverse_root(gram_matrix)
        drive = matmul(weighted, obs_meta[0])
        mean_weights = matmul(root, matmul(root, drive))
        transform = jnp.sqrt(members - 1.0) * root + mean_weights[:, None]
        update = matmul(transform.T, anomaly)
        cell_mask = (cell_rows >= starts[patch]) & (cell_rows < starts[patch] + lengths[patch])
        result = result + jnp.where(cell_mask[None, :], update, 0.0)
    return result


def per_device(ensemble, obs_cell, obs_value, obs_var, patch_rows):
    fields = ensemble
    members_dev = fields.shape[0]
    lat_rows = fields.shape[1]
    lon_cells = fields.shape[2]
    lat_count = lax.axis_size("lat")
    member_count = lax.axis_size("member")
    servers = lat_count * member_count
    width_cols = lon_cells // servers
    padded = with_halo(fields, (("lat", 1),), STEPS, False)
    global_rows = (
        lax.axis_index("lat") * lat_rows + jnp.arange(lat_rows + 2 * STEPS, dtype=jnp.int32) - STEPS
    )
    inside = ((global_rows >= 0) & (global_rows < lat_rows * lat_count)).astype(jnp.float32)
    for step_index in range(STEPS):
        padded = advance(padded)
        keeper = inside[step_index + 1 : inside.shape[0] - step_index - 1]
        padded = padded * keeper[None, :, None]
    fields = padded
    strip = joined_exchange(fields, ("member", "lat"), ("member", "lat"), (2, 2), (0, 1))
    members = strip.shape[0]
    lat_total = strip.shape[1]
    states = strip.reshape(members, lat_total * width_cols)
    cell_index = obs_cell[0]
    obs_count = cell_index.shape[0]
    spread, innov = observe(states, cell_index, obs_value[0])
    obs_meta = jnp.stack(
        [
            innov,
            obs_var[0],
            (cell_index // width_cols).astype(jnp.float32),
            (cell_index % width_cols).astype(jnp.float32),
        ]
    )
    near_spread, near_meta = (
        with_halo(spread, ((("member", "lat"), 1),), obs_count, True),
        with_halo(obs_meta, ((("member", "lat"), 1),), obs_count, True),
    )
    shifts = jnp.repeat(jnp.array([-1.0, 0.0, 1.0], jnp.float32), obs_count) * width_cols
    near_meta = jnp.concatenate([near_meta[:3], (near_meta[3] + shifts)[None, :]], axis=0)
    analysed = analyse(states, near_spread, near_meta, patch_rows[0], width_cols)
    analysed = analysed.reshape(members, lat_total, width_cols)
    returned = joined_exchange(analysed, ("member", "lat"), ("member", "lat"), (0, 1), (2, 2))
    returned = returned.reshape(members_dev, lat_rows, lat_count, member_count, width_cols)
    return returned.transpose(0, 1, 3, 2, 4).reshape(members_dev, lat_rows, lon_cells)


def solution(mesh):
    in_specs = (
        P("member", "lat", None),
        P(("member", "lat"), None),
        P(("member", "lat"), None),
        P(("member", "lat"), None),
        P(("member", "lat"), None),
    )
    out_specs = P("member", "lat", None)
    return jax.shard_map(
        per_device, mesh=mesh, in_specs=in_specs, out_specs=out_specs, check_vma=False
    )
```

profile of v0, /device:TPU:0, one launch (start us, length us, event | category | flops | bytes accessed | tf_op | source)
XLA Modules:
  0.0 299.5 jit_solution(7895239798947810683)
XLA Ops:
  0.0 4.0 %collective-permute-start = (f32[80,4,1024]{2,1,0:T(4,128)}, f32[80,4,1024]{2,1,0:T(4,128)S(1)}, u32[]{:S(2)}, u32[]{:S(2)}) collective-permute-start(f32[80,4,1024]{2,1,0:T(4,128)} %param.6), channel_id=1, source_target_pairs={{0,1},{1,2},{2,3},{3,4},{4,5},{5,6},{6,7},{7,8},{8,9},{9,10},{10,1... | collective-permute-start | bytes 3932168 | tf_op jit(solution)/shard_map/ppermute | solution.py:22
  8.3 23.9 %collective-permute-done = f32[80,4,1024]{2,1,0:T(4,128)S(1)} collective-permute-done((f32[80,4,1024]{2,1,0:T(4,128)}, f32[80,4,1024]{2,1,0:T(4,128)S(1)}, u32[]{:S(2)}, u32[]{:S(2)}) %collective-permute-start) | collective-permute-done | bytes 1310752 | tf_op jit(solution)/shard_map/ppermute | solution.py:22
  32.2 4.2 %collective-permute-done.1 = f32[80,4,1024]{2,1,0:T(4,128)S(1)} collective-permute-done((f32[80,4,1024]{2,1,0:T(4,128)}, f32[80,4,1024]{2,1,0:T(4,128)S(1)}, u32[]{:S(2)}, u32[]{:S(2)}) %collective-permute-start.1) | collective-permute-done | bytes 1310752 | tf_op jit(solution)/shard_map/ppermute | solution.py:23
  36.4 2.4 pad_maximum_fusion.4
  38.8 5.2 %fusion.116 = (f32[80,10,1023]{2,1,0:T(8,128)S(1)}, f32[80,10,1023]{2,1,0:T(8,128)}) fusion(f32[80,12,1024]{2,1,0:T(8,128)S(1)} %pad_maximum_fusion.4), kind=kLoop, calls=%fused_computation.169 | loop fusion | bytes 13094400 | tf_op jit(solution)/shard_map/jit(_roll_static)/slice | solution.py:60
  44.0 7.0 %fusion.7 = f32[80,10,1024]{2,1,0:T(8,128)S(1)} fusion(f32[80,12,1024]{2,1,0:T(8,128)S(1)} %pad_maximum_fusion.4, f32[80,4,1024]{2,1,0:T(4,128)S(1)} %collective-permute-done.1, f32[80,4,1024]{2,1,0:T(4,128)S(1)} %copy-done.3, f32[80,4,1024]{2,1,0:T(4,128)S(1)} %collective-permute-done, f32[80,10,1023]{2,1,0:T(8,128)} %get-tuple-element.12, ...), kind=kLoop, calls=%fused_computation.13 | loop fusion | flops 16384000 | bytes 23586600 | tf_op jit(solution)/shard_map/mul | solution.py:147
  51.0 1.7 fusion.114
  52.9 2.1 fusion.19
  55.0 1.4 fusion.119
  56.6 2.2 fusion.13
  60.2 2.2 fusion.57
  63.8 1.6 copy.25
  65.4 11.9 %all-to-all-start = ((f32[128,80,4,8]{1,3,2,0:T(8,128)}), f32[128,80,4,8]{1,3,2,0:T(8,128)S(1)}, u32[]{:S(2)}, u32[]{:S(2)}) async-start(f32[128,80,4,8]{1,3,2,0:T(8,128)} %bitcast.105), calls=%async_computation | async-start | bytes 4194304 | tf_op jit(solution)/shard_map/all_to_all | solution.py:46
  83.8 23.3 %all-to-all-done = f32[128,80,4,8]{1,3,2,0:T(8,128)S(1)} async-done(((f32[128,80,4,8]{1,3,2,0:T(8,128)}), f32[128,80,4,8]{1,3,2,0:T(8,128)S(1)}, u32[]{:S(2)}, u32[]{:S(2)}) %all-to-all-start) | async-done | bytes 1310752 | tf_op jit(solution)/shard_map/all_to_all | solution.py:46
  107.0 3.0 copy.26
  110.0 2.0 reshape.156
  114.4 6.0 %collective-permute-start.5 = (f32[4,128]{1,0:T(4,128)S(1)}, f32[4,128]{1,0:T(4,128)S(1)}, u32[]{:S(2)}, u32[]{:S(2)}) collective-permute-start(f32[4,128]{1,0:T(4,128)S(1)} %pad_maximum_fusion.17), channel_id=1, source_target_pairs={{1,0},{2,1},{3,2},{4,3},{5,4},{6,5},{7,6},{8,7},{9,8},{10,9},{11,1... | collective-permute-start | bytes 6152 | tf_op jit(solution)/shard_map/ppermute | solution.py:23
  120.6 7.2 %collective-permute-start.3 = (f32[640,128]{0,1:T(8,128)S(1)}, f32[640,128]{0,1:T(8,128)}, u32[]{:S(2)}, u32[]{:S(2)}) collective-permute-start(f32[640,128]{0,1:T(8,128)S(1)} %subtract_bitcast_fusion), channel_id=1, source_target_pairs={{1,0},{2,1},{3,2},{4,3},{5,4},{6,5},{7,6},{8,7},{9,8},{10,9},{11,1... | collective-permute-start | bytes 983048 | tf_op jit(solution)/shard_map/ppermute | solution.py:23
  128.5 4.5 %collective-permute-done.2 = f32[640,128]{0,1:T(8,128)} collective-permute-done((f32[640,128]{0,1:T(8,128)S(1)}, f32[640,128]{0,1:T(8,128)}, u32[]{:S(2)}, u32[]{:S(2)}) %collective-permute-start.2) | collective-permute-done | bytes 327712 | tf_op jit(solution)/shard_map/ppermute | solution.py:22
  133.1 5.7 %abs_reduce_fusion.1 = (f32[640]{0:T(1024)S(1)}, f32[640,640]{0,1:T(8,128)}) fusion(f32[640,128]{0,1:T(8,128)} %collective-permute-done.3, f32[640,128]{0,1:T(8,128)S(1)} %subtract_bitcast_fusion, f32[640,128]{0,1:T(8,128)} %collective-permute-done.2, f32[384]{0:T(512)S(1)} %get-tuple-element.5), kind=kOutput, calls=%fused_computation.52 | convolution fusion | flops 1890712960 | bytes 2625536 | tf_op jit(solution)/shard_map/dot_general | solution.py:52
  139.3 4.5 %select_subtract_fusion.5 = f32[640,640]{0,1:T(8,128)S(1)} fusion(f32[640,640]{0,1:T(8,128)} %get-tuple-element.30, f32[]{:T(128)} %reduce_max.18), kind=kOutput, calls=%fused_computation.20 | convolution fusion | flops 3148185600 | bytes 3276804 | tf_op jit(solution)/shard_map/dot_general | solution.py:52
  143.8 8.8 %fusion.78 = f32[640,640]{1,0:T(8,128)S(1)} fusion(f32[640,640]{0,1:T(8,128)S(1)} %select_subtract_fusion.5, f32[640,640]{0,1:T(8,128)S(1)} %copy-done.10, f32[]{:T(128)} %reduce_max.18), kind=kOutput, calls=%fused_computation.101 | convolution fusion | flops 3146137600 | bytes 4915204 | tf_op jit(solution)/shard_map/dot_general | solution.py:52
  152.6 4.1 %fusion.32 = f32[640,640]{1,0:T(8,128)S(1)} fusion(f32[640,640]{0,1:T(8,128)S(1)} %select_subtract_fusion.5), kind=kOutput, calls=%fused_computation.56 | convolution fusion | flops 3146137600 | bytes 3276800 | tf_op jit(solution)/shard_map/dot_general | solution.py:52
  156.7 5.1 %select_subtract_fusion.4 = f32[640,640]{0,1:T(8,128)S(1)} fusion(f32[640,640]{1,0:T(8,128)S(1)} %fusion.32, f32[640,640]{1,0:T(8,128)S(1)} %fusion.78), kind=kOutput, calls=%fused_computation.19 | convolution fusion | flops 3147366400 | bytes 4915200 | tf_op jit(solution)/shard_map/dot_general | solution.py:52
  161.8 4.8 %fusion.124 = f32[640,640]{1,0:T(8,128)S(1)} fusion(f32[640,640]{1,0:T(8,128)S(1)} %fusion.78, f32[640,640]{0,1:T(8,128)S(1)} %select_subtract_fusion.4), kind=kOutput, calls=%fused_computation.177 | convolution fusion | flops 3145728000 | bytes 4915200 | tf_op jit(solution)/shard_map/dot_general | solution.py:52
  166.7 6.2 %fusion.123 = f32[640,640]{1,0:T(8,128)} fusion(f32[640,640]{0,1:T(8,128)S(1)} %select_subtract_fusion.4, f32[640,640]{1,0:T(8,128)S(1)} %fusion.32), kind=kOutput, calls=%fused_computation.176 | convolution fusion | flops 3145728000 | bytes 4915200 | tf_op jit(solution)/shard_map/dot_general | solution.py:52
  173.5 5.7 %abs_reduce_fusion = (f32[640]{0:T(1024)S(1)}, f32[640,640]{0,1:T(8,128)}) fusion(f32[640,128]{0,1:T(8,128)} %collective-permute-done.3, f32[640,128]{0,1:T(8,128)S(1)} %subtract_bitcast_fusion, f32[640,128]{0,1:T(8,128)} %collective-permute-done.2, f32[384]{0:T(512)S(1)} %get-tuple-element.6), kind=kOutput, calls=%fused_computation.47 | convolution fusion | flops 1890712960 | bytes 2625536 | tf_op jit(solution)/shard_map/dot_general | solution.py:52
  179.8 4.9 %select_subtract_fusion.2 = f32[640,640]{0,1:T(8,128)S(1)} fusion(f32[640,640]{0,1:T(8,128)} %get-tuple-element.28, f32[]{:T(128)} %reduce_max.19), kind=kOutput, calls=%fused_computation.17 | convolution fusion | flops 3148185600 | bytes 3276804 | tf_op jit(solution)/shard_map/dot_general | solution.py:52
  184.7 8.6 %fusion.79 = f32[640,640]{1,0:T(8,128)S(1)} fusion(f32[640,640]{0,1:T(8,128)S(1)} %select_subtract_fusion.2, f32[640,640]{0,1:T(8,128)S(1)} %copy-done.9, f32[]{:T(128)} %reduce_max.19), kind=kOutput, calls=%fused_computation.102 | convolution fusion | flops 3146137600 | bytes 4915204 | tf_op jit(solution)/shard_map/dot_general | solution.py:52
  193.3 4.3 %fusion.30 = f32[640,640]{1,0:T(8,128)S(1)} fusion(f32[640,640]{0,1:T(8,128)S(1)} %select_subtract_fusion.2), kind=kOutput, calls=%fused_computation.54 | convolution fusion | flops 3146137600 | bytes 3276800 | tf_op jit(solution)/shard_map/dot_general | solution.py:52
  197.6 5.1 %select_subtract_fusion.1 = f32[640,640]{0,1:T(8,128)S(1)} fusion(f32[640,640]{1,0:T(8,128)S(1)} %fusion.30, f32[640,640]{1,0:T(8,128)S(1)} %fusion.79), kind=kOutput, calls=%fused_computation.16 | convolution fusion | flops 3147366400 | bytes 4915200 | tf_op jit(solution)/shard_map/dot_general | solution.py:52
  202.7 5.8 %fusion.127 = f32[640,640]{1,0:T(8,128)} fusion(f32[640,640]{1,0:T(8,128)S(1)} %fusion.79, f32[640,640]{0,1:T(8,128)S(1)} %select_subtract_fusion.1), kind=kOutput, calls=%fused_computation.180 | convolution fusion | flops 3145728000 | bytes 4915200 | tf_op jit(solution)/shard_map/dot_general | solution.py:52
  208.5 6.4 %fusion.126 = f32[640,640]{1,0:T(8,128)} fusion(f32[640,640]{0,1:T(8,128)S(1)} %select_subtract_fusion.1, f32[640,640]{1,0:T(8,128)S(1)} %fusion.30), kind=kOutput, calls=%fused_computation.179 | convolution fusion | flops 3145728000 | bytes 4915200 | tf_op jit(solution)/shard_map/dot_general | solution.py:52
  215.6 6.5 %fusion.125 = f32[640,640]{0,1:T(8,128)S(1)} fusion(f32[640,640]{1,0:T(8,128)} %fusion.123, f32[640,640]{1,0:T(8,128)S(1)} %fusion.124), kind=kOutput, calls=%fused_computation.178 | convolution fusion | flops 3145728000 | bytes 4915200 | tf_op jit(solution)/shard_map/dot_general | solution.py:52
  222.1 5.4 %fusion.61 = f32[640,640]{1,0:T(8,128)S(1)} fusion(f32[640,640]{1,0:T(8,128)S(1)} %copy-done, f32[640,640]{0,1:T(8,128)S(1)} %fusion.125, f32[]{:T(128)S(6)} %sqrt.6), kind=kOutput, calls=%fused_computation.81 | convolution fusion | flops 3147776000 | bytes 4915204 | tf_op jit(solution)/shard_map/dot_general | solution.py:52
  227.5 1.8 fusion.62
  229.3 1.5 convolution_bitcast_fusion.1
  230.9 1.6 convolution_reduce_fusion.1
  232.5 5.1 %fusion.128 = f32[640,640]{0,1:T(8,128)S(1)} fusion(f32[640,640]{1,0:T(8,128)S(1)} %copy-done.2, f32[640,640]{1,0:T(8,128)S(1)} %copy-done.1), kind=kOutput, calls=%fused_computation.181 | convolution fusion | flops 3145728000 | bytes 4915200 | tf_op jit(solution)/shard_map/dot_general | solution.py:52
  237.6 5.2 %fusion.60 = f32[640,640]{1,0:T(8,128)S(1)} fusion(f32[640,640]{1,0:T(8,128)S(1)} %copy-done.2, f32[640,640]{0,1:T(8,128)S(1)} %fusion.128, f32[]{:T(128)S(6)} %sqrt.7), kind=kOutput, calls=%fused_computation.80 | convolution fusion | flops 3147776000 | bytes 4915204 | tf_op jit(solution)/shard_map/dot_general | solution.py:52
  242.8 1.8 fusion.65
  244.6 1.5 convolution_bitcast_fusion
  246.1 1.6 convolution_reduce_fusion
  247.7 3.5 %fusion.43 = f32[640,512]{1,0:T(8,128)S(1)} fusion(f32[640,640]{1,0:T(8,128)S(1)} %fusion.60, f32[640,512]{1,0:T(8,128)S(1)} %copy.30, f32[640]{0:T(1024)S(1)} %convolution_reduce_fusion, f32[512]{0:T(512)S(1)} %div.86, pred[512]{0:T(512)(128)(4,1)S(1)} %fusion.93), kind=kOutput, calls=%fused_computation.61 | convolution fusion | flops 2518056960 | bytes 4264960 | tf_op jit(solution)/shard_map/dot_general | solution.py:52
  251.2 4.8 %fusion.40 = f32[640,512]{1,0:T(8,128)} fusion(f32[640,512]{1,0:T(8,128)S(1)} %fusion.43, f32[640,640]{1,0:T(8,128)S(1)} %fusion.61, f32[640,512]{1,0:T(8,128)S(1)} %copy.30, f32[640]{0:T(1024)S(1)} %convolution_reduce_fusion.1, f32[512]{0:T(512)S(1)} %div.86, pred[512]{0:T(512)(128)(4,1)S(1)} %fusion.92), kind=kOutput, calls=%fused_computation.60 | convolution fusion | flops 2518712320 | bytes 5575680 | tf_op jit(solution)/shard_map/dot_general | solution.py:52
  256.0 1.7 copy.34
  259.1 38.2 %all_to_all.10 = f32[128,80,4,8]{1,3,2,0:T(8,128)S(1)} all-to-all(f32[128,80,4,8]{1,3,2,0:T(8,128)S(1)} %bitcast.108), channel_id=1, replica_groups=mesh['member'=8,'lat'=16] {'member','lat'}, dimensions={0} | all-to-all | bytes 2621440 | tf_op jit(solution)/shard_map/all_to_all | solution.py:46
  297.6 1.7 copy.39
  (67 shorter events, 14.7 us)
Async XLA Ops:
  0.0 32.2 %collective-permute-start = (f32[80,4,1024]{2,1,0:T(4,128)}, f32[80,4,1024]{2,1,0:T(4,128)S(1)}, u32[]{:S(2)}, u32[]{:S(2)}) collective-permute-start(f32[80,4,1024]{2,1,0:T(4,128)} %param.6), channel_id=1, source_target_pairs={{0,1},{1,2},{2,3},{3,4},{4,5},{5,6},{6,7},{7,8},{8,9},{9,10},{10,1... | collective-permute-start | bytes 3932168 | tf_op jit(solution)/shard_map/ppermute | solution.py:22
  4.0 32.4 %collective-permute-start.1 = (f32[80,4,1024]{2,1,0:T(4,128)}, f32[80,4,1024]{2,1,0:T(4,128)S(1)}, u32[]{:S(2)}, u32[]{:S(2)}) collective-permute-start(f32[80,4,1024]{2,1,0:T(4,128)} %param.6), channel_id=1, source_target_pairs={{1,0},{2,1},{3,2},{4,3},{5,4},{6,5},{7,6},{8,7},{9,8},{10,9},{11,1... | collective-permute-start | bytes 3932168 | tf_op jit(solution)/shard_map/ppermute | solution.py:23
  38.8 5.2 %copy-start.3 = (f32[80,4,1024]{2,1,0:T(4,128)S(1)}, f32[80,4,1024]{2,1,0:T(4,128)}, u32[]{:S(2)}) copy-start(f32[80,4,1024]{2,1,0:T(4,128)} %param.6) | copy-start | bytes 3932164
  65.4 12.0 %copy-start.4 = (s32[1,2]{1,0:T(1,128)S(1)}, s32[1,2]{1,0:T(1,128)}, u32[]{:S(2)}) copy-start(s32[1,2]{1,0:T(1,128)} %param.10) | copy-start | bytes 28
  65.4 18.2 %copy-start.7 = (s32[1,128]{1,0:T(1,128)S(1)}, s32[1,128]{1,0:T(1,128)}, u32[]{:S(2)}) copy-start(s32[1,128]{1,0:T(1,128)} %param.7) | copy-start | bytes 1540
  65.4 18.3 %copy-start.6 = (f32[3]{0:T(128)S(1)}, f32[3]{0:T(128)}, u32[]{:S(2)}) copy-start(f32[3]{0:T(128)} %constant.134) | copy-start | bytes 40
  65.4 41.6 %all-to-all-start = ((f32[128,80,4,8]{1,3,2,0:T(8,128)}), f32[128,80,4,8]{1,3,2,0:T(8,128)S(1)}, u32[]{:S(2)}, u32[]{:S(2)}) async-start(f32[128,80,4,8]{1,3,2,0:T(8,128)} %bitcast.105), calls=%async_computation | async-start | bytes 4194304 | tf_op jit(solution)/shard_map/all_to_all | solution.py:46
  112.1 1.0 copy-start.8
  112.1 1.0 copy-start.5
  113.1 15.3 %collective-permute-start.4 = (f32[4,128]{1,0:T(4,128)S(1)}, f32[4,128]{1,0:T(4,128)S(1)}, u32[]{:S(2)}, u32[]{:S(2)}) collective-permute-start(f32[4,128]{1,0:T(4,128)S(1)} %pad_maximum_fusion.17), channel_id=1, source_target_pairs={{0,1},{1,2},{2,3},{3,4},{4,5},{5,6},{6,7},{7,8},{8,9},{9,10},{10,1... | collective-permute-start | bytes 6152 | tf_op jit(solution)/shard_map/ppermute | solution.py:22
  114.4 14.1 %collective-permute-start.5 = (f32[4,128]{1,0:T(4,128)S(1)}, f32[4,128]{1,0:T(4,128)S(1)}, u32[]{:S(2)}, u32[]{:S(2)}) collective-permute-start(f32[4,128]{1,0:T(4,128)S(1)} %pad_maximum_fusion.17), channel_id=1, source_target_pairs={{1,0},{2,1},{3,2},{4,3},{5,4},{6,5},{7,6},{8,7},{9,8},{10,9},{11,1... | collective-permute-start | bytes 6152 | tf_op jit(solution)/shard_map/ppermute | solution.py:23
  120.5 12.6 %collective-permute-start.2 = (f32[640,128]{0,1:T(8,128)S(1)}, f32[640,128]{0,1:T(8,128)}, u32[]{:S(2)}, u32[]{:S(2)}) collective-permute-start(f32[640,128]{0,1:T(8,128)S(1)} %subtract_bitcast_fusion), channel_id=1, source_target_pairs={{0,1},{1,2},{2,3},{3,4},{4,5},{5,6},{6,7},{7,8},{8,9},{9,10},{10,1... | collective-permute-start | bytes 983048 | tf_op jit(solution)/shard_map/ppermute | solution.py:22
  120.6 12.5 %collective-permute-start.3 = (f32[640,128]{0,1:T(8,128)S(1)}, f32[640,128]{0,1:T(8,128)}, u32[]{:S(2)}, u32[]{:S(2)}) collective-permute-start(f32[640,128]{0,1:T(8,128)S(1)} %subtract_bitcast_fusion), channel_id=1, source_target_pairs={{1,0},{2,1},{3,2},{4,3},{5,4},{6,5},{7,6},{8,7},{9,8},{10,9},{11,1... | collective-permute-start | bytes 983048 | tf_op jit(solution)/shard_map/ppermute | solution.py:23
  139.3 4.5 %copy-start.10 = (f32[640,640]{0,1:T(8,128)S(1)}, f32[640,640]{0,1:T(8,128)}, u32[]{:S(2)}) copy-start(f32[640,640]{0,1:T(8,128)} %get-tuple-element.30) | copy-start | bytes 4915204
  179.8 4.9 %copy-start.9 = (f32[640,640]{0,1:T(8,128)S(1)}, f32[640,640]{0,1:T(8,128)}, u32[]{:S(2)}) copy-start(f32[640,640]{0,1:T(8,128)} %get-tuple-element.28) | copy-start | bytes 4915204
  215.6 6.5 %copy-start = (f32[640,640]{1,0:T(8,128)S(1)}, f32[640,640]{1,0:T(8,128)}, u32[]{:S(2)}) copy-start(f32[640,640]{1,0:T(8,128)} %fusion.123) | copy-start | bytes 4915204
  229.3 3.1 %copy-start.1 = (f32[640,640]{1,0:T(8,128)S(1)}, f32[640,640]{1,0:T(8,128)}, u32[]{:S(2)}) copy-start(f32[640,640]{1,0:T(8,128)} %fusion.127) | copy-start | bytes 4915204
  229.3 3.1 %copy-start.2 = (f32[640,640]{1,0:T(8,128)S(1)}, f32[640,640]{1,0:T(8,128)}, u32[]{:S(2)}) copy-start(f32[640,640]{1,0:T(8,128)} %fusion.126) | copy-start | bytes 4915204
where the time goes:
time: 304 us; the launch traced here: 300 us
  matrix products  120 us (39%)
  waiting for transfers between devices  55.9 us (18%)
  blocking collectives  38.2 us (13%)
  starting transfers between devices  31.7 us (10%)
  local copies, waits for them, and re-layouts  25.9 us (9%)
  other arithmetic  20.5 us (7%)
  between operations  7.16 us (2%)
    dot_general x26, matrix products, matmul(): jnp.dot(left, right, precision=lax.Precision.HIGHEST, preferred_element_t...  120 us
    all_to_all x1, blocking collectives, joined_exchange(): parts = lax.all_to_all(parts, axis, split_axis=0, concat_axis=0, tiled=True)  38.2 us
    ppermute x3, waiting for transfers between devices, with_halo(): before = lax.ppermute(last, axis, up)  28.4 us
    all_to_all x1, waiting for transfers between devices, joined_exchange(): parts = lax.all_to_all(parts, axis, split_axis=0, concat_axis=0, tiled=True)  23.3 us
    ppermute x3, starting transfers between devices, with_halo(): after = lax.ppermute(initial, axis, down)  14.4 us
    mul x4, other arithmetic, per_device(): padded = padded * keeper[None, :, None]  13.5 us
    all_to_all x1, starting transfers between devices, joined_exchange(): parts = lax.all_to_all(parts, axis, split_axis=0, concat_axis=0, tiled=True)  11.9 us
  transfers between devices with their start and end apart: 7, of which 4 were waited for; matrix products, arithmetic and copies ran while one was open for 2% of the time, Pallas kernels for 0%

commit v1 on v0

v1 whole, which is shorter than its diff:
```python
import functools

import jax
import jax.numpy as jnp
import numpy as np
from jax import lax
from jax.experimental import pallas as pl
from jax.experimental.pallas import tpu as pltpu
from jax.sharding import PartitionSpec as P

BOTH = ("member", "lat")
K = 640
MEM = 80
NOBS = 384
CELLS = 512
F32 = jnp.float32
BF16 = jnp.bfloat16


def strip_places():
    columns = []
    for x in range(4):
        for y in range(4) if x % 2 == 0 else range(3, -1, -1):
            columns.append((x, y))
    places, z = [], 0
    for x, y in columns:
        for k in range(4):
            for core in range(2):
                places.append((y * 2 + core) * 16 + x * 4 + (z + k) % 4)
        z = (z + 3) % 4
    return places


PLACE = strip_places()


def lane_iota(rows=8):
    return lax.broadcasted_iota(jnp.int32, (rows, 128), 1)


def roll(value, shift):
    return pltpu.roll(value, shift % value.shape[-1], value.ndim - 1)


def block_transpose(values, size):
    values = list(values)
    count = len(values)
    lane = lane_iota()
    dist = 1
    while dist < count:
        low = (lane // (size * dist)) % 2 == 0
        for i in range(count):
            if i & dist:
                continue
            a, b = values[i], values[i + dist]
            values[i] = jnp.where(low, a, roll(b, size * dist))
            values[i + dist] = jnp.where(low, roll(a, -size * dist), b)
        dist *= 2
    return values


def pack_kernel(ens_ref, cell_ref, value_ref, var_ref, rows_ref, out_ref, meta_ref):
    meta_ref[...] = jnp.zeros_like(meta_ref)
    meta_ref[0:1, :] = cell_ref[...].astype(F32)
    meta_ref[1:2, :] = value_ref[...]
    meta_ref[2:3, :] = var_ref[...]
    meta_ref[3:4, :] = jnp.broadcast_to(rows_ref[0:1, 0:1].astype(F32), (1, 128))

    def body(i, carry):
        wide = []
        for h in range(2):
            for r in range(4):
                src = ens_ref[r, pl.ds(pl.multiple_of(h * 40 + i * 8, 8), 8), :]
                wide.append((roll(src, 4), roll(src, -4)))
        for g in range(8):
            for q in range(2):
                parts = [w[q][:, g * 128 : (g + 1) * 128] for w in wide]
                for w, part in enumerate(block_transpose(parts, 16)):
                    out_ref[PLACE[16 * g + 2 * w + q], pl.ds(pl.multiple_of(i * 8, 8), 8), :] = part
        return carry

    lax.fori_loop(0, 5, body, 0)


def forecast_kernel(recv_ref, meta_ref, x_ref, obs_ref):
    lane = lane_iota()

    def step(f):
        new = []
        for k in range(8):
            c = f[k]
            n = f[k - 1] if k else jnp.where(lane < 16, 0.0, roll(f[7], 16))
            s = f[k + 1] if k < 7 else jnp.where(lane >= 112, 0.0, roll(f[0], -16))
            e = roll(c, -1)
            w = roll(c, 1)
            t = 0.1 * c
            new.append(t + 0.4 * (n + s) + (0.05 - t) * e + (0.05 + t) * w)
        return new

    def body(index, carry):
        m, i = index // 5, index % 5
        rows = pl.ds(pl.multiple_of(i * 8, 8), 8)
        even = block_transpose([recv_ref[m * 16 + 2 * j, rows, :] for j in range(8)], 16)
        odd = block_transpose([recv_ref[m * 16 + 2 * j + 1, rows, :] for j in range(8)], 16)
        for h in range(2):
            f = even[4 * h : 4 * h + 4] + odd[4 * h : 4 * h + 4]
            for _ in range(4):
                f = step(f)
            dest = pl.ds(pl.multiple_of(m * 80 + h * 40 + i * 8, 8), 8)
            for r in range(4):
                x_ref[dest, r * 128 : (r + 1) * 128] = jnp.where(
                    lane % 16 < 8, roll(f[r], -4), roll(f[4 + r], 4)
                )
        return carry

    lax.fori_loop(0, 40, body, 0)
    cell = meta_ref[0:1, :].astype(jnp.int32)
    row = cell // 8
    place = (row % 4) * 128 + (row // 4) * 8 + cell % 8
    pick = jnp.where(
        lax.broadcasted_iota(jnp.int32, (CELLS, 128), 0) == place, 1.0, 0.0
    ).astype(BF16)

    def gather(i, carry):
        rows = pl.ds(pl.multiple_of(i * 128, 128), 128)
        x = x_ref[rows, :]
        x1 = x.astype(BF16)
        rest = x - x1.astype(F32)
        x2 = rest.astype(BF16)
        x3 = (rest - x2.astype(F32)).astype(BF16)
        total = jnp.dot(x1, pick, preferred_element_type=F32)
        total = total + jnp.dot(x2, pick, preferred_element_type=F32)
        obs_ref[rows, :] = total + jnp.dot(x3, pick, preferred_element_type=F32)
        return carry

    lax.fori_loop(0, 5, gather, 0)
    obs_ref[K : K + 8, :] = meta_ref[...]


def split(value):
    high = value.astype(BF16)
    return high, (value - high.astype(F32)).astype(BF16)


def left3(value):
    high, low = split(value)
    return jnp.concatenate([high, high, low], axis=1)


def right3(value):
    high, low = split(value)
    return jnp.concatenate([high, low, high], axis=0)


def mm(left, right):
    return jnp.dot(left, right, preferred_element_type=F32)


def server_kernel(
    x_ref, own_ref, before_ref, after_ref, out_ref, xa, y, yl3, yt3, xr3, p3, res, sums
):
    near = (before_ref, own_ref, after_ref)
    mean = jnp.sum(x_ref[...], axis=0, keepdims=True) * (1.0 / K)
    xa[...] = x_ref[...] - mean
    innov, var, orow, ocol = [], [], [], []
    for j, ref in enumerate(near):
        obs = ref[0:K, :]
        obs_mean = jnp.sum(obs, axis=0, keepdims=True) * (1.0 / K)
        y[:, j * 128 : (j + 1) * 128] = obs - obs_mean
        cell = ref[K : K + 1, :].astype(jnp.int32)
        innov.append(ref[K + 1 : K + 2, :] - obs_mean)
        var.append(ref[K + 2 : K + 3, :])
        orow.append((cell // 8).astype(F32))
        ocol.append((cell % 8).astype(F32) + 8.0 * (j - 1))
    innov, var, orow, ocol = (jnp.concatenate(v, axis=1) for v in (innov, var, orow, ocol))
    yv = y[...]
    yl3[...] = left3(yv)
    yt = yv.T
    yt_high, yt_low = split(yt)
    yt3[0:NOBS, :] = yt_high
    yt3[NOBS : 2 * NOBS, :] = yt_low
    yt3[2 * NOBS :, :] = yt_high
    ytl3 = jnp.concatenate([yt_high, yt_high, yt_low], axis=1)
    t_mat = mm(ytl3, right3(yv))
    xr3[...] = right3(xa[...])
    u_mat = mm(ytl3, xr3[...])

    first = own_ref[K + 3 : K + 4, 0:1]
    lane = lax.broadcasted_iota(jnp.int32, (1, CELLS), 1)
    cell_row = ((lane % 128) // 8 * 4 + lane // 128).astype(F32)
    eye = jnp.where(
        lax.broadcasted_iota(jnp.int32, (NOBS, NOBS), 0)
        == lax.broadcasted_iota(jnp.int32, (NOBS, NOBS), 1),
        1.0,
        0.0,
    )
    c_total = jnp.zeros((NOBS, CELLS), F32)
    coef = jnp.zeros((1, CELLS), F32)
    drow = jnp.zeros((1, CELLS), F32)
    for patch in range(2):
        lower = jnp.zeros_like(first) if patch == 0 else first
        upper = (first if patch == 0 else jnp.full_like(first, 64.0)) - 1.0
        gap_row = jnp.maximum(jnp.maximum(lower - orow, orow - upper), 0.0) * (1.0 / 16.0)
        gap_col = jnp.maximum(jnp.maximum(-ocol, ocol - 7.0), 0.0) * (1.0 / 8.0)
        g = jnp.exp(-gap_row * gap_row - gap_col * gap_col) / var
        sg = jnp.sqrt(g)
        both = jnp.concatenate([sg, sg * innov, jnp.zeros((6, NOBS), F32)], axis=0).T
        sg_col, sgd_col = both[:, 0:1], both[:, 1:2]
        p3[...] = left3(yv * g)
        sums[...] = jnp.zeros_like(sums)

        def gram(i, carry):
            rows = pl.ds(pl.multiple_of(i * 128, 128), 128)
            block = jnp.abs(mm(p3[rows, :], yt3[...]))
            sums[...] += jnp.sum(block.reshape(16, 8, K), axis=0)
            return carry

        lax.fori_loop(0, 5, gram, 0)
        bound = (K - 1.0) + jnp.max(
            jnp.sum(sums[...], axis=0, keepdims=True), axis=1, keepdims=True
        )
        inv = 1.0 / bound
        q0 = (K - 1.0) * inv
        a1 = 1.5 - 0.5 * q0
        m20 = 1.5 - 0.5 * q0 * a1 * a1
        z20 = a1 * m20
        z30 = z20 * (1.5 - 0.5 * q0 * z20 * z20)
        s = (sg_col * inv) * t_mat * sg
        s_left = left3(s)
        s2 = mm(s_left, right3(s))
        k2 = -0.5 * ((a1 * a1 - q0 * a1) * eye + (0.25 * q0 - a1) * s + 0.25 * s2)
        m2 = m20 * eye + mm(s_left, right3(k2))
        kz2 = a1 * k2 - 0.5 * m2
        z2 = z20 * eye + mm(s_left, right3(kz2))
        z2_left = left3(z2)
        inside = (cell_row >= lower) & (cell_row <= upper)
        spare = CELLS - 1 if patch == 0 else 0
        v = jnp.where(lane == spare, sgd_col, sg_col * u_mat)
        w1 = mm(z2_left, right3(v))
        w2 = mm(z2_left, right3(w1))
        tail = 1.5 * v - (0.5 * q0) * (w2 + z20 * w1 + (z20 * z20) * v)
        hv = mm(z2_left, right3(-0.5 * w2)) + mm(left3(kz2), right3(tail))
        h_col = hv[:, spare : spare + 1]
        z_row = jnp.sum(h_col * s, axis=0, keepdims=True)
        pair = jnp.concatenate([z_row, jnp.zeros((7, NOBS), F32)], axis=0).T
        u_col = z30 * sgd_col + pair[:, 0:1]
        su_row = jnp.sum(u_col * s, axis=0, keepdims=True)
        su_col = jnp.concatenate([su_row, jnp.zeros((7, NOBS), F32)], axis=0).T[:, 0:1]
        drift = (jnp.sum((z30 * u_col) * v + su_col * hv, axis=0, keepdims=True)) * inv
        scale = jnp.sqrt(q0)
        c_total = jnp.where(inside, (sg_col * (scale * inv)) * hv, c_total)
        coef = jnp.where(inside, scale * z30, coef)
        drow = jnp.where(inside, drift, drow)
    base = mean + drow
    c_right = right3(c_total)
    res[...] = base + coef * xa[...] + mm(yl3[...], c_right)

    def pack(m, carry):
        for k in range(3):
            parts = []
            for b in range(4):
                i = k * 4 + b
                for r in range(4):
                    if i < 10:
                        rows = pl.ds(pl.multiple_of(m * 80 + i * 8, 8), 8)
                        parts.append(res[rows, r * 128 : (r + 1) * 128])
                    else:
                        parts.append(jnp.zeros((8, 128), F32))
            for l, part in enumerate(block_transpose(parts, 8)):
                out_ref[m * 16 + l, k * 8 : (k + 1) * 8, :] = part
        return carry

    lax.fori_loop(0, 8, pack, 0)


def unpack_kernel(recv_ref, out_ref):
    for k in range(3):
        for g in range(8):
            parts = [recv_ref[PLACE[16 * g + t], k * 8 : (k + 1) * 8, :] for t in range(16)]
            parts = block_transpose(parts, 8)
            for b in range(4):
                i = k * 4 + b
                if i >= 10:
                    continue
                for r in range(4):
                    out_ref[r, i * 8 : (i + 1) * 8, g * 128 : (g + 1) * 128] = parts[4 * b + r]


def call(kernel, out_shape, *args, scratch=(), name=None):
    return pl.pallas_call(
        kernel,
        out_shape=out_shape,
        scratch_shapes=scratch,
        compiler_params=pltpu.CompilerParams(vmem_limit_bytes=56 * 1024 * 1024),
        name=name,
    )(*args)


def shaped(*shape, dtype=F32):
    return jax.ShapeDtypeStruct(shape, dtype)


def per_device(ensemble, obs_cell, obs_value, obs_var, patch_rows):
    chunks, meta = call(
        pack_kernel,
        (shaped(128, 40, 128), shaped(8, 128)),
        ensemble.transpose(1, 0, 2),
        obs_cell,
        obs_value,
        obs_var,
        patch_rows,
        name="pack",
    )
    meta = lax.ppermute(meta, BOTH, [(s, PLACE[s]) for s in range(128)])
    recv = lax.all_to_all(chunks, BOTH, split_axis=0, concat_axis=0, tiled=True)
    x, obs = call(
        forecast_kernel, (shaped(K, CELLS), shaped(K + 8, 128)), recv, meta, name="forecast"
    )
    up = [(PLACE[s], PLACE[(s + 1) % 128]) for s in range(128)]
    down = [(b, a) for a, b in up]
    before = lax.ppermute(obs, BOTH, up)
    after = lax.ppermute(obs, BOTH, down)
    back = call(
        server_kernel,
        shaped(128, 24, 128),
        x,
        obs,
        before,
        after,
        scratch=[
            pltpu.VMEM((K, CELLS), F32),
            pltpu.VMEM((K, NOBS), F32),
            pltpu.VMEM((K, 3 * NOBS), BF16),
            pltpu.VMEM((3 * NOBS, K), BF16),
            pltpu.VMEM((3 * K, CELLS), BF16),
            pltpu.VMEM((K, 3 * NOBS), BF16),
            pltpu.VMEM((K, CELLS), F32),
            pltpu.VMEM((8, K), F32),
        ],
        name="server",
    )
    back = lax.all_to_all(back, BOTH, split_axis=0, concat_axis=0, tiled=True)
    out = call(unpack_kernel, shaped(4, MEM, 1024), back, name="unpack")
    return out.transpose(1, 0, 2)


def solution(mesh):
    in_specs = (
        P("member", "lat", None),
        P(BOTH, None),
        P(BOTH, None),
        P(BOTH, None),
        P(BOTH, None),
    )
    return jax.shard_map(
        per_device,
        mesh=mesh,
        in_specs=in_specs,
        out_specs=P("member", "lat", None),
        check_vma=False,
    )
```

time: 304 us -> 170 us (0.56); the launches traced: 300 us -> 169 us
  matrix products: 120 us -> 0 us
  Pallas kernels: 0 us -> 75.9 us
  other arithmetic: 20.5 us -> 0 us
  starting transfers between devices: 31.7 us -> 12.3 us
  local copies, waits for them, and re-layouts: 25.9 us -> 8.61 us
  waiting for transfers between devices: 55.9 us -> 42.3 us
  blocking collectives: 38.2 us -> 30.2 us
  between operations: 7.16 us -> 0.05 us
    dot_general x26 -> x0, matrix products: 120 us -> none  [matmul(): jnp.dot(left, right, precision=lax.Precision.HIGHEST, preferred_element_t...]
    pallas_call x0 -> x4, Pallas kernels: none -> 75.9 us  [call(): pl.pallas_call(kernel, out_shape=out_shape, scratch_shapes=scratch, compi...]
    ppermute x6 -> x3, waiting for transfers between devices: 32.7 us -> 7.79 us  [the longest x1 4.78 us: per_device(): after = lax.ppermute(obs, BOTH, down)]
    ppermute x6 -> x3, starting transfers between devices: 19.8 us -> 1.17 us  [the longest x1 0.66 us: per_device(): meta = lax.ppermute(meta, BOTH, [(s, PLACE[s]) for s in range(128)])]
    mul x4 -> x0, other arithmetic: 13.5 us -> none  [per_device(): padded = padded * keeper[None, :, None]]
    slice x13 -> x0, local copies, waits for them, and re-layouts: 11.4 us -> none  [the longest x1 5.17 us: advance(): western = jnp.roll(centre, 1, axis=2)]
    all_to_all x1, waiting for transfers between devices: 23.3 us -> 34.5 us  [per_device(): recv = lax.all_to_all(chunks, BOTH, split_axis=0, concat_axis=0, tiled=True)]
    all_to_all x1, blocking collectives: 38.2 us -> 30.2 us  [per_device(): back = lax.all_to_all(back, BOTH, split_axis=0, concat_axis=0, tiled=True)]
  transfers between devices with their start and end apart: 7 -> 4, of which waited for: 4 -> 3; matrix products, arithmetic and copies ran while one was open for 2% -> 0% of each run, Pallas kernels for 0% -> 0%
where the time goes in v1:
time: 170 us; the launch traced here: 169 us
  Pallas kernels  75.9 us (45%)
  waiting for transfers between devices  42.3 us (25%)
  blocking collectives  30.2 us (18%)
  starting transfers between devices  12.3 us (7%)
  local copies, waits for them, and re-layouts  8.61 us (5%)
    pallas_call x4, Pallas kernels, call(): pl.pallas_call(kernel, out_shape=out_shape, scratch_shapes=scratch, compi...  75.9 us
    all_to_all x1, waiting for transfers between devices, per_device(): recv = lax.all_to_all(chunks, BOTH, split_axis=0, concat_axis=0, tiled=True)  34.5 us
    all_to_all x1, blocking collectives, per_device(): back = lax.all_to_all(back, BOTH, split_axis=0, concat_axis=0, tiled=True)  30.2 us
    all_to_all x1, starting transfers between devices, per_device(): recv = lax.all_to_all(chunks, BOTH, split_axis=0, concat_axis=0, tiled=True)  11.1 us
    unnamed x11, local copies, waits for them, and re-layouts  5.4 us
    ppermute x1, waiting for transfers between devices, per_device(): after = lax.ppermute(obs, BOTH, down)  4.78 us
  transfers between devices with their start and end apart: 4, of which 3 were waited for; matrix products, arithmetic and copies ran while one was open for 0% of the time, Pallas kernels for 0%

profile of v1, /device:TPU:0, one launch (start us, length us, event | category | flops | bytes accessed | tf_op | source)
XLA Modules:
  0.0 169.4 jit_solution(3604948938241826340)
XLA Ops:
  0.0 3.1 %copy.9 = f32[80,4,1024]{2,0,1:T(8,128)} copy(f32[80,4,1024]{2,1,0:T(4,128)} %param.5) | data formatting | bytes 2621440 | tf_op args[0]
  3.1 13.4 %pack.1 = (f32[128,40,128]{2,1,0:T(8,128)}, f32[8,128]{1,0:T(8,128)}) custom-call(f32[4,80,1024]{2,1,0:T(8,128)} %bitcast.4, s32[1,128]{1,0:T(1,128)} %cell_ref.1, f32[1,128]{1,0:T(1,128)} %value_ref.1, f32[1,128]{1,0:T(1,128)} %var_ref.1, s32[1,2]{1,0:T(1,128)} %rows_ref.1), custom_call_target="tpu_custom_call" | custom-call | tf_op jit(solution)/shard_map/pack/pallas_call | solution.py:290
  16.5 0.0 copy-start.4
  16.5 11.1 %all-to-all-start = ((f32[128,40,128]{2,1,0:T(8,128)}), f32[128,40,128]{2,1,0:T(8,128)S(1)}, u32[]{:S(2)}, u32[]{:S(2)}) async-start(f32[128,40,128]{2,1,0:T(8,128)} %get-tuple-element.9), calls=%async_computation | async-start | bytes 5242880 | tf_op jit(solution)/shard_map/all_to_all | solution.py:315
  27.7 0.0 copy-done.4
  27.7 0.7 collective-permute-start
  28.3 0.0 collective-permute-done.meta_ref
  28.4 0.0 copy-start.3
  28.4 34.5 %all-to-all-done.recv_ref = f32[128,40,128]{2,1,0:T(8,128)S(1)} async-done(((f32[128,40,128]{2,1,0:T(8,128)}), f32[128,40,128]{2,1,0:T(8,128)S(1)}, u32[]{:S(2)}, u32[]{:S(2)}) %all-to-all-start) | async-done | bytes 2621472 | tf_op jit(solution)/shard_map/all_to_all | solution.py:315
  62.9 0.0 copy-done.3
  62.9 0.0 copy-start
  62.9 1.5 copy-done
  64.4 31.1 %forecast.1 = (f32[640,512]{1,0:T(8,128)}, f32[648,128]{1,0:T(8,128)}) custom-call(f32[128,40,128]{2,1,0:T(8,128)} %copy-done, f32[8,128]{1,0:T(8,128)} %copy-done.3), custom_call_target="tpu_custom_call" | custom-call | tf_op jit(solution)/shard_map/forecast/pallas_call | solution.py:290
  95.5 0.3 collective-permute-start.2
  95.9 0.2 collective-permute-start.1
  96.0 4.8 %collective-permute-done.2.after_ref = f32[648,128]{1,0:T(8,128)S(1)} collective-permute-done((f32[648,128]{1,0:T(8,128)}, f32[648,128]{1,0:T(8,128)S(1)}, u32[]{:S(2)}, u32[]{:S(2)}) %collective-permute-start.2) | collective-permute-done | bytes 331808 | tf_op jit(solution)/shard_map/ppermute | solution.py:322
  100.8 0.0 copy-start.1
  100.8 3.0 %collective-permute-done.1.before_ref = f32[648,128]{1,0:T(8,128)S(1)} collective-permute-done((f32[648,128]{1,0:T(8,128)}, f32[648,128]{1,0:T(8,128)S(1)}, u32[]{:S(2)}, u32[]{:S(2)}) %collective-permute-start.1) | collective-permute-done | bytes 331808 | tf_op jit(solution)/shard_map/ppermute | solution.py:321
  103.8 0.0 copy-start.2
  103.8 0.0 copy-done.1
  103.8 0.7 copy-done.2
  104.6 23.9 %server.1 = f32[128,24,128]{2,1,0:T(8,128)} custom-call(f32[640,512]{1,0:T(8,128)} %get-tuple-element.11.x_ref, f32[648,128]{1,0:T(8,128)} %get-tuple-element.12.own_ref, f32[648,128]{1,0:T(8,128)} %copy-done.2, f32[648,128]{1,0:T(8,128)} %copy-done.1), custom_call_target="tpu_custom_call" | custom-call | tf_op jit(solution)/shard_map/server/pallas_call | solution.py:290
  128.5 30.2 %all_to_all.10.recv_ref = f32[128,24,128]{2,1,0:T(8,128)} all-to-all(f32[128,24,128]{2,1,0:T(8,128)} %server.1), channel_id=1, replica_groups=mesh['member'=8,'lat'=16] {'member','lat'}, dimensions={0} | all-to-all | bytes 3145728 | tf_op jit(solution)/shard_map/all_to_all | solution.py:342
  158.7 7.5 %unpack.1 = f32[4,80,1024]{2,1,0:T(8,128)} custom-call(f32[128,24,128]{2,1,0:T(8,128)} %all_to_all.10.recv_ref), custom_call_target="tpu_custom_call" | custom-call | tf_op jit(solution)/shard_map/unpack/pallas_call | solution.py:290
  166.2 3.2 %copy.7 = f32[80,4,1024]{2,1,0:T(4,128)} copy(f32[80,4,1024]{2,0,1:T(8,128)} %bitcast.5) | data formatting | bytes 2621440 | tf_op jit(solution)/shard_map/transpose | solution.py:344
Async XLA Ops:
  16.5 11.2 %copy-start.4 = (f32[8,128]{1,0:T(8,128)S(1)}, f32[8,128]{1,0:T(8,128)}, u32[]{:S(2)}) copy-start(f32[8,128]{1,0:T(8,128)} %get-tuple-element.10) | copy-start | bytes 12292
  16.5 46.4 %all-to-all-start = ((f32[128,40,128]{2,1,0:T(8,128)}), f32[128,40,128]{2,1,0:T(8,128)S(1)}, u32[]{:S(2)}, u32[]{:S(2)}) async-start(f32[128,40,128]{2,1,0:T(8,128)} %get-tuple-element.9), calls=%async_computation | async-start | bytes 5242880 | tf_op jit(solution)/shard_map/all_to_all | solution.py:315
  27.7 0.7 collective-permute-start
  28.4 34.5 %copy-start.3 = (f32[8,128]{1,0:T(8,128)}, f32[8,128]{1,0:T(8,128)S(1)}, u32[]{:S(2)}) copy-start(f32[8,128]{1,0:T(8,128)S(1)} %collective-permute-done.meta_ref) | copy-start | bytes 12292
  62.9 1.5 copy-start
  95.5 5.3 %collective-permute-start.2 = (f32[648,128]{1,0:T(8,128)}, f32[648,128]{1,0:T(8,128)S(1)}, u32[]{:S(2)}, u32[]{:S(2)}) collective-permute-start(f32[648,128]{1,0:T(8,128)} %get-tuple-element.12.own_ref), channel_id=1, source_target_pairs={{16,0},{1,16},{17,1},{2,17},{18,2},{3,18},{19,3},{35,19},{51,35},{... | collective-permute-start | bytes 995336 | tf_op jit(solution)/shard_map/ppermute | solution.py:322
  95.9 8.0 %collective-permute-start.1 = (f32[648,128]{1,0:T(8,128)}, f32[648,128]{1,0:T(8,128)S(1)}, u32[]{:S(2)}, u32[]{:S(2)}) collective-permute-start(f32[648,128]{1,0:T(8,128)} %get-tuple-element.12.own_ref), channel_id=1, source_target_pairs={{0,16},{16,1},{1,17},{17,2},{2,18},{18,3},{3,19},{19,35},{35,51},{... | collective-permute-start | bytes 995336 | tf_op jit(solution)/shard_map/ppermute | solution.py:321
  100.8 3.0 %copy-start.1 = (f32[648,128]{1,0:T(8,128)}, f32[648,128]{1,0:T(8,128)S(1)}, u32[]{:S(2)}) copy-start(f32[648,128]{1,0:T(8,128)S(1)} %collective-permute-done.2.after_ref) | copy-start | bytes 995332
  103.8 0.7 copy-start.2

commit v2 on v1

v2 whole, which is shorter than its diff:
```python
import functools

import jax
import jax.numpy as jnp
import numpy as np
from jax import lax
from jax.experimental import pallas as pl
from jax.experimental.pallas import tpu as pltpu
from jax.sharding import PartitionSpec as P

BOTH = ("member", "lat")
K = 640
MEM = 80
NOBS = 384
CELLS = 512
F32 = jnp.float32
BF16 = jnp.bfloat16


def strip_places():
    columns = []
    for x in range(4):
        for y in range(4) if x % 2 == 0 else range(3, -1, -1):
            columns.append((x, y))
    places, z = [], 0
    for x, y in columns:
        for k in range(4):
            for core in range(2):
                places.append((y * 2 + core) * 16 + x * 4 + (z + k) % 4)
        z = (z + 3) % 4
    return places


PLACE = strip_places()


def lane_iota(rows=8):
    return lax.broadcasted_iota(jnp.int32, (rows, 128), 1)


def roll(value, shift):
    return pltpu.roll(value, shift % value.shape[-1], value.ndim - 1)


def block_transpose(values, size):
    values = list(values)
    count = len(values)
    lane = lane_iota()
    dist = 1
    while dist < count:
        low = (lane // (size * dist)) % 2 == 0
        for i in range(count):
            if i & dist:
                continue
            a, b = values[i], values[i + dist]
            values[i] = jnp.where(low, a, roll(b, size * dist))
            values[i + dist] = jnp.where(low, roll(a, -size * dist), b)
        dist *= 2
    return values


def pair_swap(a, b):
    low = lane_iota() < 64
    cross = roll(jnp.where(low, b, a), 64)
    return jnp.where(low, a, cross), jnp.where(low, cross, b)


def pack_kernel(ens_ref, cell_ref, value_ref, var_ref, rows_ref, out_ref, meta_ref, ab):
    meta_ref[...] = jnp.zeros_like(meta_ref)
    meta_ref[0:1, :] = cell_ref[...].astype(F32)
    meta_ref[1:2, :] = value_ref[...]
    meta_ref[2:3, :] = var_ref[...]
    meta_ref[3:4, :] = jnp.broadcast_to(rows_ref[0:1, 0:1].astype(F32), (1, 128))

    def shift(i, carry):
        rows = pl.ds(pl.multiple_of(i * 8, 8), 8)
        for r in range(4):
            src = ens_ref[r, rows, :]
            ab[r, rows, :] = roll(src, 4)
            ab[4 + r, rows, :] = roll(src, -4)
        return carry

    lax.fori_loop(0, 10, shift, 0, unroll=2)
    for g in range(8):
        cols = slice(g * 128, (g + 1) * 128)
        for b in range(5):
            if b < 4:
                block = jnp.concatenate([ab[2 * b, 0:64, cols], ab[2 * b + 1, 0:64, cols]], axis=0)
            else:
                block = jnp.concatenate([ab[j, 64:80, cols] for j in range(8)], axis=0)
            block = block.T
            for w in range(16):
                out_ref[PLACE[16 * g + w], 8 * b : 8 * b + 8, :] = block[8 * w : 8 * w + 8, :]


def forecast_kernel(recv_ref, meta_ref, x_ref, obs_ref, fa, fb):
    for buf in (fa, fb):
        buf[0] = jnp.zeros((16, K), F32)
        buf[65] = jnp.zeros((16, K), F32)

    def place(l, carry):
        for b in range(4):
            for k in range(4):
                outs = pair_swap(
                    recv_ref[2 * k * 16 + l, 8 * b : 8 * b + 8, :],
                    recv_ref[(2 * k + 1) * 16 + l, 8 * b : 8 * b + 8, :],
                )
                for j, out in enumerate(outs):
                    t, r = divmod(2 * b + j, 4)
                    fa[1 + 4 * l + r, 8 * t : 8 * t + 8, k * 128 : (k + 1) * 128] = out
        ends = block_transpose([recv_ref[m * 16 + l, 32:40, :] for m in range(8)], 16)
        for j, out in enumerate(ends):
            t, r = divmod(j, 4)
            fa[1 + 4 * l + r, 8 * t : 8 * t + 8, 512:640] = out
        return carry

    lax.fori_loop(0, 16, place, 0, unroll=2)

    def advance(src, row):
        c = src[row]
        n = src[row - 1]
        s = src[row + 1]
        e = pltpu.roll(c, 15, 0)
        w = pltpu.roll(c, 1, 0)
        t = 0.1 * c
        return t + 0.4 * (n + s) + (0.05 - t) * e + (0.05 + t) * w

    for src, dst in ((fa, fb), (fb, fa), (fa, fb)):

        def move(i, carry):
            dst[i + 1] = advance(src, i + 1)
            return carry

        lax.fori_loop(0, 64, move, 0, unroll=4)

    def last(i, carry):
        x_ref[pl.ds(pl.multiple_of(i * 8, 8), 8), :] = advance(fb, i + 1)[4:12, :]
        return carry

    lax.fori_loop(0, 64, last, 0, unroll=4)
    cell = jnp.concatenate([meta_ref[0:1, :], jnp.zeros((7, 128), F32)], axis=0).T[:, 0:1]
    pick = jnp.where(
        lax.broadcasted_iota(jnp.int32, (128, CELLS), 1) == cell.astype(jnp.int32), 1.0, 0.0
    ).astype(BF16)
    for j in range(5):
        cols = slice(j * 128, (j + 1) * 128)
        x = x_ref[:, cols]
        x1 = x.astype(BF16)
        rest = x - x1.astype(F32)
        x2 = rest.astype(BF16)
        x3 = (rest - x2.astype(F32)).astype(BF16)
        obs_ref[0:128, cols] = mm(pick, x1) + mm(pick, x2) + mm(pick, x3)
    obs_ref[128:136, :] = jnp.zeros((8, K), F32)
    obs_ref[128:136, 0:128] = meta_ref[...]


def split(value):
    high = value.astype(BF16)
    return high, (value - high.astype(F32)).astype(BF16)


def left3(value):
    high, low = split(value)
    return jnp.concatenate([high, high, low], axis=1)


def right3(value):
    high, low = split(value)
    return jnp.concatenate([high, low, high], axis=0)


def mm(left, right):
    return jnp.dot(left, right, preferred_element_type=F32)


def as_row(column):
    return jnp.broadcast_to(column, (column.shape[0], 128)).T[0:1, :]


def server_kernel(
    x_ref, own_ref, before_ref, after_ref, out_ref, xy3, y3, yt3, g3, res, sums
):
    mean = jnp.sum(x_ref[...], axis=1, keepdims=True) * (1.0 / K)
    xa = x_ref[...] - mean
    x_high, x_low = split(xa)
    xy3[NOBS:, 0:K] = x_high
    xy3[NOBS:, K : 2 * K] = x_high
    xy3[NOBS:, 2 * K :] = x_low
    innov, var, orow, ocol = [], [], [], []
    for j, ref in enumerate((before_ref, own_ref, after_ref)):
        obs = ref[0:128, :]
        obs_mean = jnp.sum(obs, axis=1, keepdims=True) * (1.0 / K)
        spread = obs - obs_mean
        high, low = split(spread)
        rows = slice(j * 128, (j + 1) * 128)
        xy3[rows, 0:K] = high
        xy3[rows, K : 2 * K] = high
        xy3[rows, 2 * K :] = low
        for n, part in enumerate((high, low, high)):
            yt3[n * NOBS + j * 128 : n * NOBS + (j + 1) * 128, :] = part
        y_high, y_low = split(spread.T)
        for n, part in enumerate((y_high, y_high, y_low)):
            y3[:, n * NOBS + j * 128 : n * NOBS + (j + 1) * 128] = part
        cell = ref[128:129, 0:128].astype(jnp.int32)
        innov.append(ref[129:130, 0:128] - as_row(obs_mean))
        var.append(ref[130:131, 0:128])
        orow.append((cell // 8).astype(F32))
        ocol.append((cell % 8).astype(F32) + 8.0 * (j - 1))
    innov, var, orow, ocol = (jnp.concatenate(v, axis=1) for v in (innov, var, orow, ocol))
    right = jnp.concatenate(
        [xy3[0:NOBS, 0:K], xy3[0:NOBS, 2 * K :], xy3[0:NOBS, 0:K]], axis=1
    )
    tu = lax.dot_general(
        xy3[...], right, (((1,), (1,)), ((), ())), preferred_element_type=F32
    )
    t_mat, u_mat = tu[0:NOBS], tu[NOBS:]

    first = own_ref[131:132, 0:1]
    eye = jnp.where(
        lax.broadcasted_iota(jnp.int32, (NOBS, NOBS), 0)
        == lax.broadcasted_iota(jnp.int32, (NOBS, NOBS), 1),
        1.0,
        0.0,
    )
    cell_row = (lax.broadcasted_iota(jnp.int32, (CELLS, 1), 0) // 8).astype(F32)
    is_first = cell_row < first
    parts = []
    for patch in range(2):
        lower = jnp.zeros_like(first) if patch == 0 else first
        upper = (first if patch == 0 else jnp.full_like(first, 64.0)) - 1.0
        gap_row = jnp.maximum(jnp.maximum(lower - orow, orow - upper), 0.0) * (1.0 / 16.0)
        gap_col = jnp.maximum(jnp.maximum(-ocol, ocol - 7.0), 0.0) * (1.0 / 8.0)
        g = jnp.exp(-gap_row * gap_row - gap_col * gap_col) / var
        sg = jnp.sqrt(g)
        sgd = sg * innov
        cols = jnp.concatenate([sg, sgd, g, jnp.zeros((5, NOBS), F32)], axis=0).T
        sg_col, sgd_col, g_col = cols[:, 0:1], cols[:, 1:2], cols[:, 2:3]
        scaled = (yt3[0:NOBS, :].astype(F32) + yt3[NOBS : 2 * NOBS, :].astype(F32)) * g_col
        g3[...] = right3(scaled)
        sums[...] = jnp.zeros_like(sums)

        def gram(i, carry):
            rows = pl.ds(pl.multiple_of(i * 128, 128), 128)
            block = jnp.abs(mm(y3[rows, :], g3[...]))
            sums[...] += jnp.sum(block.reshape(16, 8, K), axis=0)
            return carry

        lax.fori_loop(0, 5, gram, 0)
        bound = (K - 1.0) + jnp.max(
            jnp.sum(sums[...], axis=0, keepdims=True), axis=1, keepdims=True
        )
        inv = 1.0 / bound
        q0 = (K - 1.0) * inv
        a1 = 1.5 - 0.5 * q0
        m20 = 1.5 - 0.5 * q0 * a1 * a1
        z20 = a1 * m20
        z30 = z20 * (1.5 - 0.5 * q0 * z20 * z20)
        s = (sg_col * inv) * t_mat * sg
        s_left = left3(s)
        s2 = mm(s_left, right3(s))
        k2 = -0.5 * ((a1 * a1 - q0 * a1) * eye + (0.25 * q0 - a1) * s + 0.25 * s2)
        m2 = m20 * eye + mm(s_left, right3(k2))
        kz2 = a1 * k2 - 0.5 * m2
        z2 = z20 * eye + mm(s_left, right3(kz2))
        z2_right = right3(z2)
        v = jnp.concatenate(
            [u_mat[128 * patch : 128 * patch + 384] * sg, jnp.broadcast_to(sgd, (8, NOBS))],
            axis=0,
        )
        w1 = mm(left3(v), z2_right)
        w2 = mm(left3(w1), z2_right)
        tail = 1.5 * v - (0.5 * q0) * (w2 + z20 * w1 + (z20 * z20) * v)
        hv = mm(left3(-0.5 * w2), z2_right) + mm(left3(tail), right3(kz2))
        u_col = z30 * sgd_col + jnp.sum(hv[384:385, :] * s, axis=1, keepdims=True)
        su = jnp.sum(u_col * s, axis=0, keepdims=True)
        u = as_row(u_col)
        drift = inv * jnp.sum((z30 * u) * v[0:384] + su * hv[0:384], axis=1, keepdims=True)
        scale = jnp.sqrt(q0)
        parts.append((hv[0:384] * (sg * (scale * inv)), drift, scale * z30))
    (c0, d0, k0), (c1, d1, k1) = parts
    middle = is_first[128:384]
    c_total = jnp.concatenate(
        [c0[0:128], jnp.where(middle, c0[128:384], c1[0:256]), c1[256:384]], axis=0
    )
    drift = jnp.concatenate(
        [d0[0:128], jnp.where(middle, d0[128:384], d1[0:256]), d1[256:384]], axis=0
    )
    coef = jnp.where(is_first, k0, k1)
    res[...] = (coef * x_ref[...] + (mean * (1.0 - coef) + drift)) + mm(left3(c_total), yt3[...])

    def pack(l, carry):
        def block(r, k):
            rows = pl.ds(pl.multiple_of(l * 32 + r * 8, 8), 8)
            return res[rows, k * 128 : (k + 1) * 128]

        for half in range(2):
            for k in range(4):
                outs = pair_swap(block(2 * half, k), block(2 * half + 1, k))
                for j, out in enumerate(outs):
                    out_ref[(2 * k + j) * 16 + l, 8 * half : 8 * half + 8, :] = out
        ends = [block(r, 4) for r in range(4)]
        for j, out in enumerate(block_transpose(ends, 16)):
            out_ref[j * 16 + l, 16:24, :] = out
            out_ref[(4 + j) * 16 + l, 16:24, :] = roll(out, 64)
        return carry

    lax.fori_loop(0, 16, pack, 0, unroll=2)


def unpack_kernel(recv_ref, out_ref):
    for g in range(8):
        cols = slice(g * 128, (g + 1) * 128)
        for b in range(3):
            block = jnp.concatenate(
                [recv_ref[PLACE[16 * g + w], 8 * b : 8 * b + 8, :] for w in range(16)], axis=0
            ).T
            if b < 2:
                out_ref[2 * b, 0:64, cols] = block[0:64]
                out_ref[2 * b + 1, 0:64, cols] = block[64:128]
            else:
                for r in range(4):
                    out_ref[r, 64:80, cols] = block[16 * r : 16 * r + 16]


def call(kernel, out_shape, *args, scratch=(), name=None):
    return pl.pallas_call(
        kernel,
        out_shape=out_shape,
        scratch_shapes=scratch,
        compiler_params=pltpu.CompilerParams(vmem_limit_bytes=56 * 1024 * 1024),
        name=name,
    )(*args)


def shaped(*shape, dtype=F32):
    return jax.ShapeDtypeStruct(shape, dtype)


def per_device(ensemble, obs_cell, obs_value, obs_var, patch_rows):
    chunks, meta = call(
        pack_kernel,
        (shaped(128, 40, 128), shaped(8, 128)),
        ensemble.transpose(1, 0, 2),
        obs_cell,
        obs_value,
        obs_var,
        patch_rows,
        scratch=[pltpu.VMEM((8, MEM, 1024), F32)],
        name="pack",
    )
    meta = lax.ppermute(meta, BOTH, [(s, PLACE[s]) for s in range(128)])
    recv = lax.all_to_all(chunks, BOTH, split_axis=0, concat_axis=0, tiled=True)
    x, obs = call(
        forecast_kernel,
        (shaped(CELLS, K), shaped(136, K)),
        recv,
        meta,
        scratch=[pltpu.VMEM((66, 16, K), F32)] * 2,
        name="forecast",
    )
    up = [(PLACE[s], PLACE[(s + 1) % 128]) for s in range(128)]
    down = [(b, a) for a, b in up]
    before = lax.ppermute(obs, BOTH, up)
    after = lax.ppermute(obs, BOTH, down)
    back = call(
        server_kernel,
        shaped(128, 24, 128),
        x,
        obs,
        before,
        after,
        scratch=[
            pltpu.VMEM((NOBS + CELLS, 3 * K), BF16),
            pltpu.VMEM((K, 3 * NOBS), BF16),
            pltpu.VMEM((3 * NOBS, K), BF16),
            pltpu.VMEM((3 * NOBS, K), BF16),
            pltpu.VMEM((CELLS, K), F32),
            pltpu.VMEM((8, K), F32),
        ],
        name="server",
    )
    back = lax.all_to_all(back, BOTH, split_axis=0, concat_axis=0, tiled=True)
    out = call(unpack_kernel, shaped(4, MEM, 1024), back, name="unpack")
    return out.transpose(1, 0, 2)


def solution(mesh):
    in_specs = (
        P("member", "lat", None),
        P(BOTH, None),
        P(BOTH, None),
        P(BOTH, None),
        P(BOTH, None),
    )
    return jax.shard_map(
        per_device,
        mesh=mesh,
        in_specs=in_specs,
        out_specs=P("member", "lat", None),
        check_vma=False,
    )
```

time: 170 us -> 134 us (0.79)
  Pallas kernels: 75.9 us -> 40.4 us
    pallas_call x4, Pallas kernels: 75.9 us -> 40.4 us  [call(): pl.pallas_call(kernel, out_shape=out_shape, scratch_shapes=scratch, compi...]
where the time goes in v2:
time: 134 us
  waiting for transfers between devices  42.5 us (32%)
  Pallas kernels  40.4 us (30%)
  blocking collectives  30 us (22%)
  starting transfers between devices  12.3 us (9%)
  local copies, waits for them, and re-layouts  8.61 us (6%)
    pallas_call x4, Pallas kernels, call(): pl.pallas_call(kernel, out_shape=out_shape, scratch_shapes=scratch, compi...  40.4 us
    all_to_all x1, waiting for transfers between devices, per_device(): recv = lax.all_to_all(chunks, BOTH, split_axis=0, concat_axis=0, tiled=True)  34.5 us
    all_to_all x1, blocking collectives, per_device(): back = lax.all_to_all(back, BOTH, split_axis=0, concat_axis=0, tiled=True)  30 us
    all_to_all x1, starting transfers between devices, per_device(): recv = lax.all_to_all(chunks, BOTH, split_axis=0, concat_axis=0, tiled=True)  11.1 us
    unnamed x11, local copies, waits for them, and re-layouts  5.4 us
    ppermute x1, waiting for transfers between devices, per_device(): after = lax.ppermute(obs, BOTH, down)  4.96 us
    transpose x1, local copies, waits for them, and re-layouts, per_device(): return out.transpose(1, 0, 2)  3.22 us
    ppermute x1, waiting for transfers between devices, per_device(): before = lax.ppermute(obs, BOTH, up)  3.01 us
  transfers between devices with their start and end apart: 4, of which 3 were waited for; matrix products, arithmetic and copies ran while one was open for 0% of the time, Pallas kernels for 0%

profile of v2, /device:TPU:0, one launch (start us, length us, event | category | flops | bytes accessed | tf_op | source)
XLA Modules:
  0.0 133.9 jit_solution(11888901577979735823)
XLA Ops:
  0.0 3.1 %copy.9 = f32[80,4,1024]{2,0,1:T(8,128)} copy(f32[80,4,1024]{2,1,0:T(4,128)} %param.5) | data formatting | bytes 2621440 | tf_op args[0]
  3.1 4.7 %pack.1 = (f32[128,40,128]{2,1,0:T(8,128)}, f32[8,128]{1,0:T(8,128)}) custom-call(f32[4,80,1024]{2,1,0:T(8,128)} %bitcast.4, s32[1,128]{1,0:T(1,128)} %cell_ref.1, f32[1,128]{1,0:T(1,128)} %value_ref.1, f32[1,128]{1,0:T(1,128)} %var_ref.1, s32[1,2]{1,0:T(1,128)} %rows_ref.1), custom_call_target="tpu_custom_call" | custom-call | tf_op jit(solution)/shard_map/pack/pallas_call | solution.py:326
  7.8 0.0 copy-start.4
  7.8 11.1 %all-to-all-start = ((f32[128,40,128]{2,1,0:T(8,128)}), f32[128,40,128]{2,1,0:T(8,128)S(1)}, u32[]{:S(2)}, u32[]{:S(2)}) async-start(f32[128,40,128]{2,1,0:T(8,128)} %get-tuple-element.9), calls=%async_computation | async-start | bytes 5242880 | tf_op jit(solution)/shard_map/all_to_all | solution.py:352
  19.0 0.0 copy-done.4
  19.0 0.7 collective-permute-start
  19.7 0.0 collective-permute-done.meta_ref
  19.7 0.0 copy-start.3
  19.7 34.5 %all-to-all-done.recv_ref = f32[128,40,128]{2,1,0:T(8,128)S(1)} async-done(((f32[128,40,128]{2,1,0:T(8,128)}), f32[128,40,128]{2,1,0:T(8,128)S(1)}, u32[]{:S(2)}, u32[]{:S(2)}) %all-to-all-start) | async-done | bytes 2621472 | tf_op jit(solution)/shard_map/all_to_all | solution.py:352
  54.2 0.0 copy-done.3
  54.2 0.0 copy-start
  54.2 1.5 %copy-done = f32[128,40,128]{2,1,0:T(8,128)} copy-done((f32[128,40,128]{2,1,0:T(8,128)}, f32[128,40,128]{2,1,0:T(8,128)S(1)}, u32[]{:S(2)}) %copy-start) | copy-done | bytes 2621464
  55.7 10.4 %forecast.1 = (f32[512,640]{1,0:T(8,128)}, f32[136,640]{1,0:T(8,128)}) custom-call(f32[128,40,128]{2,1,0:T(8,128)} %copy-done, f32[8,128]{1,0:T(8,128)} %copy-done.3), custom_call_target="tpu_custom_call" | custom-call | tf_op jit(solution)/shard_map/forecast/pallas_call | solution.py:326
  66.1 0.3 collective-permute-start.2
  66.5 0.2 collective-permute-start.1
  66.7 5.0 %collective-permute-done.2.after_ref = f32[136,640]{1,0:T(8,128)S(1)} collective-permute-done((f32[136,640]{1,0:T(8,128)}, f32[136,640]{1,0:T(8,128)S(1)}, u32[]{:S(2)}, u32[]{:S(2)}) %collective-permute-start.2) | collective-permute-done | bytes 348192 | tf_op jit(solution)/shard_map/ppermute | solution.py:364
  71.6 0.0 copy-start.1
  71.6 3.0 %collective-permute-done.1.before_ref = f32[136,640]{1,0:T(8,128)S(1)} collective-permute-done((f32[136,640]{1,0:T(8,128)}, f32[136,640]{1,0:T(8,128)S(1)}, u32[]{:S(2)}, u32[]{:S(2)}) %collective-permute-start.1) | collective-permute-done | bytes 348192 | tf_op jit(solution)/shard_map/ppermute | solution.py:363
  74.6 0.0 copy-start.2
  74.6 0.0 copy-done.1
  74.6 0.7 copy-done.2
  75.4 22.3 %server.1 = f32[128,24,128]{2,1,0:T(8,128)} custom-call(f32[512,640]{1,0:T(8,128)} %get-tuple-element.11.x_ref, f32[136,640]{1,0:T(8,128)} %get-tuple-element.12.own_ref, f32[136,640]{1,0:T(8,128)} %copy-done.2, f32[136,640]{1,0:T(8,128)} %copy-done.1), custom_call_target="tpu_custom_call" | custom-call | tf_op jit(solution)/shard_map/server/pallas_call | solution.py:326
  97.7 30.0 %all_to_all.10.recv_ref = f32[128,24,128]{2,1,0:T(8,128)} all-to-all(f32[128,24,128]{2,1,0:T(8,128)} %server.1), channel_id=1, replica_groups=mesh['member'=8,'lat'=16] {'member','lat'}, dimensions={0} | all-to-all | bytes 3145728 | tf_op jit(solution)/shard_map/all_to_all | solution.py:382
  127.7 3.0 %unpack.1 = f32[4,80,1024]{2,1,0:T(8,128)} custom-call(f32[128,24,128]{2,1,0:T(8,128)} %all_to_all.10.recv_ref), custom_call_target="tpu_custom_call" | custom-call | tf_op jit(solution)/shard_map/unpack/pallas_call | solution.py:326
  130.7 3.2 %copy.7 = f32[80,4,1024]{2,1,0:T(4,128)} copy(f32[80,4,1024]{2,0,1:T(8,128)} %bitcast.5) | data formatting | bytes 2621440 | tf_op jit(solution)/shard_map/transpose | solution.py:384
Async XLA Ops:
  7.8 11.2 %copy-start.4 = (f32[8,128]{1,0:T(8,128)S(1)}, f32[8,128]{1,0:T(8,128)}, u32[]{:S(2)}) copy-start(f32[8,128]{1,0:T(8,128)} %get-tuple-element.10) | copy-start | bytes 12292
  7.8 46.4 %all-to-all-start = ((f32[128,40,128]{2,1,0:T(8,128)}), f32[128,40,128]{2,1,0:T(8,128)S(1)}, u32[]{:S(2)}, u32[]{:S(2)}) async-start(f32[128,40,128]{2,1,0:T(8,128)} %get-tuple-element.9), calls=%async_computation | async-start | bytes 5242880 | tf_op jit(solution)/shard_map/all_to_all | solution.py:352
  19.0 0.7 collective-permute-start
  19.7 34.5 %copy-start.3 = (f32[8,128]{1,0:T(8,128)}, f32[8,128]{1,0:T(8,128)S(1)}, u32[]{:S(2)}) copy-start(f32[8,128]{1,0:T(8,128)S(1)} %collective-permute-done.meta_ref) | copy-start | bytes 12292
  54.2 1.5 %copy-start = (f32[128,40,128]{2,1,0:T(8,128)}, f32[128,40,128]{2,1,0:T(8,128)S(1)}, u32[]{:S(2)}) copy-start(f32[128,40,128]{2,1,0:T(8,128)S(1)} %all-to-all-done.recv_ref) | copy-start | bytes 7864324
  66.1 5.5 %collective-permute-start.2 = (f32[136,640]{1,0:T(8,128)}, f32[136,640]{1,0:T(8,128)S(1)}, u32[]{:S(2)}, u32[]{:S(2)}) collective-permute-start(f32[136,640]{1,0:T(8,128)} %get-tuple-element.12.own_ref), channel_id=1, source_target_pairs={{16,0},{1,16},{17,1},{2,17},{18,2},{3,18},{19,3},{35,19},{51,35},{... | collective-permute-start | bytes 1044488 | tf_op jit(solution)/shard_map/ppermute | solution.py:364
  66.5 8.1 %collective-permute-start.1 = (f32[136,640]{1,0:T(8,128)}, f32[136,640]{1,0:T(8,128)S(1)}, u32[]{:S(2)}, u32[]{:S(2)}) collective-permute-start(f32[136,640]{1,0:T(8,128)} %get-tuple-element.12.own_ref), channel_id=1, source_target_pairs={{0,16},{16,1},{1,17},{17,2},{2,18},{18,3},{3,19},{19,35},{35,51},{... | collective-permute-start | bytes 1044488 | tf_op jit(solution)/shard_map/ppermute | solution.py:363
  71.6 3.0 %copy-start.1 = (f32[136,640]{1,0:T(8,128)}, f32[136,640]{1,0:T(8,128)S(1)}, u32[]{:S(2)}) copy-start(f32[136,640]{1,0:T(8,128)S(1)} %collective-permute-done.2.after_ref) | copy-start | bytes 1044484
  74.6 0.7 copy-start.2

commit v3 on v2

--- a/solution.py
+++ b/solution.py
@@ -65,22 +65,30 @@
     return jnp.where(low, a, cross), jnp.where(low, cross, b)
 
 
-def pack_kernel(ens_ref, cell_ref, value_ref, var_ref, rows_ref, out_ref, meta_ref, ab):
-    meta_ref[...] = jnp.zeros_like(meta_ref)
-    meta_ref[0:1, :] = cell_ref[...].astype(F32)
-    meta_ref[1:2, :] = value_ref[...]
-    meta_ref[2:3, :] = var_ref[...]
-    meta_ref[3:4, :] = jnp.broadcast_to(rows_ref[0:1, 0:1].astype(F32), (1, 128))
-
-    def shift(i, carry):
-        rows = pl.ds(pl.multiple_of(i * 8, 8), 8)
+def pack_kernel(
+    ens_hbm, cell_hbm, value_hbm, var_hbm, rows_hbm, out_hbm, meta_ref,
+    ens, ab, stage, cell, value, var, rows_v, ens_sem, meta_sem, out_sem
+):
+    loads = [
+        pltpu.make_async_copy(ens_hbm.at[8 * i : 8 * i + 8], ens.at[8 * i : 8 * i + 8], ens_sem.at[i])
+        for i in range(10)
+    ]
+    smalls = [
+        pltpu.make_async_copy(src, dst, meta_sem.at[i])
+        for i, (src, dst) in enumerate(
+            ((cell_hbm, cell), (value_hbm, value), (var_hbm, var), (rows_hbm, rows_v))
+        )
+    ]
+    for copy in loads + smalls:
+        copy.start()
+    for i in range(10):
+        loads[i].wait()
+        rows = slice(8 * i, 8 * i + 8)
         for r in range(4):
-            src = ens_ref[r, rows, :]
+            src = ens[rows, r, :]
             ab[r, rows, :] = roll(src, 4)
             ab[4 + r, rows, :] = roll(src, -4)
-        return carry
-
-    lax.fori_loop(0, 10, shift, 0, unroll=2)
+    stores = []
     for g in range(8):
         cols = slice(g * 128, (g + 1) * 128)
         for b in range(5):
@@ -90,7 +98,22 @@
                 block = jnp.concatenate([ab[j, 64:80, cols] for j in range(8)], axis=0)
             block = block.T
             for w in range(16):
-                out_ref[PLACE[16 * g + w], 8 * b : 8 * b + 8, :] = block[8 * w : 8 * w + 8, :]
+                stage[PLACE[16 * g + w], 8 * b : 8 * b + 8, :] = block[8 * w : 8 * w + 8, :]
+        for base in sorted({PLACE[16 * g + w] // 4 * 4 for w in range(16)}):
+            part = slice(base, base + 4)
+            stores.append(
+                pltpu.make_async_copy(stage.at[part], out_hbm.at[part], out_sem.at[base // 4])
+            )
+            stores[-1].start()
+    for copy in smalls:
+        copy.wait()
+    meta_ref[...] = jnp.zeros_like(meta_ref)
+    meta_ref[0:1, :] = cell[...].astype(F32)
+    meta_ref[1:2, :] = value[...]
+    meta_ref[2:3, :] = var[...]
+    meta_ref[3:4, :] = jnp.broadcast_to(rows_v[0:1, 0:1].astype(F32), (1, 128))
+    for copy in stores:
+        copy.wait()
 
 
 def forecast_kernel(recv_ref, meta_ref, x_ref, obs_ref, fa, fb):
@@ -288,6 +311,8 @@
     coef = jnp.where(is_first, k0, k1)
     res[...] = (coef * x_ref[...] + (mean * (1.0 - coef) + drift)) + mm(left3(c_total), yt3[...])
 
+    low = lane_iota() < 64
+
     def pack(l, carry):
         def block(r, k):
             rows = pl.ds(pl.multiple_of(l * 32 + r * 8, 8), 8)
@@ -297,11 +322,15 @@
             for k in range(4):
                 outs = pair_swap(block(2 * half, k), block(2 * half + 1, k))
                 for j, out in enumerate(outs):
-                    out_ref[(2 * k + j) * 16 + l, 8 * half : 8 * half + 8, :] = out
+                    dest = (2 * k + j) * 16 + l
+                    out_ref[dest, 2 * half : 2 * half + 2, :, :] = out.reshape(2, 4, 128)
         ends = [block(r, 4) for r in range(4)]
         for j, out in enumerate(block_transpose(ends, 16)):
-            out_ref[j * 16 + l, 16:24, :] = out
-            out_ref[(4 + j) * 16 + l, 16:24, :] = roll(out, 64)
+            turned = roll(out, 64)
+            first_half = jnp.where(low, out, pltpu.roll(turned, 4, 0))
+            second_half = jnp.where(low, turned, pltpu.roll(out, 4, 0))
+            out_ref[j * 16 + l, 4, :, :] = first_half[0:4]
+            out_ref[(4 + j) * 16 + l, 4, :, :] = second_half[0:4]
         return carry
 
     lax.fori_loop(0, 16, pack, 0, unroll=2)
@@ -311,23 +340,36 @@
     for g in range(8):
         cols = slice(g * 128, (g + 1) * 128)
         for b in range(3):
-            block = jnp.concatenate(
-                [recv_ref[PLACE[16 * g + w], 8 * b : 8 * b + 8, :] for w in range(16)], axis=0
-            ).T
+            parts = []
+            for w in range(16):
+                src = PLACE[16 * g + w]
+                if b < 2:
+                    parts.append(recv_ref[src, 2 * b : 2 * b + 2, :, :].reshape(8, 128))
+                else:
+                    part = recv_ref[src, 4, :, :]
+                    parts.append(jnp.concatenate([part, roll(part, 64)], axis=0))
+            block = jnp.concatenate(parts, axis=0).T
             if b < 2:
-                out_ref[2 * b, 0:64, cols] = block[0:64]
-                out_ref[2 * b + 1, 0:64, cols] = block[64:128]
+                out_ref[0:64, 2 * b, cols] = block[0:64]
+                out_ref[0:64, 2 * b + 1, cols] = block[64:128]
             else:
                 for r in range(4):
-                    out_ref[r, 64:80, cols] = block[16 * r : 16 * r + 16]
-
-
-def call(kernel, out_shape, *args, scratch=(), name=None):
+                    out_ref[64:80, r, cols] = block[16 * r : 16 * r + 16]
+
+
+WHOLE = pl.BlockSpec(memory_space=pltpu.VMEM)
+THERE = pl.BlockSpec(memory_space=pltpu.HBM)
+
+
+def call(kernel, out_shape, *args, scratch=(), name=None, vmem=16, ins=None, outs=None, cost=None):
     return pl.pallas_call(
         kernel,
         out_shape=out_shape,
+        in_specs=ins or [WHOLE] * len(args),
+        out_specs=outs or jax.tree.map(lambda _: WHOLE, out_shape),
         scratch_shapes=scratch,
-        compiler_params=pltpu.CompilerParams(vmem_limit_bytes=56 * 1024 * 1024),
+        compiler_params=pltpu.CompilerParams(vmem_limit_bytes=vmem * 1024 * 1024),
+        cost_estimate=cost,
         name=name,
     )(*args)
 
@@ -340,13 +382,27 @@
     chunks, meta = call(
         pack_kernel,
         (shaped(128, 40, 128), shaped(8, 128)),
-        ensemble.transpose(1, 0, 2),
+        ensemble,
         obs_cell,
         obs_value,
         obs_var,
         patch_rows,
-        scratch=[pltpu.VMEM((8, MEM, 1024), F32)],
+        scratch=[
+            pltpu.VMEM((MEM, 4, 1024), F32),
+            pltpu.VMEM((8, MEM, 1024), F32),
+            pltpu.VMEM((128, 40, 128), F32),
+            pltpu.VMEM((1, 128), jnp.int32),
+            pltpu.VMEM((1, 128), F32),
+            pltpu.VMEM((1, 128), F32),
+            pltpu.VMEM((1, 2), jnp.int32),
+            pltpu.SemaphoreType.DMA((10,)),
+            pltpu.SemaphoreType.DMA((4,)),
+            pltpu.SemaphoreType.DMA((32,)),
+        ],
+        ins=[THERE] * 5,
+        outs=(THERE, WHOLE),
         name="pack",
+        vmem=58,
     )
     meta = lax.ppermute(meta, BOTH, [(s, PLACE[s]) for s in range(128)])
     recv = lax.all_to_all(chunks, BOTH, split_axis=0, concat_axis=0, tiled=True)
@@ -357,6 +413,7 @@
         meta,
         scratch=[pltpu.VMEM((66, 16, K), F32)] * 2,
         name="forecast",
+        vmem=12,
     )
     up = [(PLACE[s], PLACE[(s + 1) % 128]) for s in range(128)]
     down = [(b, a) for a, b in up]
@@ -364,7 +421,7 @@
     after = lax.ppermute(obs, BOTH, down)
     back = call(
         server_kernel,
-        shaped(128, 24, 128),
+        shaped(128, 5, 4, 128),
         x,
         obs,
         before,
@@ -378,10 +435,10 @@
             pltpu.VMEM((8, K), F32),
         ],
         name="server",
+        vmem=28,
     )
     back = lax.all_to_all(back, BOTH, split_axis=0, concat_axis=0, tiled=True)
-    out = call(unpack_kernel, shaped(4, MEM, 1024), back, name="unpack")
-    return out.transpose(1, 0, 2)
+    return call(unpack_kernel, shaped(MEM, 4, 1024), back, name="unpack", vmem=6)
 
 
 def solution(mesh):

time: 134 us -> 116 us (0.87)
  local copies, waits for them, and re-layouts: 8.61 us -> 0.01 us
  Pallas kernels: 40.4 us -> 34.8 us
  blocking collectives: 30 us -> 26.4 us
    pallas_call x4, Pallas kernels: 40.4 us -> 34.8 us  [call(): pl.pallas_call(kernel, out_shape=out_shape, in_specs=ins or [WHOLE] * len...]
    unnamed x11 -> x2, local copies, waits for them, and re-layouts: 5.4 us -> 0.01 us
    all_to_all x1, blocking collectives: 30 us -> 26.4 us  [per_device(): back = lax.all_to_all(back, BOTH, split_axis=0, concat_axis=0, tiled=True)]
    transpose x1 -> x0, local copies, waits for them, and re-layouts: 3.22 us -> none  [per_device(): return out.transpose(1, 0, 2)]
where the time goes in v3:
time: 116 us
  waiting for transfers between devices  42.3 us (36%)
  Pallas kernels  34.8 us (30%)
  blocking collectives  26.4 us (23%)
  starting transfers between devices  12.4 us (11%)
    pallas_call x4, Pallas kernels, call(): pl.pallas_call(kernel, out_shape=out_shape, in_specs=ins or [WHOLE] * len...  34.8 us
    all_to_all x1, waiting for transfers between devices, per_device(): recv = lax.all_to_all(chunks, BOTH, split_axis=0, concat_axis=0, tiled=True)  34.5 us
    all_to_all x1, blocking collectives, per_device(): back = lax.all_to_all(back, BOTH, split_axis=0, concat_axis=0, tiled=True)  26.4 us
    all_to_all x1, starting transfers between devices, per_device(): recv = lax.all_to_all(chunks, BOTH, split_axis=0, concat_axis=0, tiled=True)  11.1 us
    ppermute x1, waiting for transfers between devices, per_device(): after = lax.ppermute(obs, BOTH, down)  4.63 us
    ppermute x1, waiting for transfers between devices, per_device(): before = lax.ppermute(obs, BOTH, up)  3.12 us
  transfers between devices with their start and end apart: 4, of which 3 were waited for; matrix products, arithmetic and copies ran while one was open for 0% of the time, Pallas kernels for 0%

profile of v3, /device:TPU:0, one launch (start us, length us, event | category | flops | bytes accessed | tf_op | source)
XLA Modules:
  0.0 115.9 jit_solution(1810990796671599508)
XLA Ops:
  0.0 5.0 %pack.1 = (f32[128,40,128]{2,1,0:T(8,128)}, f32[8,128]{1,0:T(8,128)}) custom-call(f32[80,4,1024]{2,1,0:T(4,128)} %ens_hbm.1, s32[1,128]{1,0:T(1,128)} %cell_hbm.1, f32[1,128]{1,0:T(1,128)} %value_hbm.1, f32[1,128]{1,0:T(1,128)} %var_hbm.1, s32[1,2]{1,0:T(1,128)} %rows_hbm.1), custom_call_target="tpu_custom_call" | custom-call | tf_op jit(solution)/shard_map/pack/pallas_call | solution.py:365
  5.0 0.0 copy-start
  5.0 11.1 %all-to-all-start = ((f32[128,40,128]{2,1,0:T(8,128)}), f32[128,40,128]{2,1,0:T(8,128)S(1)}, u32[]{:S(2)}, u32[]{:S(2)}) async-start(f32[128,40,128]{2,1,0:T(8,128)} %get-tuple-element.9), calls=%async_computation | async-start | bytes 5242880 | tf_op jit(solution)/shard_map/all_to_all | solution.py:408
  16.2 0.0 copy-done
  16.2 0.7 collective-permute-start
  16.8 0.0 collective-permute-done.meta_ref
  16.9 34.5 %all-to-all-done.recv_ref = f32[128,40,128]{2,1,0:T(8,128)S(1)} async-done(((f32[128,40,128]{2,1,0:T(8,128)}), f32[128,40,128]{2,1,0:T(8,128)S(1)}, u32[]{:S(2)}, u32[]{:S(2)}) %all-to-all-start) | async-done | bytes 2621472 | tf_op jit(solution)/shard_map/all_to_all | solution.py:408
  51.4 7.9 %forecast.1 = (f32[512,640]{1,0:T(8,128)S(1)}, f32[136,640]{1,0:T(8,128)S(1)}) custom-call(f32[128,40,128]{2,1,0:T(8,128)S(1)} %all-to-all-done.recv_ref, f32[8,128]{1,0:T(8,128)S(1)} %collective-permute-done.meta_ref), custom_call_target="tpu_custom_call" | custom-call | tf_op jit(solution)/shard_map/forecast/pallas_call | solution.py:365
  59.3 0.4 collective-permute-start.2
  59.7 0.2 collective-permute-start.1
  59.9 4.6 %collective-permute-done.2.after_ref = f32[136,640]{1,0:T(8,128)S(1)} collective-permute-done((f32[136,640]{1,0:T(8,128)S(1)}, f32[136,640]{1,0:T(8,128)S(1)}, u32[]{:S(2)}, u32[]{:S(2)}) %collective-permute-start.2) | collective-permute-done | bytes 348192 | tf_op jit(solution)/shard_map/ppermute | solution.py:421
  64.5 3.1 %collective-permute-done.1.before_ref = f32[136,640]{1,0:T(8,128)S(1)} collective-permute-done((f32[136,640]{1,0:T(8,128)S(1)}, f32[136,640]{1,0:T(8,128)S(1)}, u32[]{:S(2)}, u32[]{:S(2)}) %collective-permute-start.1) | collective-permute-done | bytes 348192 | tf_op jit(solution)/shard_map/ppermute | solution.py:420
  67.6 19.6 %server.1 = f32[128,5,4,128]{3,2,1,0:T(4,128)S(1)} custom-call(f32[512,640]{1,0:T(8,128)S(1)} %get-tuple-element.11.x_ref, f32[136,640]{1,0:T(8,128)S(1)} %get-tuple-element.12.own_ref, f32[136,640]{1,0:T(8,128)S(1)} %collective-permute-done.1.before_ref, f32[136,640]{1,0:T(8,128)S(1)} %collective-permute-done.2.after_ref), custom_call_target="tpu_custom_call" | custom-call | tf_op jit(solution)/shard_map/server/pallas_call | solution.py:365
  87.3 26.4 %all_to_all.10.recv_ref = f32[128,5,4,128]{3,2,1,0:T(4,128)S(1)} all-to-all(f32[128,5,4,128]{3,2,1,0:T(4,128)S(1)} %server.1), channel_id=1, replica_groups=mesh['member'=8,'lat'=16] {'member','lat'}, dimensions={0} | all-to-all | bytes 2621440 | tf_op jit(solution)/shard_map/all_to_all | solution.py:440
  113.7 2.2 %unpack.1 = f32[80,4,1024]{2,1,0:T(4,128)} custom-call(f32[128,5,4,128]{3,2,1,0:T(4,128)S(1)} %all_to_all.10.recv_ref), custom_call_target="tpu_custom_call" | custom-call | tf_op jit(solution)/shard_map/unpack/pallas_call | solution.py:365
Async XLA Ops:
  5.0 11.2 %copy-start = (f32[8,128]{1,0:T(8,128)S(1)}, f32[8,128]{1,0:T(8,128)}, u32[]{:S(2)}) copy-start(f32[8,128]{1,0:T(8,128)} %get-tuple-element.10) | copy-start | bytes 12292
  5.0 46.4 %all-to-all-start = ((f32[128,40,128]{2,1,0:T(8,128)}), f32[128,40,128]{2,1,0:T(8,128)S(1)}, u32[]{:S(2)}, u32[]{:S(2)}) async-start(f32[128,40,128]{2,1,0:T(8,128)} %get-tuple-element.9), calls=%async_computation | async-start | bytes 5242880 | tf_op jit(solution)/shard_map/all_to_all | solution.py:408
  16.2 0.7 collective-permute-start
  59.3 5.2 %collective-permute-start.2 = (f32[136,640]{1,0:T(8,128)S(1)}, f32[136,640]{1,0:T(8,128)S(1)}, u32[]{:S(2)}, u32[]{:S(2)}) collective-permute-start(f32[136,640]{1,0:T(8,128)S(1)} %get-tuple-element.12.own_ref), channel_id=1, source_target_pairs={{16,0},{1,16},{17,1},{2,17},{18,2},{3,18},{19,3},{35,19},{51,35},{... | collective-permute-start | bytes 1044488 | tf_op jit(solution)/shard_map/ppermute | solution.py:421
  59.7 7.9 %collective-permute-start.1 = (f32[136,640]{1,0:T(8,128)S(1)}, f32[136,640]{1,0:T(8,128)S(1)}, u32[]{:S(2)}, u32[]{:S(2)}) collective-permute-start(f32[136,640]{1,0:T(8,128)S(1)} %get-tuple-element.12.own_ref), channel_id=1, source_target_pairs={{0,16},{16,1},{1,17},{17,2},{2,18},{18,3},{3,19},{19,35},{35,51},{... | collective-permute-start | bytes 1044488 | tf_op jit(solution)/shard_map/ppermute | solution.py:420

commit v4 on v3

--- a/solution.py
+++ b/solution.py
@@ -137,7 +137,7 @@
             fa[1 + 4 * l + r, 8 * t : 8 * t + 8, 512:640] = out
         return carry
 
-    lax.fori_loop(0, 16, place, 0, unroll=2)
+    lax.fori_loop(0, 16, place, 0, unroll=4)
 
     def advance(src, row):
         c = src[row]
@@ -154,13 +154,13 @@
             dst[i + 1] = advance(src, i + 1)
             return carry
 
-        lax.fori_loop(0, 64, move, 0, unroll=4)
+        lax.fori_loop(0, 64, move, 0, unroll=8)
 
     def last(i, carry):
         x_ref[pl.ds(pl.multiple_of(i * 8, 8), 8), :] = advance(fb, i + 1)[4:12, :]
         return carry
 
-    lax.fori_loop(0, 64, last, 0, unroll=4)
+    lax.fori_loop(0, 64, last, 0, unroll=8)
     cell = jnp.concatenate([meta_ref[0:1, :], jnp.zeros((7, 128), F32)], axis=0).T[:, 0:1]
     pick = jnp.where(
         lax.broadcasted_iota(jnp.int32, (128, CELLS), 1) == cell.astype(jnp.int32), 1.0, 0.0
@@ -200,140 +200,214 @@
     return jnp.broadcast_to(column, (column.shape[0], 128)).T[0:1, :]
 
 
+def prepare_kernel(x_ref, own_ref, x3_ref, own3_ref, y_ref, tu_ref, mean_ref):
+    mean = jnp.sum(x_ref[...], axis=1, keepdims=True) * (1.0 / K)
+    mean_ref[...] = mean
+    high, low = split(x_ref[...] - mean)
+    x3_ref[:, 0:K] = high
+    x3_ref[:, K : 2 * K] = high
+    x3_ref[:, 2 * K :] = low
+    obs = own_ref[0:128, :]
+    spread = obs - jnp.sum(obs, axis=1, keepdims=True) * (1.0 / K)
+    high, low = split(spread)
+    own3_ref[:, 0:K] = high
+    own3_ref[:, K : 2 * K] = high
+    own3_ref[:, 2 * K :] = low
+    y_ref[...] = spread.T.astype(BF16)
+    right = jnp.concatenate([high, low, high], axis=1)
+    tu_ref[0:128, :] = mm_nt(own3_ref[...], right)
+    tu_ref[128:, :] = mm_nt(x3_ref[...], right)
+
+
+def mm_nt(left, right):
+    return lax.dot_general(left, right, (((1,), (1,)), ((), ())), preferred_element_type=F32)
+
+
 def server_kernel(
-    x_ref, own_ref, before_ref, after_ref, out_ref, xy3, y3, yt3, g3, res, sums
+    x_ref, own_ref, x3_ref, own3_ref, y_ref, tu_ref, mean_ref, before_ref, after_ref, out_ref,
+    near3, yr, y2, yt3, g2, u_ref, c_ref, d_ref, res
 ):
-    mean = jnp.sum(x_ref[...], axis=1, keepdims=True) * (1.0 / K)
-    xa = x_ref[...] - mean
-    x_high, x_low = split(xa)
-    xy3[NOBS:, 0:K] = x_high
-    xy3[NOBS:, K : 2 * K] = x_high
-    xy3[NOBS:, 2 * K :] = x_low
     innov, var, orow, ocol = [], [], [], []
-    for j, ref in enumerate((before_ref, own_ref, after_ref)):
+    yt3[0:128, :] = own3_ref[:, 0:K]
+    yt3[NOBS : NOBS + 128, :] = own3_ref[:, 2 * K :]
+    yt3[2 * NOBS : 2 * NOBS + 128, :] = own3_ref[:, 0:K]
+    y2[:, 0:128] = y_ref[...]
+    y2[:, NOBS : NOBS + 128] = y_ref[...]
+    for j, ref in enumerate((own_ref, before_ref, after_ref)):
         obs = ref[0:128, :]
         obs_mean = jnp.sum(obs, axis=1, keepdims=True) * (1.0 / K)
-        spread = obs - obs_mean
-        high, low = split(spread)
-        rows = slice(j * 128, (j + 1) * 128)
-        xy3[rows, 0:K] = high
-        xy3[rows, K : 2 * K] = high
-        xy3[rows, 2 * K :] = low
-        for n, part in enumerate((high, low, high)):
-            yt3[n * NOBS + j * 128 : n * NOBS + (j + 1) * 128, :] = part
-        y_high, y_low = split(spread.T)
-        for n, part in enumerate((y_high, y_high, y_low)):
-            y3[:, n * NOBS + j * 128 : n * NOBS + (j + 1) * 128] = part
+        if j:
+            spread = obs - obs_mean
+            high, low = split(spread)
+            rows = slice((j - 1) * 128, j * 128)
+            for n, (left, right) in enumerate(((high, high), (high, low), (low, high))):
+                near3[rows, n * K : (n + 1) * K] = left
+                yr[rows, n * K : (n + 1) * K] = right
+                yt3[n * NOBS + j * 128 : n * NOBS + (j + 1) * 128, :] = right
+            turned = spread.T.astype(BF16)
+            y2[:, j * 128 : (j + 1) * 128] = turned
+            y2[:, NOBS + j * 128 : NOBS + (j + 1) * 128] = turned
         cell = ref[128:129, 0:128].astype(jnp.int32)
         innov.append(ref[129:130, 0:128] - as_row(obs_mean))
         var.append(ref[130:131, 0:128])
         orow.append((cell // 8).astype(F32))
-        ocol.append((cell % 8).astype(F32) + 8.0 * (j - 1))
+        ocol.append((cell % 8).astype(F32) + (0.0, -8.0, 8.0)[j])
     innov, var, orow, ocol = (jnp.concatenate(v, axis=1) for v in (innov, var, orow, ocol))
-    right = jnp.concatenate(
-        [xy3[0:NOBS, 0:K], xy3[0:NOBS, 2 * K :], xy3[0:NOBS, 0:K]], axis=1
-    )
-    tu = lax.dot_general(
-        xy3[...], right, (((1,), (1,)), ((), ())), preferred_element_type=F32
-    )
-    t_mat, u_mat = tu[0:NOBS], tu[NOBS:]
 
     first = own_ref[131:132, 0:1]
+    swap = first > 32.0
+    swap_scalar = jnp.max(first) > 32.0
+    eye128 = lax.broadcasted_iota(jnp.int32, (128, 128), 0) == lax.broadcasted_iota(
+        jnp.int32, (128, 128), 1
+    )
     eye = jnp.where(
         lax.broadcasted_iota(jnp.int32, (NOBS, NOBS), 0)
         == lax.broadcasted_iota(jnp.int32, (NOBS, NOBS), 1),
         1.0,
         0.0,
     )
-    cell_row = (lax.broadcasted_iota(jnp.int32, (CELLS, 1), 0) // 8).astype(F32)
-    is_first = cell_row < first
-    parts = []
-    for patch in range(2):
-        lower = jnp.zeros_like(first) if patch == 0 else first
-        upper = (first if patch == 0 else jnp.full_like(first, 64.0)) - 1.0
-        gap_row = jnp.maximum(jnp.maximum(lower - orow, orow - upper), 0.0) * (1.0 / 16.0)
+    both = range(2)
+    zero, full = jnp.zeros_like(first), jnp.full_like(first, 64.0)
+    lower = [jnp.where(swap, first, zero), jnp.where(swap, zero, first)]
+    upper = [jnp.where(swap, full, first) - 1.0, jnp.where(swap, first, full) - 1.0]
+    sg, sgd, sg_col, sgd_col, diag = [], [], [], [], []
+    yt = yt3[0:NOBS, :].astype(F32) + yt3[NOBS : 2 * NOBS, :].astype(F32)
+    for p in both:
+        gap_row = jnp.maximum(jnp.maximum(lower[p] - orow, orow - upper[p]), 0.0) * (1.0 / 16.0)
         gap_col = jnp.maximum(jnp.maximum(-ocol, ocol - 7.0), 0.0) * (1.0 / 8.0)
         g = jnp.exp(-gap_row * gap_row - gap_col * gap_col) / var
-        sg = jnp.sqrt(g)
-        sgd = sg * innov
-        cols = jnp.concatenate([sg, sgd, g, jnp.zeros((5, NOBS), F32)], axis=0).T
-        sg_col, sgd_col, g_col = cols[:, 0:1], cols[:, 1:2], cols[:, 2:3]
-        scaled = (yt3[0:NOBS, :].astype(F32) + yt3[NOBS : 2 * NOBS, :].astype(F32)) * g_col
-        g3[...] = right3(scaled)
-        sums[...] = jnp.zeros_like(sums)
-
-        def gram(i, carry):
-            rows = pl.ds(pl.multiple_of(i * 128, 128), 128)
-            block = jnp.abs(mm(y3[rows, :], g3[...]))
-            sums[...] += jnp.sum(block.reshape(16, 8, K), axis=0)
-            return carry
-
-        lax.fori_loop(0, 5, gram, 0)
-        bound = (K - 1.0) + jnp.max(
-            jnp.sum(sums[...], axis=0, keepdims=True), axis=1, keepdims=True
+        sg.append(jnp.sqrt(g))
+        sgd.append(sg[p] * innov)
+        cols = jnp.concatenate([sg[p], sgd[p], g, jnp.zeros((5, NOBS), F32)], axis=0).T
+        sg_col.append(cols[:, 0:1])
+        sgd_col.append(cols[:, 1:2])
+        scaled = yt * cols[:, 2:3]
+        diag.append(jnp.sum(scaled * yt, axis=0, keepdims=True))
+        high, low = split(scaled)
+        g2[0:NOBS, p * K : (p + 1) * K] = high
+        g2[NOBS:, p * K : (p + 1) * K] = low
+
+    tu = mm_nt(near3[...], yr[...])
+    cross = mm_nt(own3_ref[...], yr[...])
+    t_mat = jnp.concatenate(
+        [
+            jnp.concatenate([tu_ref[0:128, :], cross], axis=1),
+            jnp.concatenate([cross.T, tu], axis=1),
+        ],
+        axis=0,
+    )
+    u_ref[:, 0:128] = tu_ref[128:, :]
+    u_ref[:, 128:] = mm_nt(x3_ref[...], yr[...])
+
+    sums = []
+    for n in range(5):
+        block = jnp.abs(mm(y2[...], g2[:, n * 256 : (n + 1) * 256]))
+        for half in range(2):
+            own = (2 * n + half) % 5
+            part = block[:, half * 128 : (half + 1) * 128]
+            rows = [part[i * 128 : (i + 1) * 128] for i in range(5)]
+            rows[own] = jnp.where(eye128, 0.0, rows[own])
+            total = (rows[0] + rows[1]) + (rows[2] + rows[3]) + rows[4]
+            sums.append(jnp.sum(total, axis=0, keepdims=True))
+    inv, q0, a1, m20, z20, z30 = [], [], [], [], [], []
+    for p in both:
+        total = jnp.concatenate(sums[5 * p : 5 * p + 5], axis=1) + diag[p]
+        bound = (K - 1.0) + jnp.max(total, axis=1, keepdims=True)
+        inv.append(1.0 / bound)
+        q0.append((K - 1.0) * inv[p])
+        a1.append(1.5 - 0.5 * q0[p])
+        m20.append(1.5 - 0.5 * q0[p] * a1[p] * a1[p])
+        z20.append(a1[p] * m20[p])
+        z30.append(z20[p] * (1.5 - 0.5 * q0[p] * z20[p] * z20[p]))
+    s = [(sg_col[p] * inv[p]) * t_mat * sg[p] for p in both]
+    s_left = [left3(s[p]) for p in both]
+    s2 = [mm(s_left[p], right3(s[p])) for p in both]
+    k2 = [
+        -0.5
+        * (
+            (a1[p] * a1[p] - q0[p] * a1[p]) * eye
+            + (0.25 * q0[p] - a1[p]) * s[p]
+            + 0.25 * s2[p]
         )
-        inv = 1.0 / bound
-        q0 = (K - 1.0) * inv
-        a1 = 1.5 - 0.5 * q0
-        m20 = 1.5 - 0.5 * q0 * a1 * a1
-        z20 = a1 * m20
-        z30 = z20 * (1.5 - 0.5 * q0 * z20 * z20)
-        s = (sg_col * inv) * t_mat * sg
-        s_left = left3(s)
-        s2 = mm(s_left, right3(s))
-        k2 = -0.5 * ((a1 * a1 - q0 * a1) * eye + (0.25 * q0 - a1) * s + 0.25 * s2)
-        m2 = m20 * eye + mm(s_left, right3(k2))
-        kz2 = a1 * k2 - 0.5 * m2
-        z2 = z20 * eye + mm(s_left, right3(kz2))
-        z2_right = right3(z2)
-        v = jnp.concatenate(
-            [u_mat[128 * patch : 128 * patch + 384] * sg, jnp.broadcast_to(sgd, (8, NOBS))],
+        for p in both
+    ]
+    m2 = [m20[p] * eye + mm(s_left[p], right3(k2[p])) for p in both]
+    kz2 = [a1[p] * k2[p] - 0.5 * m2[p] for p in both]
+    z2 = [z20[p] * eye + mm(s_left[p], right3(kz2[p])) for p in both]
+    z2_right = [right3(z2[p]) for p in both]
+    size = (256, 384)
+    start = [
+        pl.multiple_of(jnp.where(swap_scalar, 256, 0), 128),
+        pl.multiple_of(jnp.where(swap_scalar, 0, 128), 128),
+    ]
+    v = [
+        jnp.concatenate(
+            [u_ref[pl.ds(start[p], size[p]), :] * sg[p], jnp.broadcast_to(sgd[p], (8, NOBS))],
             axis=0,
         )
-        w1 = mm(left3(v), z2_right)
-        w2 = mm(left3(w1), z2_right)
-        tail = 1.5 * v - (0.5 * q0) * (w2 + z20 * w1 + (z20 * z20) * v)
-        hv = mm(left3(-0.5 * w2), z2_right) + mm(left3(tail), right3(kz2))
-        u_col = z30 * sgd_col + jnp.sum(hv[384:385, :] * s, axis=1, keepdims=True)
-        su = jnp.sum(u_col * s, axis=0, keepdims=True)
+        for p in both
+    ]
+    w1 = [mm(left3(v[p]), z2_right[p]) for p in both]
+    w2 = [mm(left3(w1[p]), z2_right[p]) for p in both]
+    tail = [
+        1.5 * v[p] - (0.5 * q0[p]) * (w2[p] + z20[p] * w1[p] + (z20[p] * z20[p]) * v[p])
+        for p in both
+    ]
+    hv = [
+        mm(
+            jnp.concatenate([left3(-0.5 * w2[p]), left3(tail[p])], axis=1),
+            jnp.concatenate([z2_right[p], right3(kz2[p])], axis=0),
+        )
+        for p in both
+    ]
+    scale = [jnp.sqrt(q0[p]) for p in both]
+    for p in (1, 0):
+        n = size[p]
+        rows = pl.ds(start[p], n)
+        u_col = z30[p] * sgd_col[p] + jnp.sum(hv[p][n : n + 1] * s[p], axis=1, keepdims=True)
+        su = jnp.sum(u_col * s[p], axis=0, keepdims=True)
         u = as_row(u_col)
-        drift = inv * jnp.sum((z30 * u) * v[0:384] + su * hv[0:384], axis=1, keepdims=True)
-        scale = jnp.sqrt(q0)
-        parts.append((hv[0:384] * (sg * (scale * inv)), drift, scale * z30))
-    (c0, d0, k0), (c1, d1, k1) = parts
-    middle = is_first[128:384]
-    c_total = jnp.concatenate(
-        [c0[0:128], jnp.where(middle, c0[128:384], c1[0:256]), c1[256:384]], axis=0
-    )
-    drift = jnp.concatenate(
-        [d0[0:128], jnp.where(middle, d0[128:384], d1[0:256]), d1[256:384]], axis=0
-    )
-    coef = jnp.where(is_first, k0, k1)
-    res[...] = (coef * x_ref[...] + (mean * (1.0 - coef) + drift)) + mm(left3(c_total), yt3[...])
-
+        drift = inv[p] * jnp.sum(
+            (z30[p] * u) * v[p][0:n] + su * hv[p][0:n], axis=1, keepdims=True
+        )
+        part = hv[p][0:n] * (sg[p] * (scale[p] * inv[p]))
+        if p == 0:
+            cell_row = (
+                (lax.broadcasted_iota(jnp.int32, (n, 1), 0) + start[p]) // 8
+            ).astype(F32)
+            inside = (cell_row >= lower[0]) & (cell_row <= upper[0])
+            part = jnp.where(inside, part, c_ref[rows, :])
+            drift = jnp.where(inside, drift, d_ref[rows, :])
+        c_ref[rows, :] = part
+        d_ref[rows, :] = drift
+    cell_row = (lax.broadcasted_iota(jnp.int32, (CELLS, 1), 0) // 8).astype(F32)
+    inside = (cell_row >= lower[0]) & (cell_row <= upper[0])
+    coef = jnp.where(inside, scale[0] * z30[0], scale[1] * z30[1])
+    base = mean_ref[...] * (1.0 - coef) + d_ref[...]
     low = lane_iota() < 64
-
-    def pack(l, carry):
-        def block(r, k):
-            rows = pl.ds(pl.multiple_of(l * 32 + r * 8, 8), 8)
-            return res[rows, k * 128 : (k + 1) * 128]
-
-        for half in range(2):
-            for k in range(4):
-                outs = pair_swap(block(2 * half, k), block(2 * half + 1, k))
-                for j, out in enumerate(outs):
-                    dest = (2 * k + j) * 16 + l
-                    out_ref[dest, 2 * half : 2 * half + 2, :, :] = out.reshape(2, 4, 128)
-        ends = [block(r, 4) for r in range(4)]
-        for j, out in enumerate(block_transpose(ends, 16)):
-            turned = roll(out, 64)
-            first_half = jnp.where(low, out, pltpu.roll(turned, 4, 0))
-            second_half = jnp.where(low, turned, pltpu.roll(out, 4, 0))
-            out_ref[j * 16 + l, 4, :, :] = first_half[0:4]
-            out_ref[(4 + j) * 16 + l, 4, :, :] = second_half[0:4]
-        return carry
-
-    lax.fori_loop(0, 16, pack, 0, unroll=2)
+    for i in range(4):
+        rows = slice(i * 128, (i + 1) * 128)
+        res[rows, :] = (
+            coef[rows] * x_ref[rows, :] + base[rows] + mm(left3(c_ref[rows, :]), yt3[...])
+        )
+        for l in range(4 * i, 4 * i + 4):
+
+            def block(r, k):
+                return res[32 * l + 8 * r : 32 * l + 8 * r + 8, k * 128 : (k + 1) * 128]
+
+            for half in range(2):
+                for k in range(4):
+                    outs = pair_swap(block(2 * half, k), block(2 * half + 1, k))
+                    for j, out in enumerate(outs):
+                        dest = (2 * k + j) * 16 + l
+                        out_ref[dest, 2 * half : 2 * half + 2, :, :] = out.reshape(2, 4, 128)
+            ends = [block(r, 4) for r in range(4)]
+            for j, out in enumerate(block_transpose(ends, 16)):
+                turned = roll(out, 64)
+                first_half = jnp.where(low, out, pltpu.roll(turned, 4, 0))
+                second_half = jnp.where(low, turned, pltpu.roll(out, 4, 0))
+                out_ref[j * 16 + l, 4, :, :] = first_half[0:4]
+                out_ref[(4 + j) * 16 + l, 4, :, :] = second_half[0:4]
 
 
 def unpack_kernel(recv_ref, out_ref):
@@ -419,23 +493,42 @@
     down = [(b, a) for a, b in up]
     before = lax.ppermute(obs, BOTH, up)
     after = lax.ppermute(obs, BOTH, down)
+    own = call(
+        prepare_kernel,
+        (
+            shaped(CELLS, 3 * K, dtype=BF16),
+            shaped(128, 3 * K, dtype=BF16),
+            shaped(K, 128, dtype=BF16),
+            shaped(128 + CELLS, 128),
+            shaped(CELLS, 1),
+        ),
+        x,
+        obs,
+        name="prepare",
+        vmem=6,
+        cost=pl.CostEstimate(flops=2 * K * K * 128 * 3, bytes_accessed=8 << 20, transcendentals=0),
+    )
     back = call(
         server_kernel,
         shaped(128, 5, 4, 128),
         x,
         obs,
+        *own,
         before,
         after,
         scratch=[
-            pltpu.VMEM((NOBS + CELLS, 3 * K), BF16),
-            pltpu.VMEM((K, 3 * NOBS), BF16),
+            pltpu.VMEM((256, 3 * K), BF16),
+            pltpu.VMEM((256, 3 * K), BF16),
+            pltpu.VMEM((K, 2 * NOBS), BF16),
             pltpu.VMEM((3 * NOBS, K), BF16),
-            pltpu.VMEM((3 * NOBS, K), BF16),
+            pltpu.VMEM((2 * NOBS, 2 * K), BF16),
+            pltpu.VMEM((CELLS, NOBS), F32),
+            pltpu.VMEM((CELLS, NOBS), F32),
+            pltpu.VMEM((CELLS, 1), F32),
             pltpu.VMEM((CELLS, K), F32),
-            pltpu.VMEM((8, K), F32),
         ],
         name="server",
-        vmem=28,
+        vmem=32,
     )
     back = lax.all_to_all(back, BOTH, split_axis=0, concat_axis=0, tiled=True)
     return call(unpack_kernel, shaped(MEM, 4, 1024), back, name="unpack", vmem=6)

time: 116 us -> 107 us (0.922)
  Pallas kernels: 34.8 us -> 27.2 us
    pallas_call x4 -> x5, Pallas kernels: 34.8 us -> 27.2 us  [call(): pl.pallas_call(kernel, out_shape=out_shape, in_specs=ins or [WHOLE] * len...]
  transfers between devices with their start and end apart: 4 -> 4, of which waited for: 3 -> 3; matrix products, arithmetic and copies ran while one was open for 0% -> 0% of each run, Pallas kernels for 0% -> 1%
where the time goes in v4:
time: 107 us
  waiting for transfers between devices  41.2 us (39%)
  Pallas kernels  27.2 us (25%)
  blocking collectives  26.4 us (25%)
  starting transfers between devices  12.4 us (12%)
    all_to_all x1, waiting for transfers between devices, per_device(): recv = lax.all_to_all(chunks, BOTH, split_axis=0, concat_axis=0, tiled=True)  34.5 us
    pallas_call x5, Pallas kernels, call(): pl.pallas_call(kernel, out_shape=out_shape, in_specs=ins or [WHOLE] * len...  27.2 us
    all_to_all x1, blocking collectives, per_device(): back = lax.all_to_all(back, BOTH, split_axis=0, concat_axis=0, tiled=True)  26.4 us
    all_to_all x1, starting transfers between devices, per_device(): recv = lax.all_to_all(chunks, BOTH, split_axis=0, concat_axis=0, tiled=True)  11.1 us
    ppermute x1, waiting for transfers between devices, per_device(): after = lax.ppermute(obs, BOTH, down)  3.55 us
    ppermute x1, waiting for transfers between devices, per_device(): before = lax.ppermute(obs, BOTH, up)  3.12 us
  transfers between devices with their start and end apart: 4, of which 3 were waited for; matrix products, arithmetic and copies ran while one was open for 0% of the time, Pallas kernels for 1%

profile of v4, /device:TPU:0, one launch (start us, length us, event | category | flops | bytes accessed | tf_op | source)
XLA Modules:
  0.0 107.2 jit_solution(70728362955439067)
XLA Ops:
  0.0 5.0 %pack.1 = (f32[128,40,128]{2,1,0:T(8,128)}, f32[8,128]{1,0:T(8,128)}) custom-call(f32[80,4,1024]{2,1,0:T(4,128)} %ens_hbm.1, s32[1,128]{1,0:T(1,128)} %cell_hbm.1, f32[1,128]{1,0:T(1,128)} %value_hbm.1, f32[1,128]{1,0:T(1,128)} %var_hbm.1, s32[1,2]{1,0:T(1,128)} %rows_hbm.1), custom_call_target="tpu_custom_call" | custom-call | tf_op jit(solution)/shard_map/pack/pallas_call | solution.py:439
  5.0 0.0 copy-start
  5.0 11.1 %all-to-all-start = ((f32[128,40,128]{2,1,0:T(8,128)}), f32[128,40,128]{2,1,0:T(8,128)S(1)}, u32[]{:S(2)}, u32[]{:S(2)}) async-start(f32[128,40,128]{2,1,0:T(8,128)} %get-tuple-element.14), calls=%async_computation | async-start | bytes 5242880 | tf_op jit(solution)/shard_map/all_to_all | solution.py:482
  16.2 0.0 copy-done
  16.2 0.7 collective-permute-start
  16.9 0.0 collective-permute-done.meta_ref
  16.9 34.5 %all-to-all-done.recv_ref = f32[128,40,128]{2,1,0:T(8,128)S(1)} async-done(((f32[128,40,128]{2,1,0:T(8,128)}), f32[128,40,128]{2,1,0:T(8,128)S(1)}, u32[]{:S(2)}, u32[]{:S(2)}) %all-to-all-start) | async-done | bytes 2621472 | tf_op jit(solution)/shard_map/all_to_all | solution.py:482
  51.4 7.1 %forecast.1 = (f32[512,640]{1,0:T(8,128)S(1)}, f32[136,640]{1,0:T(8,128)S(1)}) custom-call(f32[128,40,128]{2,1,0:T(8,128)S(1)} %all-to-all-done.recv_ref, f32[8,128]{1,0:T(8,128)S(1)} %collective-permute-done.meta_ref), custom_call_target="tpu_custom_call" | custom-call | tf_op jit(solution)/shard_map/forecast/pallas_call | solution.py:439
  58.5 0.4 collective-permute-start.2
  58.9 0.2 collective-permute-start.1
  59.1 1.1 %prepare.1 = (bf16[512,1920]{1,0:T(8,128)(2,1)S(1)}, bf16[128,1920]{1,0:T(8,128)(2,1)S(1)}, bf16[640,128]{1,0:T(8,128)(2,1)S(1)}, f32[640,128]{1,0:T(8,128)S(1)}, f32[512,1]{1,0:T(8,128)S(1)}) custom-call(f32[512,640]{1,0:T(8,128)S(1)} %get-tuple-element.16.x_ref, f32[136,640]{1,0:T(8,128)S(1)} %get-tuple-element.17.own_ref), custom_call_target="tpu_custom_call" | custom-call | flops 314572800 | bytes 8388608 | tf_op jit(solution)/shard_map/prepare/pallas_call | solution.py:439
  60.2 3.6 %collective-permute-done.2.after_ref = f32[136,640]{1,0:T(8,128)S(1)} collective-permute-done((f32[136,640]{1,0:T(8,128)S(1)}, f32[136,640]{1,0:T(8,128)S(1)}, u32[]{:S(2)}, u32[]{:S(2)}) %collective-permute-start.2) | collective-permute-done | bytes 348192 | tf_op jit(solution)/shard_map/ppermute | solution.py:495
  63.8 3.1 %collective-permute-done.1.before_ref = f32[136,640]{1,0:T(8,128)S(1)} collective-permute-done((f32[136,640]{1,0:T(8,128)S(1)}, f32[136,640]{1,0:T(8,128)S(1)}, u32[]{:S(2)}, u32[]{:S(2)}) %collective-permute-start.1) | collective-permute-done | bytes 348192 | tf_op jit(solution)/shard_map/ppermute | solution.py:494
  66.9 11.7 %server.1 = f32[128,5,4,128]{3,2,1,0:T(4,128)S(1)} custom-call(f32[512,640]{1,0:T(8,128)S(1)} %get-tuple-element.16.x_ref, f32[136,640]{1,0:T(8,128)S(1)} %get-tuple-element.17.own_ref, bf16[512,1920]{1,0:T(8,128)(2,1)S(1)} %get-tuple-element.18.x3_ref, bf16[128,1920]{1,0:T(8,128)(2,1)S(1)} %get-tuple-element.19.own3_ref, ...), custom_call_target="tpu_custom_call" | custom-call | tf_op jit(solution)/shard_map/server/pallas_call | solution.py:439
  78.6 26.4 %all_to_all.10.recv_ref = f32[128,5,4,128]{3,2,1,0:T(4,128)S(1)} all-to-all(f32[128,5,4,128]{3,2,1,0:T(4,128)S(1)} %server.1), channel_id=1, replica_groups=mesh['member'=8,'lat'=16] {'member','lat'}, dimensions={0} | all-to-all | bytes 2621440 | tf_op jit(solution)/shard_map/all_to_all | solution.py:533
  105.0 2.2 %unpack.1 = f32[80,4,1024]{2,1,0:T(4,128)} custom-call(f32[128,5,4,128]{3,2,1,0:T(4,128)S(1)} %all_to_all.10.recv_ref), custom_call_target="tpu_custom_call" | custom-call | tf_op jit(solution)/shard_map/unpack/pallas_call | solution.py:439
Async XLA Ops:
  5.0 11.2 %copy-start = (f32[8,128]{1,0:T(8,128)S(1)}, f32[8,128]{1,0:T(8,128)}, u32[]{:S(2)}) copy-start(f32[8,128]{1,0:T(8,128)} %get-tuple-element.15) | copy-start | bytes 12292
  5.0 46.4 %all-to-all-start = ((f32[128,40,128]{2,1,0:T(8,128)}), f32[128,40,128]{2,1,0:T(8,128)S(1)}, u32[]{:S(2)}, u32[]{:S(2)}) async-start(f32[128,40,128]{2,1,0:T(8,128)} %get-tuple-element.14), calls=%async_computation | async-start | bytes 5242880 | tf_op jit(solution)/shard_map/all_to_all | solution.py:482
  16.2 0.7 collective-permute-start
  58.5 5.2 %collective-permute-start.2 = (f32[136,640]{1,0:T(8,128)S(1)}, f32[136,640]{1,0:T(8,128)S(1)}, u32[]{:S(2)}, u32[]{:S(2)}) collective-permute-start(f32[136,640]{1,0:T(8,128)S(1)} %get-tuple-element.17.own_ref), channel_id=1, source_target_pairs={{16,0},{1,16},{17,1},{2,17},{18,2},{3,18},{19,3},{35,19},{51,35},{... | collective-permute-start | bytes 1044488 | tf_op jit(solution)/shard_map/ppermute | solution.py:495
  58.9 7.9 %collective-permute-start.1 = (f32[136,640]{1,0:T(8,128)S(1)}, f32[136,640]{1,0:T(8,128)S(1)}, u32[]{:S(2)}, u32[]{:S(2)}) collective-permute-start(f32[136,640]{1,0:T(8,128)S(1)} %get-tuple-element.17.own_ref), channel_id=1, source_target_pairs={{0,16},{16,1},{1,17},{17,2},{2,18},{18,3},{3,19},{19,35},{35,51},{... | collective-permute-start | bytes 1044488 | tf_op jit(solution)/shard_map/ppermute | solution.py:494

commit v5 on v4

--- a/solution.py
+++ b/solution.py
@@ -6,9 +6,11 @@
 from jax import lax
 from jax.experimental import pallas as pl
 from jax.experimental.pallas import tpu as pltpu
+from jax.sharding import Mesh
 from jax.sharding import PartitionSpec as P
 
-BOTH = ("member", "lat")
+ALL = ("y", "core", "lat")
+CHIPS = ("y", "lat")
 K = 640
 MEM = 80
 NOBS = 384
@@ -32,6 +34,7 @@
 
 
 PLACE = strip_places()
+CHIP = [PLACE[2 * j] // 32 * 16 + PLACE[2 * j] % 16 for j in range(64)]
 
 
 def lane_iota(rows=8):
@@ -66,8 +69,8 @@
 
 
 def pack_kernel(
-    ens_hbm, cell_hbm, value_hbm, var_hbm, rows_hbm, out_hbm, meta_ref,
-    ens, ab, stage, cell, value, var, rows_v, ens_sem, meta_sem, out_sem
+    ens_hbm, cell_hbm, value_hbm, var_hbm, rows_hbm, out_hbm,
+    ens, moved, stage, cell, value, var, rows_v, ens_sem, meta_sem, out_sem
 ):
     loads = [
         pltpu.make_async_copy(ens_hbm.at[8 * i : 8 * i + 8], ens.at[8 * i : 8 * i + 8], ens_sem.at[i])
@@ -85,83 +88,185 @@
         loads[i].wait()
         rows = slice(8 * i, 8 * i + 8)
         for r in range(4):
-            src = ens[rows, r, :]
-            ab[r, rows, :] = roll(src, 4)
-            ab[4 + r, rows, :] = roll(src, -4)
+            moved[r, rows, :] = roll(ens[rows, r, :], 4)
+    for copy in smalls:
+        copy.wait()
+    meta = jnp.concatenate(
+        [
+            cell[...].astype(F32),
+            value[...],
+            var[...],
+            jnp.broadcast_to(rows_v[0:1, 0:1].astype(F32), (1, 128)),
+        ],
+        axis=0,
+    )
+    for chip in range(64):
+        stage[chip, 15, :, :] = meta
     stores = []
+
+    def send(column):
+        base = min(CHIP[4 * column : 4 * column + 4])
+        part = slice(base, base + 4)
+        stores.append(
+            pltpu.make_async_copy(stage.at[part], out_hbm.at[part], out_sem.at[column])
+        )
+        stores[-1].start()
+
+    low = lane_iota() < 64
+
+    def put(j, t, pair):
+        for h in range(2):
+            tile = 4 * t + 2 * h
+            stage[CHIP[j % 64], tile : tile + 2, :, :] = pair[h].reshape(2, 4, 128)
+
     for g in range(8):
         cols = slice(g * 128, (g + 1) * 128)
-        for b in range(5):
-            if b < 4:
-                block = jnp.concatenate([ab[2 * b, 0:64, cols], ab[2 * b + 1, 0:64, cols]], axis=0)
+        main = [
+            jnp.concatenate([moved[2 * h, 0:64, cols], moved[2 * h + 1, 0:64, cols]], axis=0).T
+            for h in range(2)
+        ]
+        tails = jnp.concatenate([moved[r, 64:80, cols] for r in range(4)] * 2, axis=0).T
+        for w in range(16):
+            rows = slice(8 * w, 8 * w + 8)
+            pair = [main[0][rows], main[1][rows]]
+            tail = tails[rows]
+            j = 8 * g + w // 2
+            if w % 2 == 0:
+                put(j - 1, 2, pair)
+                put(j, 0, pair)
+                both = jnp.where(low, tail, pltpu.roll(tail, 4, 0))
+                stage[CHIP[(j - 1) % 64], 14, :, :] = both[0:4]
             else:
-                block = jnp.concatenate([ab[j, 64:80, cols] for j in range(8)], axis=0)
-            block = block.T
-            for w in range(16):
-                stage[PLACE[16 * g + w], 8 * b : 8 * b + 8, :] = block[8 * w : 8 * w + 8, :]
-        for base in sorted({PLACE[16 * g + w] // 4 * 4 for w in range(16)}):
-            part = slice(base, base + 4)
-            stores.append(
-                pltpu.make_async_copy(stage.at[part], out_hbm.at[part], out_sem.at[base // 4])
-            )
-            stores[-1].start()
-    for copy in smalls:
-        copy.wait()
-    meta_ref[...] = jnp.zeros_like(meta_ref)
-    meta_ref[0:1, :] = cell[...].astype(F32)
-    meta_ref[1:2, :] = value[...]
-    meta_ref[2:3, :] = var[...]
-    meta_ref[3:4, :] = jnp.broadcast_to(rows_v[0:1, 0:1].astype(F32), (1, 128))
+                put(j, 1, pair)
+                both = jnp.where(low, tails[8 * w - 8 : 8 * w], tail)
+                stage[CHIP[j], 12:14, :, :] = both.reshape(2, 4, 128)
+            if w % 8 == 0 and j > 0:
+                send(j // 4 - 1)
+    send(15)
     for copy in stores:
         copy.wait()
 
 
-def forecast_kernel(recv_ref, meta_ref, x_ref, obs_ref, fa, fb):
+def chip_pair():
+    y, lat = lax.axis_index("y"), lax.axis_index("lat")
+    x, z = lat // 4, lat % 4
+    column = x * 4 + jnp.where(x % 2 == 0, y, 3 - y)
+    return 4 * column + (z + column) % 4
+
+
+def place_kernel(recv_ref, own_ref, send_ref):
+    def run(core):
+        def put(row, t, cols, value):
+            if t in (core, core + 1):
+                at = 8 * (t - core)
+                own_ref[row, at : at + 8, cols] = value
+            other = 1 - core
+            if t in (other, other + 1):
+                at = 8 * (t - other)
+                send_ref[row, at : at + 8, cols] = value
+
+        def place(l, carry):
+            def vreg(y, tile):
+                return recv_ref[y * 16 + l, tile : tile + 2, :, :].reshape(8, 128)
+
+            for t in range(3):
+                for h in range(2):
+                    for k in range(2):
+                        tile = 4 * t + 2 * h
+                        outs = pair_swap(vreg(2 * k, tile), vreg(2 * k + 1, tile))
+                        for j, out in enumerate(outs):
+                            put(4 * l + 2 * h + j, t, slice(128 * k, 128 * k + 128), out)
+            last = slice(256, 384)
+            outs = block_transpose([vreg(y, 12) for y in range(4)], 16)
+            for r, out in enumerate(outs):
+                turned = roll(out, 64)
+                put(4 * l + r, 0, last, turned if core else out)
+                put(4 * l + r, 1, last, out if core else turned)
+            ends = []
+            for y in range(4):
+                part = recv_ref[y * 16 + l, 14, :, :]
+                ends.append(jnp.concatenate([part, roll(part, 64)], axis=0))
+            for r, out in enumerate(block_transpose(ends, 16)):
+                put(4 * l + r, 2, last, roll(out, 64) if core else out)
+            return carry
+
+        lax.fori_loop(0, 16, place, 0, unroll=4)
+        for ref, strip in (
+            (own_ref, 2 * chip_pair() + core),
+            (send_ref, 2 * chip_pair() + 1 - core),
+        ):
+            ref[64, 0:4, 0:128] = recv_ref[strip // 32 * 16 + strip % 16, 15, :, :]
+
+    core = lax.axis_index("core")
+    for value in range(2):
+        pl.when(core == value)(functools.partial(run, value))
+
+
+def advance(src, row, cols):
+    c = src[row, :, cols]
+    n = src[row - 1, :, cols]
+    s = src[row + 1, :, cols]
+    e = pltpu.roll(c, 15, 0)
+    w = pltpu.roll(c, 1, 0)
+    t = 0.1 * c
+    return t + 0.4 * (n + s) + (0.05 - t) * e + (0.05 + t) * w
+
+
+def march(first, fa, fb, finish):
+    every = slice(None)
     for buf in (fa, fb):
-        buf[0] = jnp.zeros((16, K), F32)
-        buf[65] = jnp.zeros((16, K), F32)
-
-    def place(l, carry):
-        for b in range(4):
-            for k in range(4):
-                outs = pair_swap(
-                    recv_ref[2 * k * 16 + l, 8 * b : 8 * b + 8, :],
-                    recv_ref[(2 * k + 1) * 16 + l, 8 * b : 8 * b + 8, :],
-                )
-                for j, out in enumerate(outs):
-                    t, r = divmod(2 * b + j, 4)
-                    fa[1 + 4 * l + r, 8 * t : 8 * t + 8, k * 128 : (k + 1) * 128] = out
-        ends = block_transpose([recv_ref[m * 16 + l, 32:40, :] for m in range(8)], 16)
-        for j, out in enumerate(ends):
-            t, r = divmod(j, 4)
-            fa[1 + 4 * l + r, 8 * t : 8 * t + 8, 512:640] = out
+        buf[0] = jnp.zeros(buf.shape[1:], F32)
+        buf[65] = jnp.zeros(buf.shape[1:], F32)
+
+    def load(i, carry):
+        fa[i + 1] = first(i)
         return carry
 
-    lax.fori_loop(0, 16, place, 0, unroll=4)
-
-    def advance(src, row):
-        c = src[row]
-        n = src[row - 1]
-        s = src[row + 1]
-        e = pltpu.roll(c, 15, 0)
-        w = pltpu.roll(c, 1, 0)
-        t = 0.1 * c
-        return t + 0.4 * (n + s) + (0.05 - t) * e + (0.05 + t) * w
-
+    lax.fori_loop(0, 64, load, 0, unroll=8)
     for src, dst in ((fa, fb), (fb, fa), (fa, fb)):
 
         def move(i, carry):
-            dst[i + 1] = advance(src, i + 1)
+            dst[i + 1] = advance(src, i + 1, every)
             return carry
 
         lax.fori_loop(0, 64, move, 0, unroll=8)
 
     def last(i, carry):
-        x_ref[pl.ds(pl.multiple_of(i * 8, 8), 8), :] = advance(fb, i + 1)[4:12, :]
+        finish(i, advance(fb, i + 1, every)[4:12, :])
         return carry
 
     lax.fori_loop(0, 64, last, 0, unroll=8)
-    cell = jnp.concatenate([meta_ref[0:1, :], jnp.zeros((7, 128), F32)], axis=0).T[:, 0:1]
+
+
+def forecast_own_kernel(own_ref, x_ref, fa, fb):
+    def finish(i, value):
+        x_ref[pl.ds(pl.multiple_of(i * 8, 8), 8), :] = value
+
+    march(lambda i: own_ref[i, :, 0:256], fa, fb, finish)
+
+
+def forecast_kernel(own_ref, other_ref, part_ref, x_ref, obs_ref, fa, fb):
+    core = lax.axis_index("core")
+    low_core = core == 0
+    low = lax.broadcasted_iota(jnp.int32, (16, 128), 1) < 64
+    own_low = jnp.where(low_core, 1, 0)
+    pick_own = low == (jnp.broadcast_to(own_low, (16, 128)) > 0)
+
+    def first(i):
+        ends = jnp.where(pick_own, own_ref[i, :, 256:384], other_ref[i, :, 256:384])
+        return jnp.concatenate([other_ref[i, :, 0:256], ends], axis=1)
+
+    def finish(i, value):
+        rows = pl.ds(pl.multiple_of(i * 8, 8), 8)
+        x_ref[rows, pl.ds(pl.multiple_of((1 - core) * 256, 128), 256)] = value[:, 0:256]
+        x_ref[rows, pl.ds(pl.multiple_of(core * 256, 128), 256)] = part_ref[rows, :]
+        x_ref[rows, 512:640] = value[:, 256:384]
+
+    march(first, fa, fb, finish)
+    here = jnp.broadcast_to(jnp.where((chip_pair() // 8) % 2 == core, 1, 0), (4, 128)) > 0
+    meta = jnp.where(here, own_ref[64, 0:4, 0:128], other_ref[64, 0:4, 0:128])
+    meta = jnp.concatenate([meta, jnp.zeros((4, 128), F32)], axis=0)
+    cell = meta.T[:, 0:1]
     pick = jnp.where(
         lax.broadcasted_iota(jnp.int32, (128, CELLS), 1) == cell.astype(jnp.int32), 1.0, 0.0
     ).astype(BF16)
@@ -174,7 +279,7 @@
         x3 = (rest - x2.astype(F32)).astype(BF16)
         obs_ref[0:128, cols] = mm(pick, x1) + mm(pick, x2) + mm(pick, x3)
     obs_ref[128:136, :] = jnp.zeros((8, K), F32)
-    obs_ref[128:136, 0:128] = meta_ref[...]
+    obs_ref[128:136, 0:128] = meta
 
 
 def split(value):
@@ -399,15 +504,15 @@
                 for k in range(4):
                     outs = pair_swap(block(2 * half, k), block(2 * half + 1, k))
                     for j, out in enumerate(outs):
-                        dest = (2 * k + j) * 16 + l
+                        dest = (2 * (2 * (k % 2) + j) + k // 2) * 16 + l
                         out_ref[dest, 2 * half : 2 * half + 2, :, :] = out.reshape(2, 4, 128)
             ends = [block(r, 4) for r in range(4)]
             for j, out in enumerate(block_transpose(ends, 16)):
                 turned = roll(out, 64)
                 first_half = jnp.where(low, out, pltpu.roll(turned, 4, 0))
                 second_half = jnp.where(low, turned, pltpu.roll(out, 4, 0))
-                out_ref[j * 16 + l, 4, :, :] = first_half[0:4]
-                out_ref[(4 + j) * 16 + l, 4, :, :] = second_half[0:4]
+                out_ref[2 * j * 16 + l, 4, :, :] = first_half[0:4]
+                out_ref[(2 * j + 1) * 16 + l, 4, :, :] = second_half[0:4]
 
 
 def unpack_kernel(recv_ref, out_ref):
@@ -453,9 +558,9 @@
 
 
 def per_device(ensemble, obs_cell, obs_value, obs_var, patch_rows):
-    chunks, meta = call(
+    chunks = call(
         pack_kernel,
-        (shaped(128, 40, 128), shaped(8, 128)),
+        shaped(64, 16, 4, 128),
         ensemble,
         obs_cell,
         obs_value,
@@ -463,36 +568,49 @@
         patch_rows,
         scratch=[
             pltpu.VMEM((MEM, 4, 1024), F32),
-            pltpu.VMEM((8, MEM, 1024), F32),
-            pltpu.VMEM((128, 40, 128), F32),
+            pltpu.VMEM((4, MEM, 1024), F32),
+            pltpu.VMEM((64, 16, 4, 128), F32),
             pltpu.VMEM((1, 128), jnp.int32),
             pltpu.VMEM((1, 128), F32),
             pltpu.VMEM((1, 128), F32),
             pltpu.VMEM((1, 2), jnp.int32),
             pltpu.SemaphoreType.DMA((10,)),
             pltpu.SemaphoreType.DMA((4,)),
-            pltpu.SemaphoreType.DMA((32,)),
+            pltpu.SemaphoreType.DMA((16,)),
         ],
         ins=[THERE] * 5,
-        outs=(THERE, WHOLE),
+        outs=THERE,
         name="pack",
         vmem=58,
     )
-    meta = lax.ppermute(meta, BOTH, [(s, PLACE[s]) for s in range(128)])
-    recv = lax.all_to_all(chunks, BOTH, split_axis=0, concat_axis=0, tiled=True)
+    recv = lax.all_to_all(chunks, CHIPS, split_axis=0, concat_axis=0, tiled=True)
+    own, other = call(
+        place_kernel, (shaped(65, 16, 384), shaped(65, 16, 384)), recv, name="place", vmem=4
+    )
+    other = lax.ppermute(other, "core", [(0, 1), (1, 0)])
+    part = call(
+        forecast_own_kernel,
+        shaped(CELLS, 256),
+        own,
+        scratch=[pltpu.VMEM((66, 16, 256), F32)] * 2,
+        name="forecast_own",
+        vmem=6,
+        cost=pl.CostEstimate(flops=8 << 20, bytes_accessed=8 << 20, transcendentals=0),
+    )
     x, obs = call(
         forecast_kernel,
         (shaped(CELLS, K), shaped(136, K)),
-        recv,
-        meta,
-        scratch=[pltpu.VMEM((66, 16, K), F32)] * 2,
+        own,
+        other,
+        part,
+        scratch=[pltpu.VMEM((66, 16, 384), F32)] * 2,
         name="forecast",
-        vmem=12,
+        vmem=10,
     )
     up = [(PLACE[s], PLACE[(s + 1) % 128]) for s in range(128)]
     down = [(b, a) for a, b in up]
-    before = lax.ppermute(obs, BOTH, up)
-    after = lax.ppermute(obs, BOTH, down)
+    before = lax.ppermute(obs, ALL, up)
+    after = lax.ppermute(obs, ALL, down)
     own = call(
         prepare_kernel,
         (
@@ -530,22 +648,17 @@
         name="server",
         vmem=32,
     )
-    back = lax.all_to_all(back, BOTH, split_axis=0, concat_axis=0, tiled=True)
+    back = lax.all_to_all(back, ALL, split_axis=0, concat_axis=0, tiled=True)
     return call(unpack_kernel, shaped(MEM, 4, 1024), back, name="unpack", vmem=6)
 
 
 def solution(mesh):
-    in_specs = (
-        P("member", "lat", None),
-        P(BOTH, None),
-        P(BOTH, None),
-        P(BOTH, None),
-        P(BOTH, None),
-    )
+    split_mesh = Mesh(mesh.devices.reshape(4, 2, 16), ALL)
+    in_specs = (P(("y", "core"), "lat", None),) + (P(ALL, None),) * 4
     return jax.shard_map(
         per_device,
-        mesh=mesh,
+        mesh=split_mesh,
         in_specs=in_specs,
-        out_specs=P("member", "lat", None),
+        out_specs=P(("y", "core"), "lat", None),
         check_vma=False,
     )

time: 107 us -> 103 us (0.963)
  blocking collectives: 26.4 us -> 67.4 us
  waiting for transfers between devices: 41.2 us -> 7.76 us
  starting transfers between devices: 12.4 us -> 0.66 us
    all_to_all x1 -> x2, blocking collectives: 26.4 us -> 67.4 us  [the longest x1 41.1 us: per_device(): lax.all_to_all(chunks, CHIPS, split_axis=0, concat_axis=0, tiled=True)]
    all_to_all x1 -> x0, waiting for transfers between devices: 34.5 us -> none  [per_device(): recv = lax.all_to_all(chunks, BOTH, split_axis=0, concat_axis=0, tiled=True)]
    all_to_all x1 -> x0, starting transfers between devices: 11.1 us -> none  [per_device(): recv = lax.all_to_all(chunks, BOTH, split_axis=0, concat_axis=0, tiled=True)]
    ppermute x3, waiting for transfers between devices: 6.67 us -> 7.76 us  [the longest x1 3.37 us: per_device(): before = lax.ppermute(obs, ALL, up)]
    pallas_call x5 -> x7, Pallas kernels: 27.2 us -> 26.3 us  [call(): pl.pallas_call(kernel, out_shape=out_shape, in_specs=ins or [WHOLE] * len...]
  transfers between devices with their start and end apart: 4 -> 3, of which waited for: 3 -> 3; matrix products, arithmetic and copies ran while one was open for 0% -> 0% of each run, Pallas kernels for 1% -> 3%
where the time goes in v5:
time: 103 us; the launch traced here: 102 us
  blocking collectives  67.4 us (65%)
  Pallas kernels  26.3 us (26%)
  waiting for transfers between devices  7.76 us (8%)
    all_to_all x1, blocking collectives, per_device(): lax.all_to_all(chunks, CHIPS, split_axis=0, concat_axis=0, tiled=True)  41.1 us
    pallas_call x7, Pallas kernels, call(): pl.pallas_call(kernel, out_shape=out_shape, in_specs=ins or [WHOLE] * len...  26.3 us
    all_to_all x1, blocking collectives, per_device(): back = lax.all_to_all(back, ALL, split_axis=0, concat_axis=0, tiled=True)  26.3 us
    ppermute x1, waiting for transfers between devices, per_device(): before = lax.ppermute(obs, ALL, up)  3.37 us
    ppermute x1, waiting for transfers between devices, per_device(): after = lax.ppermute(obs, ALL, down)  3.22 us
  transfers between devices with their start and end apart: 3, of which 3 were waited for; matrix products, arithmetic and copies ran while one was open for 0% of the time, Pallas kernels for 3%

profile of v5, /device:TPU:0, one launch (start us, length us, event | category | flops | bytes accessed | tf_op | source)
XLA Modules:
  0.0 102.3 jit_solution(14514739655138602514)
XLA Ops:
  0.0 3.7 %pack.1 = f32[64,16,4,128]{3,2,1,0:T(4,128)} custom-call(f32[80,4,1024]{2,1,0:T(4,128)} %ens_hbm.1, s32[1,128]{1,0:T(1,128)} %cell_hbm.1, f32[1,128]{1,0:T(1,128)} %value_hbm.1, f32[1,128]{1,0:T(1,128)} %var_hbm.1, s32[1,2]{1,0:T(1,128)} %rows_hbm.1), custom_call_target="tpu_custom_call" | custom-call | tf_op jit(solution)/shard_map/pack/pallas_call | solution.py:544
  3.7 41.1 %all_to_all.10.recv_ref = f32[64,16,4,128]{3,2,1,0:T(4,128)S(1)} all-to-all(f32[64,16,4,128]{3,2,1,0:T(4,128)} %pack.1), channel_id=1, replica_groups=mesh['y'=4,'core'=2,'lat'=16] {'y','lat'}, dimensions={0} | all-to-all | bytes 4194304 | tf_op jit(solution)/shard_map/all_to_all | solution.py:586
  44.9 1.1 %place.1 = (f32[65,16,384]{2,1,0:T(8,128)S(1)}, f32[65,16,384]{2,1,0:T(8,128)S(1)}) custom-call(f32[64,16,4,128]{3,2,1,0:T(4,128)S(1)} %all_to_all.10.recv_ref), custom_call_target="tpu_custom_call" | custom-call | tf_op jit(solution)/shard_map/place/pallas_call | solution.py:544
  46.0 0.1 collective-permute-start
  46.1 2.3 %forecast_own.1.part_ref = f32[512,256]{1,0:T(8,128)S(1)} custom-call(f32[65,16,384]{2,1,0:T(8,128)S(1)} %get-tuple-element.14.own_ref), custom_call_target="tpu_custom_call" | custom-call | flops 8388608 | bytes 8388608 | tf_op jit(solution)/shard_map/forecast_own/pallas_call | solution.py:544
  48.4 1.2 %collective-permute-done.other_ref = f32[65,16,384]{2,1,0:T(8,128)S(1)} collective-permute-done((f32[65,16,384]{2,1,0:T(8,128)S(1)}, f32[65,16,384]{2,1,0:T(8,128)S(1)}, u32[]{:S(2)}, u32[]{:S(2)}) %collective-permute-start) | collective-permute-done | bytes 1597472 | tf_op jit(solution)/shard_map/ppermute | solution.py:590
  49.5 4.2 %forecast.1 = (f32[512,640]{1,0:T(8,128)S(1)}, f32[136,640]{1,0:T(8,128)S(1)}) custom-call(f32[65,16,384]{2,1,0:T(8,128)S(1)} %get-tuple-element.14.own_ref, f32[65,16,384]{2,1,0:T(8,128)S(1)} %collective-permute-done.other_ref, f32[512,256]{1,0:T(8,128)S(1)} %forecast_own.1.part_ref), custom_call_target="tpu_custom_call" | custom-call | tf_op jit(solution)/shard_map/forecast/pallas_call | solution.py:544
  53.7 0.1 collective-permute-start.2
  53.8 0.5 collective-permute-start.1
  54.3 1.1 %prepare.1 = (bf16[512,1920]{1,0:T(8,128)(2,1)S(1)}, bf16[128,1920]{1,0:T(8,128)(2,1)S(1)}, bf16[640,128]{1,0:T(8,128)(2,1)S(1)}, f32[640,128]{1,0:T(8,128)S(1)}, f32[512,1]{1,0:T(8,128)S(1)}) custom-call(f32[512,640]{1,0:T(8,128)S(1)} %get-tuple-element.16.x_ref, f32[136,640]{1,0:T(8,128)S(1)} %get-tuple-element.17.own_ref), custom_call_target="tpu_custom_call" | custom-call | flops 314572800 | bytes 8388608 | tf_op jit(solution)/shard_map/prepare/pallas_call | solution.py:544
  55.4 3.2 %collective-permute-done.2.after_ref = f32[136,640]{1,0:T(8,128)S(1)} collective-permute-done((f32[136,640]{1,0:T(8,128)S(1)}, f32[136,640]{1,0:T(8,128)S(1)}, u32[]{:S(2)}, u32[]{:S(2)}) %collective-permute-start.2) | collective-permute-done | bytes 348192 | tf_op jit(solution)/shard_map/ppermute | solution.py:613
  58.6 3.4 %collective-permute-done.1.before_ref = f32[136,640]{1,0:T(8,128)S(1)} collective-permute-done((f32[136,640]{1,0:T(8,128)S(1)}, f32[136,640]{1,0:T(8,128)S(1)}, u32[]{:S(2)}, u32[]{:S(2)}) %collective-permute-start.1) | collective-permute-done | bytes 348192 | tf_op jit(solution)/shard_map/ppermute | solution.py:612
  62.0 11.7 %server.1 = f32[128,5,4,128]{3,2,1,0:T(4,128)S(1)} custom-call(f32[512,640]{1,0:T(8,128)S(1)} %get-tuple-element.16.x_ref, f32[136,640]{1,0:T(8,128)S(1)} %get-tuple-element.17.own_ref, bf16[512,1920]{1,0:T(8,128)(2,1)S(1)} %get-tuple-element.18.x3_ref, bf16[128,1920]{1,0:T(8,128)(2,1)S(1)} %get-tuple-element.19.own3_ref, ...), custom_call_target="tpu_custom_call" | custom-call | tf_op jit(solution)/shard_map/server/pallas_call | solution.py:544
  73.7 26.3 %all_to_all.11.recv_ref = f32[128,5,4,128]{3,2,1,0:T(4,128)S(1)} all-to-all(f32[128,5,4,128]{3,2,1,0:T(4,128)S(1)} %server.1), channel_id=1, replica_groups=mesh['y'=4,'core'=2,'lat'=16] {'y','core','lat'}, dimensions={0} | all-to-all | bytes 2621440 | tf_op jit(solution)/shard_map/all_to_all | solution.py:651
  100.0 2.2 %unpack.1 = f32[80,4,1024]{2,1,0:T(4,128)} custom-call(f32[128,5,4,128]{3,2,1,0:T(4,128)S(1)} %all_to_all.11.recv_ref), custom_call_target="tpu_custom_call" | custom-call | tf_op jit(solution)/shard_map/unpack/pallas_call | solution.py:544
Async XLA Ops:
  46.0 3.5 %collective-permute-start = (f32[65,16,384]{2,1,0:T(8,128)S(1)}, f32[65,16,384]{2,1,0:T(8,128)S(1)}, u32[]{:S(2)}, u32[]{:S(2)}) collective-permute-start(f32[65,16,384]{2,1,0:T(8,128)S(1)} %get-tuple-element.15), channel_id=1, source_target_pairs={{0,16},{16,0},{1,17},{17,1},{2,18},{18,2},{3,19},{19,3},{4,20},{20... | collective-permute-start | bytes 4792328 | tf_op jit(solution)/shard_map/ppermute | solution.py:590
  53.7 4.9 %collective-permute-start.2 = (f32[136,640]{1,0:T(8,128)S(1)}, f32[136,640]{1,0:T(8,128)S(1)}, u32[]{:S(2)}, u32[]{:S(2)}) collective-permute-start(f32[136,640]{1,0:T(8,128)S(1)} %get-tuple-element.17.own_ref), channel_id=1, source_target_pairs={{16,0},{1,16},{17,1},{2,17},{18,2},{3,18},{19,3},{35,19},{51,35},{... | collective-permute-start | bytes 1044488 | tf_op jit(solution)/shard_map/ppermute | solution.py:613
  53.8 8.2 %collective-permute-start.1 = (f32[136,640]{1,0:T(8,128)S(1)}, f32[136,640]{1,0:T(8,128)S(1)}, u32[]{:S(2)}, u32[]{:S(2)}) collective-permute-start(f32[136,640]{1,0:T(8,128)S(1)} %get-tuple-element.17.own_ref), channel_id=1, source_target_pairs={{0,16},{16,1},{1,17},{17,2},{2,18},{18,3},{3,19},{19,35},{35,51},{... | collective-permute-start | bytes 1044488 | tf_op jit(solution)/shard_map/ppermute | solution.py:612

commit v6 on v5

--- a/solution.py
+++ b/solution.py
@@ -324,39 +324,55 @@
     tu_ref[128:, :] = mm_nt(x3_ref[...], right)
 
 
+def beside_kernel(obs_ref, x3_ref, own3_ref, near3_ref, y_ref, tu_ref):
+    obs = obs_ref[0:128, :]
+    spread = obs - jnp.sum(obs, axis=1, keepdims=True) * (1.0 / K)
+    high, low = split(spread)
+    near3_ref[:, 0:K] = high
+    near3_ref[:, K : 2 * K] = high
+    near3_ref[:, 2 * K :] = low
+    y_ref[...] = spread.T.astype(BF16)
+    right = jnp.concatenate([high, low, high], axis=1)
+    tu_ref[0:128, :] = mm_nt(own3_ref[...], right)
+    tu_ref[128:256, :] = mm_nt(near3_ref[...], right)
+    tu_ref[256:, :] = mm_nt(x3_ref[...], right)
+
+
 def mm_nt(left, right):
     return lax.dot_general(left, right, (((1,), (1,)), ((), ())), preferred_element_type=F32)
 
 
 def server_kernel(
-    x_ref, own_ref, x3_ref, own3_ref, y_ref, tu_ref, mean_ref, before_ref, after_ref, out_ref,
-    near3, yr, y2, yt3, g2, u_ref, c_ref, d_ref, res
+    x_ref, own_ref, x3_ref, own3_ref, y_ref, tu_ref, mean_ref,
+    near_ref, near3_ref, ny_ref, ntu_ref, far_ref, out_ref,
+    far3, y2, yt3, g2, u_ref, c_ref, d_ref, res
 ):
     innov, var, orow, ocol = [], [], [], []
-    yt3[0:128, :] = own3_ref[:, 0:K]
-    yt3[NOBS : NOBS + 128, :] = own3_ref[:, 2 * K :]
-    yt3[2 * NOBS : 2 * NOBS + 128, :] = own3_ref[:, 0:K]
-    y2[:, 0:128] = y_ref[...]
-    y2[:, NOBS : NOBS + 128] = y_ref[...]
-    for j, ref in enumerate((own_ref, before_ref, after_ref)):
+    side = jnp.where(lax.axis_index("core") == 0, 8.0, -8.0)
+    for j, (ref, three, turned) in enumerate(
+        ((own_ref, own3_ref, y_ref), (near_ref, near3_ref, ny_ref), (far_ref, None, None))
+    ):
         obs = ref[0:128, :]
         obs_mean = jnp.sum(obs, axis=1, keepdims=True) * (1.0 / K)
-        if j:
+        if three is None:
             spread = obs - obs_mean
             high, low = split(spread)
-            rows = slice((j - 1) * 128, j * 128)
-            for n, (left, right) in enumerate(((high, high), (high, low), (low, high))):
-                near3[rows, n * K : (n + 1) * K] = left
-                yr[rows, n * K : (n + 1) * K] = right
-                yt3[n * NOBS + j * 128 : n * NOBS + (j + 1) * 128, :] = right
+            far3[:, 0:K] = high
+            far3[:, K : 2 * K] = high
+            far3[:, 2 * K :] = low
+            far_right = jnp.concatenate([high, low, high], axis=1)
             turned = spread.T.astype(BF16)
-            y2[:, j * 128 : (j + 1) * 128] = turned
-            y2[:, NOBS + j * 128 : NOBS + (j + 1) * 128] = turned
+        else:
+            high, low, turned = three[:, 0:K], three[:, 2 * K :], turned[...]
+        for n, part in enumerate((high, low, high)):
+            yt3[n * NOBS + j * 128 : n * NOBS + (j + 1) * 128, :] = part
+        y2[:, j * 128 : (j + 1) * 128] = turned
+        y2[:, NOBS + j * 128 : NOBS + (j + 1) * 128] = turned
         cell = ref[128:129, 0:128].astype(jnp.int32)
         innov.append(ref[129:130, 0:128] - as_row(obs_mean))
         var.append(ref[130:131, 0:128])
         orow.append((cell // 8).astype(F32))
-        ocol.append((cell % 8).astype(F32) + (0.0, -8.0, 8.0)[j])
+        ocol.append((cell % 8).astype(F32) + (0.0, side, -side)[j])
     innov, var, orow, ocol = (jnp.concatenate(v, axis=1) for v in (innov, var, orow, ocol))
 
     first = own_ref[131:132, 0:1]
@@ -392,17 +408,19 @@
         g2[0:NOBS, p * K : (p + 1) * K] = high
         g2[NOBS:, p * K : (p + 1) * K] = low
 
-    tu = mm_nt(near3[...], yr[...])
-    cross = mm_nt(own3_ref[...], yr[...])
+    t_own, t_near, t_far = (mm_nt(far_right, ref[...]) for ref in (own3_ref, near3_ref, far3))
+    cross = ntu_ref[0:128, :]
     t_mat = jnp.concatenate(
         [
-            jnp.concatenate([tu_ref[0:128, :], cross], axis=1),
-            jnp.concatenate([cross.T, tu], axis=1),
+            jnp.concatenate([tu_ref[0:128, :], cross, t_own.T], axis=1),
+            jnp.concatenate([cross.T, ntu_ref[128:256, :], t_near.T], axis=1),
+            jnp.concatenate([t_own, t_near, t_far], axis=1),
         ],
         axis=0,
     )
     u_ref[:, 0:128] = tu_ref[128:, :]
-    u_ref[:, 128:] = mm_nt(x3_ref[...], yr[...])
+    u_ref[:, 128:256] = ntu_ref[256:, :]
+    u_ref[:, 256:384] = mm_nt(far_right, x3_ref[...]).T
 
     sums = []
     for n in range(5):
@@ -425,20 +443,19 @@
         z20.append(a1[p] * m20[p])
         z30.append(z20[p] * (1.5 - 0.5 * q0[p] * z20[p] * z20[p]))
     s = [(sg_col[p] * inv[p]) * t_mat * sg[p] for p in both]
-    s_left = [left3(s[p]) for p in both]
-    s2 = [mm(s_left[p], right3(s[p])) for p in both]
-    k2 = [
-        -0.5
-        * (
-            (a1[p] * a1[p] - q0[p] * a1[p]) * eye
-            + (0.25 * q0[p] - a1[p]) * s[p]
-            + 0.25 * s2[p]
-        )
-        for p in both
-    ]
-    m2 = [m20[p] * eye + mm(s_left[p], right3(k2[p])) for p in both]
-    kz2 = [a1[p] * k2[p] - 0.5 * m2[p] for p in both]
-    z2 = [z20[p] * eye + mm(s_left[p], right3(kz2[p])) for p in both]
+    s_right = [right3(s[p]) for p in both]
+    s2 = [mm(left3(s[p]), s_right[p]) for p in both]
+    s34 = [mm(left3(s2[p]), jnp.concatenate([s_right[p], right3(s2[p])], axis=1)) for p in both]
+    kz2, z2 = [], []
+    for p in both:
+        s3, s4 = s34[p][:, 0:NOBS], s34[p][:, NOBS:]
+        e0 = -0.5 * (a1[p] * a1[p] - q0[p] * a1[p])
+        e1 = -0.5 * (0.25 * q0[p] - a1[p])
+        c0 = a1[p] * e0 - 0.5 * m20[p]
+        c1 = a1[p] * e1 - 0.5 * e0
+        c2 = -0.125 * a1[p] - 0.5 * e1
+        kz2.append(c0 * eye + c1 * s[p] + c2 * s2[p] + 0.0625 * s3)
+        z2.append(z20[p] * eye + c0 * s[p] + c1 * s2[p] + c2 * s3 + 0.0625 * s4)
     z2_right = [right3(z2[p]) for p in both]
     size = (256, 384)
     start = [
@@ -452,19 +469,17 @@
         )
         for p in both
     ]
-    w1 = [mm(left3(v[p]), z2_right[p]) for p in both]
-    w2 = [mm(left3(w1[p]), z2_right[p]) for p in both]
-    tail = [
-        1.5 * v[p] - (0.5 * q0[p]) * (w2[p] + z20[p] * w1[p] + (z20[p] * z20[p]) * v[p])
-        for p in both
-    ]
-    hv = [
+    w1 = [
         mm(
-            jnp.concatenate([left3(-0.5 * w2[p]), left3(tail[p])], axis=1),
-            jnp.concatenate([z2_right[p], right3(kz2[p])], axis=0),
+            left3(v[p]),
+            jnp.concatenate([right3(z2[p] + q0[p] * kz2[p]), right3(kz2[p])], axis=1),
         )
         for p in both
     ]
+    kv = [w1[p][:, NOBS:] for p in both]
+    w2 = [mm(left3(w1[p][:, 0:NOBS]), z2_right[p]) for p in both]
+    w3 = [mm(left3(w2[p] + (q0[p] * z20[p]) * kv[p]), z2_right[p]) for p in both]
+    hv = [(1.5 - 0.5 * q0[p] * z20[p] * z20[p]) * kv[p] - 0.5 * w3[p] for p in both]
     scale = [jnp.sqrt(q0[p]) for p in both]
     for p in (1, 0):
         n = size[p]
@@ -607,10 +622,9 @@
         name="forecast",
         vmem=10,
     )
-    up = [(PLACE[s], PLACE[(s + 1) % 128]) for s in range(128)]
-    down = [(b, a) for a, b in up]
-    before = lax.ppermute(obs, ALL, up)
-    after = lax.ppermute(obs, ALL, down)
+    far_pairs = [(PLACE[s], PLACE[(s + 1) % 128]) for s in range(1, 128, 2)]
+    far = lax.ppermute(obs, ALL, far_pairs + [(b, a) for a, b in far_pairs])
+    near = lax.ppermute(obs, "core", [(0, 1), (1, 0)])
     own = call(
         prepare_kernel,
         (
@@ -626,17 +640,30 @@
         vmem=6,
         cost=pl.CostEstimate(flops=2 * K * K * 128 * 3, bytes_accessed=8 << 20, transcendentals=0),
     )
+    beside = call(
+        beside_kernel,
+        (
+            shaped(128, 3 * K, dtype=BF16),
+            shaped(K, 128, dtype=BF16),
+            shaped(256 + CELLS, 128),
+        ),
+        near,
+        *own[0:2],
+        name="beside",
+        vmem=6,
+        cost=pl.CostEstimate(flops=2 * K * K * 128 * 3, bytes_accessed=8 << 20, transcendentals=0),
+    )
     back = call(
         server_kernel,
         shaped(128, 5, 4, 128),
         x,
         obs,
         *own,
-        before,
-        after,
+        near,
+        *beside,
+        far,
         scratch=[
-            pltpu.VMEM((256, 3 * K), BF16),
-            pltpu.VMEM((256, 3 * K), BF16),
+            pltpu.VMEM((128, 3 * K), BF16),
             pltpu.VMEM((K, 2 * NOBS), BF16),
             pltpu.VMEM((3 * NOBS, K), BF16),
             pltpu.VMEM((2 * NOBS, 2 * K), BF16),

time: 103 us -> 102 us (level)
    pallas_call x7 -> x8, Pallas kernels: 26.3 us -> 26.6 us  [call(): pl.pallas_call(kernel, out_shape=out_shape, in_specs=ins or [WHOLE] * len...]
  transfers between devices with their start and end apart: 3 -> 3, of which waited for: 3 -> 3; matrix products, arithmetic and copies ran while one was open for 0% -> 0% of each run, Pallas kernels for 3% -> 4%
where the time goes in v6:
time: 102 us; the launch traced here: 101 us
  blocking collectives  67.2 us (66%)
  Pallas kernels  26.6 us (26%)
  waiting for transfers between devices  6.92 us (7%)
    all_to_all x1, blocking collectives, per_device(): lax.all_to_all(chunks, CHIPS, split_axis=0, concat_axis=0, tiled=True)  41.1 us
    pallas_call x8, Pallas kernels, call(): pl.pallas_call(kernel, out_shape=out_shape, in_specs=ins or [WHOLE] * len...  26.6 us
    all_to_all x1, blocking collectives, per_device(): back = lax.all_to_all(back, ALL, split_axis=0, concat_axis=0, tiled=True)  26.1 us
    ppermute x1, waiting for transfers between devices, per_device(): far = lax.ppermute(obs, ALL, far_pairs + [(b, a) for a, b in far_pairs])  5.47 us
  transfers between devices with their start and end apart: 3, of which 3 were waited for; matrix products, arithmetic and copies ran while one was open for 0% of the time, Pallas kernels for 4%

profile of v6, /device:TPU:0, one launch (start us, length us, event | category | flops | bytes accessed | tf_op | source)
XLA Modules:
  0.0 101.3 jit_solution(11703019735543670910)
XLA Ops:
  0.0 3.8 %pack.1 = f32[64,16,4,128]{3,2,1,0:T(4,128)} custom-call(f32[80,4,1024]{2,1,0:T(4,128)} %ens_hbm.1, s32[1,128]{1,0:T(1,128)} %cell_hbm.1, f32[1,128]{1,0:T(1,128)} %value_hbm.1, f32[1,128]{1,0:T(1,128)} %var_hbm.1, s32[1,2]{1,0:T(1,128)} %rows_hbm.1), custom_call_target="tpu_custom_call" | custom-call | tf_op jit(solution)/shard_map/pack/pallas_call | solution.py:559
  3.8 41.1 %all_to_all.10.recv_ref = f32[64,16,4,128]{3,2,1,0:T(4,128)S(1)} all-to-all(f32[64,16,4,128]{3,2,1,0:T(4,128)} %pack.1), channel_id=1, replica_groups=mesh['y'=4,'core'=2,'lat'=16] {'y','lat'}, dimensions={0} | all-to-all | bytes 4194304 | tf_op jit(solution)/shard_map/all_to_all | solution.py:601
  44.9 1.1 %place.1 = (f32[65,16,384]{2,1,0:T(8,128)S(1)}, f32[65,16,384]{2,1,0:T(8,128)S(1)}) custom-call(f32[64,16,4,128]{3,2,1,0:T(4,128)S(1)} %all_to_all.10.recv_ref), custom_call_target="tpu_custom_call" | custom-call | tf_op jit(solution)/shard_map/place/pallas_call | solution.py:559
  46.0 0.1 collective-permute-start
  46.1 2.3 %forecast_own.1.part_ref = f32[512,256]{1,0:T(8,128)S(1)} custom-call(f32[65,16,384]{2,1,0:T(8,128)S(1)} %get-tuple-element.17.own_ref), custom_call_target="tpu_custom_call" | custom-call | flops 8388608 | bytes 8388608 | tf_op jit(solution)/shard_map/forecast_own/pallas_call | solution.py:559
  48.4 1.2 %collective-permute-done.other_ref = f32[65,16,384]{2,1,0:T(8,128)S(1)} collective-permute-done((f32[65,16,384]{2,1,0:T(8,128)S(1)}, f32[65,16,384]{2,1,0:T(8,128)S(1)}, u32[]{:S(2)}, u32[]{:S(2)}) %collective-permute-start) | collective-permute-done | bytes 1597472 | tf_op jit(solution)/shard_map/ppermute | solution.py:605
  49.5 4.2 %forecast.1 = (f32[512,640]{1,0:T(8,128)S(1)}, f32[136,640]{1,0:T(8,128)S(1)}) custom-call(f32[65,16,384]{2,1,0:T(8,128)S(1)} %get-tuple-element.17.own_ref, f32[65,16,384]{2,1,0:T(8,128)S(1)} %collective-permute-done.other_ref, f32[512,256]{1,0:T(8,128)S(1)} %forecast_own.1.part_ref), custom_call_target="tpu_custom_call" | custom-call | tf_op jit(solution)/shard_map/forecast/pallas_call | solution.py:559
  53.7 0.2 collective-permute-start.1
  53.9 0.1 collective-permute-start.2
  54.1 1.1 %prepare.1 = (bf16[512,1920]{1,0:T(8,128)(2,1)S(1)}, bf16[128,1920]{1,0:T(8,128)(2,1)S(1)}, bf16[640,128]{1,0:T(8,128)(2,1)S(1)}, f32[640,128]{1,0:T(8,128)S(1)}, f32[512,1]{1,0:T(8,128)S(1)}) custom-call(f32[512,640]{1,0:T(8,128)S(1)} %get-tuple-element.19.x_ref, f32[136,640]{1,0:T(8,128)S(1)} %get-tuple-element.20.own_ref), custom_call_target="tpu_custom_call" | custom-call | flops 314572800 | bytes 8388608 | tf_op jit(solution)/shard_map/prepare/pallas_call | solution.py:559
  55.2 0.3 collective-permute-done.1.obs_ref.near_ref
  55.5 1.1 %beside.1 = (bf16[128,1920]{1,0:T(8,128)(2,1)S(1)}, bf16[640,128]{1,0:T(8,128)(2,1)S(1)}, f32[768,128]{1,0:T(8,128)S(1)}) custom-call(f32[136,640]{1,0:T(8,128)S(1)} %collective-permute-done.1.obs_ref.near_ref, bf16[512,1920]{1,0:T(8,128)(2,1)S(1)} %get-tuple-element.21.x3_ref, bf16[128,1920]{1,0:T(8,128)(2,1)S(1)} %get-tuple-element.22.own3_ref), custom_call_target="tpu_custom_call" | custom-call | flops 314572800 | bytes 8388608 | tf_op jit(solution)/shard_map/beside/pallas_call | solution.py:559
  56.5 5.5 %collective-permute-done.2.far_ref = f32[136,640]{1,0:T(8,128)S(1)} collective-permute-done((f32[136,640]{1,0:T(8,128)S(1)}, f32[136,640]{1,0:T(8,128)S(1)}, u32[]{:S(2)}, u32[]{:S(2)}) %collective-permute-start.2) | collective-permute-done | bytes 348192 | tf_op jit(solution)/shard_map/ppermute | solution.py:626
  62.0 10.9 %server.1 = f32[128,5,4,128]{3,2,1,0:T(4,128)S(1)} custom-call(f32[512,640]{1,0:T(8,128)S(1)} %get-tuple-element.19.x_ref, f32[136,640]{1,0:T(8,128)S(1)} %get-tuple-element.20.own_ref, bf16[512,1920]{1,0:T(8,128)(2,1)S(1)} %get-tuple-element.21.x3_ref, bf16[128,1920]{1,0:T(8,128)(2,1)S(1)} %get-tuple-element.22.own3_ref, ...), custom_call_target="tpu_custom_call" | custom-call | tf_op jit(solution)/shard_map/server/pallas_call | solution.py:559
  72.9 26.1 %all_to_all.11.recv_ref = f32[128,5,4,128]{3,2,1,0:T(4,128)S(1)} all-to-all(f32[128,5,4,128]{3,2,1,0:T(4,128)S(1)} %server.1), channel_id=1, replica_groups=mesh['y'=4,'core'=2,'lat'=16] {'y','core','lat'}, dimensions={0} | all-to-all | bytes 2621440 | tf_op jit(solution)/shard_map/all_to_all | solution.py:678
  99.0 2.2 %unpack.1 = f32[80,4,1024]{2,1,0:T(4,128)} custom-call(f32[128,5,4,128]{3,2,1,0:T(4,128)S(1)} %all_to_all.11.recv_ref), custom_call_target="tpu_custom_call" | custom-call | tf_op jit(solution)/shard_map/unpack/pallas_call | solution.py:559
Async XLA Ops:
  46.0 3.5 %collective-permute-start = (f32[65,16,384]{2,1,0:T(8,128)S(1)}, f32[65,16,384]{2,1,0:T(8,128)S(1)}, u32[]{:S(2)}, u32[]{:S(2)}) collective-permute-start(f32[65,16,384]{2,1,0:T(8,128)S(1)} %get-tuple-element.18), channel_id=1, source_target_pairs={{0,16},{16,0},{1,17},{17,1},{2,18},{18,2},{3,19},{19,3},{4,20},{20... | collective-permute-start | bytes 4792328 | tf_op jit(solution)/shard_map/ppermute | solution.py:605
  53.7 1.7 %collective-permute-start.1 = (f32[136,640]{1,0:T(8,128)S(1)}, f32[136,640]{1,0:T(8,128)S(1)}, u32[]{:S(2)}, u32[]{:S(2)}) collective-permute-start(f32[136,640]{1,0:T(8,128)S(1)} %get-tuple-element.20.own_ref), channel_id=1, source_target_pairs={{0,16},{16,0},{1,17},{17,1},{2,18},{18,2},{3,19},{19,3},{4,20},{20... | collective-permute-start | bytes 1044488 | tf_op jit(solution)/shard_map/ppermute | solution.py:627
  53.9 8.1 %collective-permute-start.2 = (f32[136,640]{1,0:T(8,128)S(1)}, f32[136,640]{1,0:T(8,128)S(1)}, u32[]{:S(2)}, u32[]{:S(2)}) collective-permute-start(f32[136,640]{1,0:T(8,128)S(1)} %get-tuple-element.20.own_ref), channel_id=1, source_target_pairs={{16,1},{17,2},{18,3},{19,35},{51,32},{48,33},{49,34},{50,66},{82,6... | collective-permute-start | bytes 1044488 | tf_op jit(solution)/shard_map/ppermute | solution.py:626

commit v7 on v6

--- a/solution.py
+++ b/solution.py
@@ -324,18 +324,62 @@
     tu_ref[128:, :] = mm_nt(x3_ref[...], right)
 
 
-def beside_kernel(obs_ref, x3_ref, own3_ref, near3_ref, y_ref, tu_ref):
+def patch_bounds(first):
+    swap = first > 32.0
+    zero, full = jnp.zeros_like(first), jnp.full_like(first, 64.0)
+    lower = [jnp.where(swap, first, zero), jnp.where(swap, zero, first)]
+    upper = [jnp.where(swap, full, first) - 1.0, jnp.where(swap, first, full) - 1.0]
+    return lower, upper
+
+
+def observed_places(ref, shift):
+    cell = ref[128:129, 0:128].astype(jnp.int32)
+    return (cell // 8).astype(F32), (cell % 8).astype(F32) + shift
+
+
+def localize(orow, ocol, var, lower, upper):
+    gap_row = jnp.maximum(jnp.maximum(lower - orow, orow - upper), 0.0) * (1.0 / 16.0)
+    gap_col = jnp.maximum(jnp.maximum(-ocol, ocol - 7.0), 0.0) * (1.0 / 8.0)
+    return jnp.exp(-gap_row * gap_row - gap_col * gap_col) / var
+
+
+def side_shift():
+    return jnp.where(lax.axis_index("core") == 0, 8.0, -8.0)
+
+
+def beside_kernel(
+    own_ref, obs_ref, x3_ref, own3_ref, turned_ref, near3_ref, tu_ref, gram_ref, y2, g2
+):
     obs = obs_ref[0:128, :]
     spread = obs - jnp.sum(obs, axis=1, keepdims=True) * (1.0 / K)
     high, low = split(spread)
     near3_ref[:, 0:K] = high
     near3_ref[:, K : 2 * K] = high
     near3_ref[:, 2 * K :] = low
-    y_ref[...] = spread.T.astype(BF16)
     right = jnp.concatenate([high, low, high], axis=1)
     tu_ref[0:128, :] = mm_nt(own3_ref[...], right)
     tu_ref[128:256, :] = mm_nt(near3_ref[...], right)
     tu_ref[256:, :] = mm_nt(x3_ref[...], right)
+    turned = spread.T.astype(BF16)
+    for n in range(2):
+        y2[:, 256 * n : 256 * n + 128] = turned_ref[...]
+        y2[:, 256 * n + 128 : 256 * n + 256] = turned
+    places = [observed_places(own_ref, 0.0), observed_places(obs_ref, side_shift())]
+    orow, ocol = (jnp.concatenate(v, axis=1) for v in zip(*places))
+    var = jnp.concatenate([own_ref[130:131, 0:128], obs_ref[130:131, 0:128]], axis=1)
+    lower, upper = patch_bounds(own_ref[131:132, 0:1])
+    g = [localize(orow, ocol, var, lower[p], upper[p]) for p in range(2)]
+    g_cols = jnp.concatenate(g + [jnp.zeros((6, 256), F32)], axis=0).T
+    yt = jnp.concatenate(
+        [own3_ref[:, 0:K].astype(F32) + own3_ref[:, 2 * K :].astype(F32), spread], axis=0
+    )
+    for p in range(2):
+        high, low = split(yt * g_cols[:, p : p + 1])
+        g2[0:256, p * K : (p + 1) * K] = high
+        g2[256:512, p * K : (p + 1) * K] = low
+    for n in range(5):
+        cols = slice(n * 256, (n + 1) * 256)
+        gram_ref[:, cols] = mm(y2[...], g2[:, cols])
 
 
 def mm_nt(left, right):
@@ -343,14 +387,14 @@
 
 
 def server_kernel(
-    x_ref, own_ref, x3_ref, own3_ref, y_ref, tu_ref, mean_ref,
-    near_ref, near3_ref, ny_ref, ntu_ref, far_ref, out_ref,
+    x_ref, own_ref, x3_ref, own3_ref, tu_ref, mean_ref,
+    near_ref, near3_ref, ntu_ref, gram_ref, far_ref, out_ref,
     far3, y2, yt3, g2, u_ref, c_ref, d_ref, res
 ):
     innov, var, orow, ocol = [], [], [], []
-    side = jnp.where(lax.axis_index("core") == 0, 8.0, -8.0)
-    for j, (ref, three, turned) in enumerate(
-        ((own_ref, own3_ref, y_ref), (near_ref, near3_ref, ny_ref), (far_ref, None, None))
+    side = side_shift()
+    for j, (ref, three) in enumerate(
+        ((own_ref, own3_ref), (near_ref, near3_ref), (far_ref, None))
     ):
         obs = ref[0:128, :]
         obs_mean = jnp.sum(obs, axis=1, keepdims=True) * (1.0 / K)
@@ -362,21 +406,20 @@
             far3[:, 2 * K :] = low
             far_right = jnp.concatenate([high, low, high], axis=1)
             turned = spread.T.astype(BF16)
+            y2[:, 0:128] = turned
+            y2[:, 128:256] = turned
         else:
-            high, low, turned = three[:, 0:K], three[:, 2 * K :], turned[...]
+            high, low = three[:, 0:K], three[:, 2 * K :]
         for n, part in enumerate((high, low, high)):
             yt3[n * NOBS + j * 128 : n * NOBS + (j + 1) * 128, :] = part
-        y2[:, j * 128 : (j + 1) * 128] = turned
-        y2[:, NOBS + j * 128 : NOBS + (j + 1) * 128] = turned
-        cell = ref[128:129, 0:128].astype(jnp.int32)
         innov.append(ref[129:130, 0:128] - as_row(obs_mean))
         var.append(ref[130:131, 0:128])
-        orow.append((cell // 8).astype(F32))
-        ocol.append((cell % 8).astype(F32) + (0.0, side, -side)[j])
+        place = observed_places(ref, (0.0, side, -side)[j])
+        orow.append(place[0])
+        ocol.append(place[1])
     innov, var, orow, ocol = (jnp.concatenate(v, axis=1) for v in (innov, var, orow, ocol))
 
     first = own_ref[131:132, 0:1]
-    swap = first > 32.0
     swap_scalar = jnp.max(first) > 32.0
     eye128 = lax.broadcasted_iota(jnp.int32, (128, 128), 0) == lax.broadcasted_iota(
         jnp.int32, (128, 128), 1
@@ -388,15 +431,11 @@
         0.0,
     )
     both = range(2)
-    zero, full = jnp.zeros_like(first), jnp.full_like(first, 64.0)
-    lower = [jnp.where(swap, first, zero), jnp.where(swap, zero, first)]
-    upper = [jnp.where(swap, full, first) - 1.0, jnp.where(swap, first, full) - 1.0]
+    lower, upper = patch_bounds(first)
     sg, sgd, sg_col, sgd_col, diag = [], [], [], [], []
     yt = yt3[0:NOBS, :].astype(F32) + yt3[NOBS : 2 * NOBS, :].astype(F32)
     for p in both:
-        gap_row = jnp.maximum(jnp.maximum(lower[p] - orow, orow - upper[p]), 0.0) * (1.0 / 16.0)
-        gap_col = jnp.maximum(jnp.maximum(-ocol, ocol - 7.0), 0.0) * (1.0 / 8.0)
-        g = jnp.exp(-gap_row * gap_row - gap_col * gap_col) / var
+        g = localize(orow, ocol, var, lower[p], upper[p])
         sg.append(jnp.sqrt(g))
         sgd.append(sg[p] * innov)
         cols = jnp.concatenate([sg[p], sgd[p], g, jnp.zeros((5, NOBS), F32)], axis=0).T
@@ -404,9 +443,9 @@
         sgd_col.append(cols[:, 1:2])
         scaled = yt * cols[:, 2:3]
         diag.append(jnp.sum(scaled * yt, axis=0, keepdims=True))
-        high, low = split(scaled)
-        g2[0:NOBS, p * K : (p + 1) * K] = high
-        g2[NOBS:, p * K : (p + 1) * K] = low
+        high, low = split(scaled[256:384])
+        g2[0:128, p * K : (p + 1) * K] = high
+        g2[128:256, p * K : (p + 1) * K] = low
 
     t_own, t_near, t_far = (mm_nt(far_right, ref[...]) for ref in (own3_ref, near3_ref, far3))
     cross = ntu_ref[0:128, :]
@@ -424,7 +463,8 @@
 
     sums = []
     for n in range(5):
-        block = jnp.abs(mm(y2[...], g2[:, n * 256 : (n + 1) * 256]))
+        cols = slice(n * 256, (n + 1) * 256)
+        block = jnp.abs(gram_ref[:, cols] + mm(y2[...], g2[:, cols]))
         for half in range(2):
             own = (2 * n + half) % 5
             part = block[:, half * 128 : (half + 1) * 128]
@@ -640,33 +680,41 @@
         vmem=6,
         cost=pl.CostEstimate(flops=2 * K * K * 128 * 3, bytes_accessed=8 << 20, transcendentals=0),
     )
+    x3, own3, turned, tu, mean = own
     beside = call(
         beside_kernel,
         (
             shaped(128, 3 * K, dtype=BF16),
-            shaped(K, 128, dtype=BF16),
             shaped(256 + CELLS, 128),
+            shaped(K, 2 * K),
         ),
+        obs,
         near,
-        *own[0:2],
+        x3,
+        own3,
+        turned,
+        scratch=[pltpu.VMEM((K, 512), BF16), pltpu.VMEM((512, 2 * K), BF16)],
         name="beside",
-        vmem=6,
-        cost=pl.CostEstimate(flops=2 * K * K * 128 * 3, bytes_accessed=8 << 20, transcendentals=0),
+        vmem=10,
+        cost=pl.CostEstimate(flops=2 * K * K * 512 * 3, bytes_accessed=8 << 20, transcendentals=0),
     )
     back = call(
         server_kernel,
         shaped(128, 5, 4, 128),
         x,
         obs,
-        *own,
+        x3,
+        own3,
+        tu,
+        mean,
         near,
         *beside,
         far,
         scratch=[
             pltpu.VMEM((128, 3 * K), BF16),
-            pltpu.VMEM((K, 2 * NOBS), BF16),
+            pltpu.VMEM((K, 256), BF16),
             pltpu.VMEM((3 * NOBS, K), BF16),
-            pltpu.VMEM((2 * NOBS, 2 * K), BF16),
+            pltpu.VMEM((256, 2 * K), BF16),
             pltpu.VMEM((CELLS, NOBS), F32),
             pltpu.VMEM((CELLS, NOBS), F32),
             pltpu.VMEM((CELLS, 1), F32),

time: 102 us -> 101 us (level)
  transfers between devices with their start and end apart: 3 -> 3, of which waited for: 3 -> 3; matrix products, arithmetic and copies ran while one was open for 0% -> 0% of each run, Pallas kernels for 4% -> 5%
where the time goes in v7:
time: 101 us; the launch traced here: 100 us
  blocking collectives  67.2 us (67%)
  Pallas kernels  26.7 us (26%)
  waiting for transfers between devices  5.96 us (6%)
    all_to_all x1, blocking collectives, per_device(): lax.all_to_all(chunks, CHIPS, split_axis=0, concat_axis=0, tiled=True)  41.1 us
    pallas_call x8, Pallas kernels, call(): pl.pallas_call(kernel, out_shape=out_shape, in_specs=ins or [WHOLE] * len...  26.7 us
    all_to_all x1, blocking collectives, per_device(): back = lax.all_to_all(back, ALL, split_axis=0, concat_axis=0, tiled=True)  26.1 us
    ppermute x1, waiting for transfers between devices, per_device(): far = lax.ppermute(obs, ALL, far_pairs + [(b, a) for a, b in far_pairs])  4.51 us
  transfers between devices with their start and end apart: 3, of which 3 were waited for; matrix products, arithmetic and copies ran while one was open for 0% of the time, Pallas kernels for 5%

profile of v7, /device:TPU:0, one launch (start us, length us, event | category | flops | bytes accessed | tf_op | source)
XLA Modules:
  0.0 100.4 jit_solution(6394516436713187530)
XLA Ops:
  0.0 3.8 %pack.1 = f32[64,16,4,128]{3,2,1,0:T(4,128)} custom-call(f32[80,4,1024]{2,1,0:T(4,128)} %ens_hbm.1, s32[1,128]{1,0:T(1,128)} %cell_hbm.1, f32[1,128]{1,0:T(1,128)} %value_hbm.1, f32[1,128]{1,0:T(1,128)} %var_hbm.1, s32[1,2]{1,0:T(1,128)} %rows_hbm.1), custom_call_target="tpu_custom_call" | custom-call | tf_op jit(solution)/shard_map/pack/pallas_call | solution.py:599
  3.8 41.1 %all_to_all.10.recv_ref = f32[64,16,4,128]{3,2,1,0:T(4,128)S(1)} all-to-all(f32[64,16,4,128]{3,2,1,0:T(4,128)} %pack.1), channel_id=1, replica_groups=mesh['y'=4,'core'=2,'lat'=16] {'y','lat'}, dimensions={0} | all-to-all | bytes 4194304 | tf_op jit(solution)/shard_map/all_to_all | solution.py:641
  44.9 1.1 %place.1 = (f32[65,16,384]{2,1,0:T(8,128)S(1)}, f32[65,16,384]{2,1,0:T(8,128)S(1)}) custom-call(f32[64,16,4,128]{3,2,1,0:T(4,128)S(1)} %all_to_all.10.recv_ref), custom_call_target="tpu_custom_call" | custom-call | tf_op jit(solution)/shard_map/place/pallas_call | solution.py:599
  46.0 0.1 collective-permute-start
  46.1 2.3 %forecast_own.1.part_ref = f32[512,256]{1,0:T(8,128)S(1)} custom-call(f32[65,16,384]{2,1,0:T(8,128)S(1)} %get-tuple-element.17.own_ref), custom_call_target="tpu_custom_call" | custom-call | flops 8388608 | bytes 8388608 | tf_op jit(solution)/shard_map/forecast_own/pallas_call | solution.py:599
  48.4 1.2 %collective-permute-done.other_ref = f32[65,16,384]{2,1,0:T(8,128)S(1)} collective-permute-done((f32[65,16,384]{2,1,0:T(8,128)S(1)}, f32[65,16,384]{2,1,0:T(8,128)S(1)}, u32[]{:S(2)}, u32[]{:S(2)}) %collective-permute-start) | collective-permute-done | bytes 1597472 | tf_op jit(solution)/shard_map/ppermute | solution.py:645
  49.5 4.2 %forecast.1 = (f32[512,640]{1,0:T(8,128)S(1)}, f32[136,640]{1,0:T(8,128)S(1)}) custom-call(f32[65,16,384]{2,1,0:T(8,128)S(1)} %get-tuple-element.17.own_ref, f32[65,16,384]{2,1,0:T(8,128)S(1)} %collective-permute-done.other_ref, f32[512,256]{1,0:T(8,128)S(1)} %forecast_own.1.part_ref), custom_call_target="tpu_custom_call" | custom-call | tf_op jit(solution)/shard_map/forecast/pallas_call | solution.py:599
  53.7 0.2 collective-permute-start.1
  53.9 0.1 collective-permute-start.2
  54.1 1.1 %prepare.1 = (bf16[512,1920]{1,0:T(8,128)(2,1)S(1)}, bf16[128,1920]{1,0:T(8,128)(2,1)S(1)}, bf16[640,128]{1,0:T(8,128)(2,1)S(1)}, f32[640,128]{1,0:T(8,128)S(1)}, f32[512,1]{1,0:T(8,128)S(1)}) custom-call(f32[512,640]{1,0:T(8,128)S(1)} %get-tuple-element.19.x_ref, f32[136,640]{1,0:T(8,128)S(1)} %get-tuple-element.20.own_ref), custom_call_target="tpu_custom_call" | custom-call | flops 314572800 | bytes 8388608 | tf_op jit(solution)/shard_map/prepare/pallas_call | solution.py:599
  55.2 0.3 collective-permute-done.1.obs_ref.near_ref
  55.5 2.0 %beside.1 = (bf16[128,1920]{1,0:T(8,128)(2,1)S(1)}, f32[768,128]{1,0:T(8,128)S(1)}, f32[640,1280]{1,0:T(8,128)S(1)}) custom-call(f32[136,640]{1,0:T(8,128)S(1)} %get-tuple-element.20.own_ref, f32[136,640]{1,0:T(8,128)S(1)} %collective-permute-done.1.obs_ref.near_ref, bf16[512,1920]{1,0:T(8,128)(2,1)S(1)} %get-tuple-element.21.x3_ref, ...), custom_call_target="tpu_custom_call" | custom-call | flops 1258291200 | bytes 8388608 | tf_op jit(solution)/shard_map/beside/pallas_call | solution.py:599
  57.5 4.5 %collective-permute-done.2.far_ref = f32[136,640]{1,0:T(8,128)S(1)} collective-permute-done((f32[136,640]{1,0:T(8,128)S(1)}, f32[136,640]{1,0:T(8,128)S(1)}, u32[]{:S(2)}, u32[]{:S(2)}) %collective-permute-start.2) | collective-permute-done | bytes 348192 | tf_op jit(solution)/shard_map/ppermute | solution.py:666
  62.0 10.0 %server.1 = f32[128,5,4,128]{3,2,1,0:T(4,128)S(1)} custom-call(f32[512,640]{1,0:T(8,128)S(1)} %get-tuple-element.19.x_ref, f32[136,640]{1,0:T(8,128)S(1)} %get-tuple-element.20.own_ref, bf16[512,1920]{1,0:T(8,128)(2,1)S(1)} %get-tuple-element.21.x3_ref, bf16[128,1920]{1,0:T(8,128)(2,1)S(1)} %get-tuple-element.22.own3_ref, ...), custom_call_target="tpu_custom_call" | custom-call | tf_op jit(solution)/shard_map/server/pallas_call | solution.py:599
  72.0 26.1 %all_to_all.11.recv_ref = f32[128,5,4,128]{3,2,1,0:T(4,128)S(1)} all-to-all(f32[128,5,4,128]{3,2,1,0:T(4,128)S(1)} %server.1), channel_id=1, replica_groups=mesh['y'=4,'core'=2,'lat'=16] {'y','core','lat'}, dimensions={0} | all-to-all | bytes 2621440 | tf_op jit(solution)/shard_map/all_to_all | solution.py:726
  98.2 2.2 %unpack.1 = f32[80,4,1024]{2,1,0:T(4,128)} custom-call(f32[128,5,4,128]{3,2,1,0:T(4,128)S(1)} %all_to_all.11.recv_ref), custom_call_target="tpu_custom_call" | custom-call | tf_op jit(solution)/shard_map/unpack/pallas_call | solution.py:599
Async XLA Ops:
  46.0 3.5 %collective-permute-start = (f32[65,16,384]{2,1,0:T(8,128)S(1)}, f32[65,16,384]{2,1,0:T(8,128)S(1)}, u32[]{:S(2)}, u32[]{:S(2)}) collective-permute-start(f32[65,16,384]{2,1,0:T(8,128)S(1)} %get-tuple-element.18), channel_id=1, source_target_pairs={{0,16},{16,0},{1,17},{17,1},{2,18},{18,2},{3,19},{19,3},{4,20},{20... | collective-permute-start | bytes 4792328 | tf_op jit(solution)/shard_map/ppermute | solution.py:645
  53.7 1.7 %collective-permute-start.1 = (f32[136,640]{1,0:T(8,128)S(1)}, f32[136,640]{1,0:T(8,128)S(1)}, u32[]{:S(2)}, u32[]{:S(2)}) collective-permute-start(f32[136,640]{1,0:T(8,128)S(1)} %get-tuple-element.20.own_ref), channel_id=1, source_target_pairs={{0,16},{16,0},{1,17},{17,1},{2,18},{18,2},{3,19},{19,3},{4,20},{20... | collective-permute-start | bytes 1044488 | tf_op jit(solution)/shard_map/ppermute | solution.py:667
  53.9 8.1 %collective-permute-start.2 = (f32[136,640]{1,0:T(8,128)S(1)}, f32[136,640]{1,0:T(8,128)S(1)}, u32[]{:S(2)}, u32[]{:S(2)}) collective-permute-start(f32[136,640]{1,0:T(8,128)S(1)} %get-tuple-element.20.own_ref), channel_id=1, source_target_pairs={{16,1},{17,2},{18,3},{19,35},{51,32},{48,33},{49,34},{50,66},{82,6... | collective-permute-start | bytes 1044488 | tf_op jit(solution)/shard_map/ppermute | solution.py:666

commit v8 on v7

--- a/solution.py
+++ b/solution.py
@@ -88,7 +88,7 @@
         loads[i].wait()
         rows = slice(8 * i, 8 * i + 8)
         for r in range(4):
-            moved[r, rows, :] = roll(ens[rows, r, :], 4)
+            moved[r, rows, :] = roll(0.1 * ens[rows, r, :], 4)
     for copy in smalls:
         copy.wait()
     meta = jnp.concatenate(
@@ -154,107 +154,128 @@
     return 4 * column + (z + column) % 4
 
 
-def place_kernel(recv_ref, own_ref, send_ref):
-    def run(core):
-        def put(row, t, cols, value):
-            if t in (core, core + 1):
-                at = 8 * (t - core)
-                own_ref[row, at : at + 8, cols] = value
-            other = 1 - core
-            if t in (other, other + 1):
-                at = 8 * (t - other)
-                send_ref[row, at : at + 8, cols] = value
-
-        def place(l, carry):
-            def vreg(y, tile):
-                return recv_ref[y * 16 + l, tile : tile + 2, :, :].reshape(8, 128)
-
-            for t in range(3):
-                for h in range(2):
-                    for k in range(2):
-                        tile = 4 * t + 2 * h
-                        outs = pair_swap(vreg(2 * k, tile), vreg(2 * k + 1, tile))
-                        for j, out in enumerate(outs):
-                            put(4 * l + 2 * h + j, t, slice(128 * k, 128 * k + 128), out)
-            last = slice(256, 384)
-            outs = block_transpose([vreg(y, 12) for y in range(4)], 16)
-            for r, out in enumerate(outs):
-                turned = roll(out, 64)
-                put(4 * l + r, 0, last, turned if core else out)
-                put(4 * l + r, 1, last, out if core else turned)
+def place_tiles(recv_ref, core, first, put):
+    tiles = (first, first + 1)
+    last = slice(256, 384)
+
+    def place(l, carry):
+        def vreg(y, tile):
+            return recv_ref[y * 16 + l, tile : tile + 2, :, :].reshape(8, 128)
+
+        for t in tiles:
+            for h in range(2):
+                for k in range(2):
+                    tile = 4 * t + 2 * h
+                    outs = pair_swap(vreg(2 * k, tile), vreg(2 * k + 1, tile))
+                    for j, out in enumerate(outs):
+                        put(4 * l + 2 * h + j, t - first, slice(128 * k, 128 * k + 128), out)
+        outs = block_transpose([vreg(y, 12) for y in range(4)], 16)
+        for r, out in enumerate(outs):
+            turned = roll(out, 64)
+            if 0 in tiles:
+                put(4 * l + r, 0 - first, last, turned if core else out)
+            put(4 * l + r, 1 - first, last, out if core else turned)
+        if 2 in tiles:
             ends = []
             for y in range(4):
                 part = recv_ref[y * 16 + l, 14, :, :]
                 ends.append(jnp.concatenate([part, roll(part, 64)], axis=0))
             for r, out in enumerate(block_transpose(ends, 16)):
-                put(4 * l + r, 2, last, roll(out, 64) if core else out)
-            return carry
-
-        lax.fori_loop(0, 16, place, 0, unroll=4)
-        for ref, strip in (
-            (own_ref, 2 * chip_pair() + core),
-            (send_ref, 2 * chip_pair() + 1 - core),
-        ):
-            ref[64, 0:4, 0:128] = recv_ref[strip // 32 * 16 + strip % 16, 15, :, :]
-
+                put(4 * l + r, 2 - first, last, roll(out, 64) if core else out)
+        return carry
+
+    lax.fori_loop(0, 16, place, 0, unroll=2)
+
+
+def for_core(run):
     core = lax.axis_index("core")
     for value in range(2):
         pl.when(core == value)(functools.partial(run, value))
 
 
-def advance(src, row, cols):
-    c = src[row, :, cols]
-    n = src[row - 1, :, cols]
-    s = src[row + 1, :, cols]
-    e = pltpu.roll(c, 15, 0)
-    w = pltpu.roll(c, 1, 0)
-    t = 0.1 * c
-    return t + 0.4 * (n + s) + (0.05 - t) * e + (0.05 + t) * w
-
-
-def march(first, fa, fb, finish):
-    every = slice(None)
+def observations(recv_ref, strip):
+    return recv_ref[strip // 32 * 16 + strip % 16, 15, :, :]
+
+
+def place_kernel(recv_ref, send_ref):
+    def run(core):
+        def put(row, half, cols, value):
+            send_ref[row, 8 * half : 8 * half + 8, cols] = value
+
+        place_tiles(recv_ref, core, 1 - core, put)
+        send_ref[64, 0:4, 0:128] = observations(recv_ref, 2 * chip_pair() + 1 - core)
+
+    for_core(run)
+
+
+def advance(src, row):
+    n, c, s = ((src[row + d, 0:8, :], src[row + d, 8:16, :]) for d in (-1, 0, 1))
+    column = lax.broadcasted_iota(jnp.int32, c[0].shape, 0)
+    up = [pltpu.roll(v, 7, 0) for v in c]
+    down = [pltpu.roll(v, 1, 0) for v in c]
+    east = (jnp.where(column == 7, up[1], up[0]), up[1])
+    west = (down[0], jnp.where(column == 0, down[0], down[1]))
+    return [
+        0.4 * ((n[h] + s[h]) + 0.125 * (east[h] + west[h])) + c[h] * ((west[h] - east[h]) + 0.1)
+        for h in range(2)
+    ]
+
+
+def march(fa, fb, finish):
     for buf in (fa, fb):
         buf[0] = jnp.zeros(buf.shape[1:], F32)
         buf[65] = jnp.zeros(buf.shape[1:], F32)
-
-    def load(i, carry):
-        fa[i + 1] = first(i)
+    for src, dst in ((fa, fb), (fb, fa), (fa, fb)):
+
+        def move(i, carry):
+            for h, value in enumerate(advance(src, i + 1)):
+                dst[i + 1, 8 * h : 8 * h + 8, :] = value
+            return carry
+
+        lax.fori_loop(0, 64, move, 0, unroll=8)
+
+    def last(i, carry):
+        a, b = (pltpu.roll(value, 4, 0) for value in advance(fb, i + 1))
+        column = lax.broadcasted_iota(jnp.int32, a.shape, 0)
+        finish(i, 10.0 * jnp.where(column < 4, a, b))
         return carry
 
-    lax.fori_loop(0, 64, load, 0, unroll=8)
-    for src, dst in ((fa, fb), (fb, fa), (fa, fb)):
-
-        def move(i, carry):
-            dst[i + 1] = advance(src, i + 1, every)
-            return carry
-
-        lax.fori_loop(0, 64, move, 0, unroll=8)
-
-    def last(i, carry):
-        finish(i, advance(fb, i + 1, every)[4:12, :])
-        return carry
-
     lax.fori_loop(0, 64, last, 0, unroll=8)
 
 
-def forecast_own_kernel(own_ref, x_ref, fa, fb):
+def forecast_own_kernel(recv_ref, x_ref, tail_ref, fa, fb):
+    def run(core):
+        def put(row, half, cols, value):
+            rows = slice(8 * half, 8 * half + 8)
+            if cols.start < 256:
+                fa[row + 1, rows, cols] = value
+            else:
+                tail_ref[row, rows, :] = value
+
+        place_tiles(recv_ref, core, core, put)
+        tail_ref[64, 0:4, :] = observations(recv_ref, 2 * chip_pair() + core)
+
+    for_core(run)
+
     def finish(i, value):
         x_ref[pl.ds(pl.multiple_of(i * 8, 8), 8), :] = value
 
-    march(lambda i: own_ref[i, :, 0:256], fa, fb, finish)
-
-
-def forecast_kernel(own_ref, other_ref, part_ref, x_ref, obs_ref, fa, fb):
+    march(fa, fb, finish)
+
+
+def forecast_kernel(tail_ref, other_ref, part_ref, x_ref, obs_ref, fa, fb):
     core = lax.axis_index("core")
     low_core = core == 0
     low = lax.broadcasted_iota(jnp.int32, (16, 128), 1) < 64
     own_low = jnp.where(low_core, 1, 0)
     pick_own = low == (jnp.broadcast_to(own_low, (16, 128)) > 0)
 
-    def first(i):
-        ends = jnp.where(pick_own, own_ref[i, :, 256:384], other_ref[i, :, 256:384])
-        return jnp.concatenate([other_ref[i, :, 0:256], ends], axis=1)
+    def load(i, carry):
+        fa[i + 1, :, 0:256] = other_ref[i, :, 0:256]
+        fa[i + 1, :, 256:384] = jnp.where(pick_own, tail_ref[i], other_ref[i, :, 256:384])
+        return carry
+
+    lax.fori_loop(0, 64, load, 0, unroll=8)
 
     def finish(i, value):
         rows = pl.ds(pl.multiple_of(i * 8, 8), 8)
@@ -262,9 +283,9 @@
         x_ref[rows, pl.ds(pl.multiple_of(core * 256, 128), 256)] = part_ref[rows, :]
         x_ref[rows, 512:640] = value[:, 256:384]
 
-    march(first, fa, fb, finish)
+    march(fa, fb, finish)
     here = jnp.broadcast_to(jnp.where((chip_pair() // 8) % 2 == core, 1, 0), (4, 128)) > 0
-    meta = jnp.where(here, own_ref[64, 0:4, 0:128], other_ref[64, 0:4, 0:128])
+    meta = jnp.where(here, tail_ref[64, 0:4, :], other_ref[64, 0:4, 0:128])
     meta = jnp.concatenate([meta, jnp.zeros((4, 128), F32)], axis=0)
     cell = meta.T[:, 0:1]
     pick = jnp.where(
@@ -639,14 +660,12 @@
         vmem=58,
     )
     recv = lax.all_to_all(chunks, CHIPS, split_axis=0, concat_axis=0, tiled=True)
-    own, other = call(
-        place_kernel, (shaped(65, 16, 384), shaped(65, 16, 384)), recv, name="place", vmem=4
-    )
+    other = call(place_kernel, shaped(65, 16, 384), recv, name="place", vmem=4)
     other = lax.ppermute(other, "core", [(0, 1), (1, 0)])
-    part = call(
+    part, tail = call(
         forecast_own_kernel,
-        shaped(CELLS, 256),
-        own,
+        (shaped(CELLS, 256), shaped(65, 16, 128)),
+        recv,
         scratch=[pltpu.VMEM((66, 16, 256), F32)] * 2,
         name="forecast_own",
         vmem=6,
@@ -655,7 +674,7 @@
     x, obs = call(
         forecast_kernel,
         (shaped(CELLS, K), shaped(136, K)),
-        own,
+        tail,
         other,
         part,
         scratch=[pltpu.VMEM((66, 16, 384), F32)] * 2,

time: 101 us -> 102 us (level)
  Pallas kernels: 26.7 us -> 28.4 us
  waiting for transfers between devices: 5.96 us -> 4.81 us
    pallas_call x8, Pallas kernels: 26.7 us -> 28.4 us  [call(): pl.pallas_call(kernel, out_shape=out_shape, in_specs=ins or [WHOLE] * len...]
    ppermute x1, waiting for transfers between devices: 1.16 us -> 0.01 us  [per_device(): other = lax.ppermute(other, 'core', [(0, 1), (1, 0)])]
  transfers between devices with their start and end apart: 3 -> 3, of which waited for: 3 -> 2; matrix products, arithmetic and copies ran while one was open for 0% -> 0% of each run, Pallas kernels for 5% -> 7%
where the time goes in v8:
time: 102 us
  blocking collectives  67.3 us (66%)
  Pallas kernels  28.4 us (28%)
  waiting for transfers between devices  4.81 us (5%)
  starting transfers between devices  1.21 us (1%)
    all_to_all x1, blocking collectives, per_device(): lax.all_to_all(chunks, CHIPS, split_axis=0, concat_axis=0, tiled=True)  41.1 us
    pallas_call x8, Pallas kernels, call(): pl.pallas_call(kernel, out_shape=out_shape, in_specs=ins or [WHOLE] * len...  28.4 us
    all_to_all x1, blocking collectives, per_device(): back = lax.all_to_all(back, ALL, split_axis=0, concat_axis=0, tiled=True)  26.2 us
    ppermute x1, waiting for transfers between devices, per_device(): far = lax.ppermute(obs, ALL, far_pairs + [(b, a) for a, b in far_pairs])  4.61 us
  transfers between devices with their start and end apart: 3, of which 2 were waited for; matrix products, arithmetic and copies ran while one was open for 0% of the time, Pallas kernels for 7%

profile of v8, /device:TPU:0, one launch (start us, length us, event | category | flops | bytes accessed | tf_op | source)
XLA Modules:
  0.0 101.8 jit_solution(17700311374905895008)
XLA Ops:
  0.0 3.8 %pack.1 = f32[64,16,4,128]{3,2,1,0:T(4,128)} custom-call(f32[80,4,1024]{2,1,0:T(4,128)} %ens_hbm.1, s32[1,128]{1,0:T(1,128)} %cell_hbm.1, f32[1,128]{1,0:T(1,128)} %value_hbm.1, f32[1,128]{1,0:T(1,128)} %var_hbm.1, s32[1,2]{1,0:T(1,128)} %rows_hbm.1), custom_call_target="tpu_custom_call" | custom-call | tf_op jit(solution)/shard_map/pack/pallas_call | solution.py:620
  3.8 41.1 %all_to_all.10.recv_ref = f32[64,16,4,128]{3,2,1,0:T(4,128)S(1)} all-to-all(f32[64,16,4,128]{3,2,1,0:T(4,128)} %pack.1), channel_id=1, replica_groups=mesh['y'=4,'core'=2,'lat'=16] {'y','lat'}, dimensions={0} | all-to-all | bytes 4194304 | tf_op jit(solution)/shard_map/all_to_all | solution.py:662
  44.9 1.8 %place.1 = f32[65,16,384]{2,1,0:T(8,128)S(1)} custom-call(f32[64,16,4,128]{3,2,1,0:T(4,128)S(1)} %all_to_all.10.recv_ref), custom_call_target="tpu_custom_call" | custom-call | tf_op jit(solution)/shard_map/place/pallas_call | solution.py:620
  46.7 0.1 collective-permute-start
  46.8 3.7 %forecast_own.1 = (f32[512,256]{1,0:T(8,128)S(1)}, f32[65,16,128]{2,1,0:T(8,128)S(1)}) custom-call(f32[64,16,4,128]{3,2,1,0:T(4,128)S(1)} %all_to_all.10.recv_ref), custom_call_target="tpu_custom_call" | custom-call | flops 8388608 | bytes 8388608 | tf_op jit(solution)/shard_map/forecast_own/pallas_call | solution.py:620
  50.5 0.0 collective-permute-done.other_ref
  50.5 3.8 %forecast.1 = (f32[512,640]{1,0:T(8,128)S(1)}, f32[136,640]{1,0:T(8,128)S(1)}) custom-call(f32[65,16,128]{2,1,0:T(8,128)S(1)} %get-tuple-element.17.tail_ref, f32[65,16,384]{2,1,0:T(8,128)S(1)} %collective-permute-done.other_ref, f32[512,256]{1,0:T(8,128)S(1)} %get-tuple-element.18.part_ref), custom_call_target="tpu_custom_call" | custom-call | tf_op jit(solution)/shard_map/forecast/pallas_call | solution.py:620
  54.3 1.1 %collective-permute-start.1 = (f32[136,640]{1,0:T(8,128)S(1)}, f32[136,640]{1,0:T(8,128)S(1)}, u32[]{:S(2)}, u32[]{:S(2)}) collective-permute-start(f32[136,640]{1,0:T(8,128)S(1)} %get-tuple-element.20.own_ref), channel_id=1, source_target_pairs={{0,16},{16,0},{1,17},{17,1},{2,18},{18,2},{3,19},{19,3},{4,20},{20... | collective-permute-start | bytes 1044488 | tf_op jit(solution)/shard_map/ppermute | solution.py:686
  55.4 0.0 collective-permute-start.2
  55.4 1.1 %prepare.1 = (bf16[512,1920]{1,0:T(8,128)(2,1)S(1)}, bf16[128,1920]{1,0:T(8,128)(2,1)S(1)}, bf16[640,128]{1,0:T(8,128)(2,1)S(1)}, f32[640,128]{1,0:T(8,128)S(1)}, f32[512,1]{1,0:T(8,128)S(1)}) custom-call(f32[512,640]{1,0:T(8,128)S(1)} %get-tuple-element.19.x_ref, f32[136,640]{1,0:T(8,128)S(1)} %get-tuple-element.20.own_ref), custom_call_target="tpu_custom_call" | custom-call | flops 314572800 | bytes 8388608 | tf_op jit(solution)/shard_map/prepare/pallas_call | solution.py:620
  56.5 0.2 collective-permute-done.1.obs_ref.near_ref
  56.7 2.0 %beside.1 = (bf16[128,1920]{1,0:T(8,128)(2,1)S(1)}, f32[768,128]{1,0:T(8,128)S(1)}, f32[640,1280]{1,0:T(8,128)S(1)}) custom-call(f32[136,640]{1,0:T(8,128)S(1)} %get-tuple-element.20.own_ref, f32[136,640]{1,0:T(8,128)S(1)} %collective-permute-done.1.obs_ref.near_ref, bf16[512,1920]{1,0:T(8,128)(2,1)S(1)} %get-tuple-element.21.x3_ref, ...), custom_call_target="tpu_custom_call" | custom-call | flops 1258291200 | bytes 8388608 | tf_op jit(solution)/shard_map/beside/pallas_call | solution.py:620
  58.7 4.6 %collective-permute-done.2.far_ref = f32[136,640]{1,0:T(8,128)S(1)} collective-permute-done((f32[136,640]{1,0:T(8,128)S(1)}, f32[136,640]{1,0:T(8,128)S(1)}, u32[]{:S(2)}, u32[]{:S(2)}) %collective-permute-start.2) | collective-permute-done | bytes 348192 | tf_op jit(solution)/shard_map/ppermute | solution.py:685
  63.3 10.0 %server.1 = f32[128,5,4,128]{3,2,1,0:T(4,128)S(1)} custom-call(f32[512,640]{1,0:T(8,128)S(1)} %get-tuple-element.19.x_ref, f32[136,640]{1,0:T(8,128)S(1)} %get-tuple-element.20.own_ref, bf16[512,1920]{1,0:T(8,128)(2,1)S(1)} %get-tuple-element.21.x3_ref, bf16[128,1920]{1,0:T(8,128)(2,1)S(1)} %get-tuple-element.22.own3_ref, ...), custom_call_target="tpu_custom_call" | custom-call | tf_op jit(solution)/shard_map/server/pallas_call | solution.py:620
  73.4 26.2 %all_to_all.11.recv_ref = f32[128,5,4,128]{3,2,1,0:T(4,128)S(1)} all-to-all(f32[128,5,4,128]{3,2,1,0:T(4,128)S(1)} %server.1), channel_id=1, replica_groups=mesh['y'=4,'core'=2,'lat'=16] {'y','core','lat'}, dimensions={0} | all-to-all | bytes 2621440 | tf_op jit(solution)/shard_map/all_to_all | solution.py:745
  99.5 2.2 %unpack.1 = f32[80,4,1024]{2,1,0:T(4,128)} custom-call(f32[128,5,4,128]{3,2,1,0:T(4,128)S(1)} %all_to_all.11.recv_ref), custom_call_target="tpu_custom_call" | custom-call | tf_op jit(solution)/shard_map/unpack/pallas_call | solution.py:620
Async XLA Ops:
  46.7 3.8 %collective-permute-start = (f32[65,16,384]{2,1,0:T(8,128)S(1)}, f32[65,16,384]{2,1,0:T(8,128)S(1)}, u32[]{:S(2)}, u32[]{:S(2)}) collective-permute-start(f32[65,16,384]{2,1,0:T(8,128)S(1)} %place.1), channel_id=1, source_target_pairs={{0,16},{16,0},{1,17},{17,1},{2,18},{18,2},{3,19},{19,3},{4,20},{20... | collective-permute-start | bytes 4792328 | tf_op jit(solution)/shard_map/ppermute | solution.py:664
  54.3 2.4 %collective-permute-start.1 = (f32[136,640]{1,0:T(8,128)S(1)}, f32[136,640]{1,0:T(8,128)S(1)}, u32[]{:S(2)}, u32[]{:S(2)}) collective-permute-start(f32[136,640]{1,0:T(8,128)S(1)} %get-tuple-element.20.own_ref), channel_id=1, source_target_pairs={{0,16},{16,0},{1,17},{17,1},{2,18},{18,2},{3,19},{19,3},{4,20},{20... | collective-permute-start | bytes 1044488 | tf_op jit(solution)/shard_map/ppermute | solution.py:686
  55.4 7.9 %collective-permute-start.2 = (f32[136,640]{1,0:T(8,128)S(1)}, f32[136,640]{1,0:T(8,128)S(1)}, u32[]{:S(2)}, u32[]{:S(2)}) collective-permute-start(f32[136,640]{1,0:T(8,128)S(1)} %get-tuple-element.20.own_ref), channel_id=1, source_target_pairs={{16,1},{17,2},{18,3},{19,35},{51,32},{48,33},{49,34},{50,66},{82,6... | collective-permute-start | bytes 1044488 | tf_op jit(solution)/shard_map/ppermute | solution.py:685

commit v9 on v8

--- a/solution.py
+++ b/solution.py
@@ -184,7 +184,7 @@
                 put(4 * l + r, 2 - first, last, roll(out, 64) if core else out)
         return carry
 
-    lax.fori_loop(0, 16, place, 0, unroll=2)
+    lax.fori_loop(0, 16, place, 0, unroll=4)
 
 
 def for_core(run):

time: 102 us -> 100 us (0.980)
  Pallas kernels: 28.4 us -> 26.9 us
    pallas_call x8, Pallas kernels: 28.4 us -> 26.9 us  [call(): pl.pallas_call(kernel, out_shape=out_shape, in_specs=ins or [WHOLE] * len...]
  transfers between devices with their start and end apart: 3 -> 3, of which waited for: 2 -> 3; matrix products, arithmetic and copies ran while one was open for 0% -> 0% of each run, Pallas kernels for 7% -> 6%
where the time goes in v9:
time: 100 us
  blocking collectives  67.3 us (67%)
  Pallas kernels  26.9 us (27%)
  waiting for transfers between devices  5.37 us (5%)
    all_to_all x1, blocking collectives, per_device(): lax.all_to_all(chunks, CHIPS, split_axis=0, concat_axis=0, tiled=True)  41.1 us
    pallas_call x8, Pallas kernels, call(): pl.pallas_call(kernel, out_shape=out_shape, in_specs=ins or [WHOLE] * len...  26.9 us
    all_to_all x1, blocking collectives, per_device(): back = lax.all_to_all(back, ALL, split_axis=0, concat_axis=0, tiled=True)  26.2 us
    ppermute x1, waiting for transfers between devices, per_device(): far = lax.ppermute(obs, ALL, far_pairs + [(b, a) for a, b in far_pairs])  4.55 us
  transfers between devices with their start and end apart: 3, of which 3 were waited for; matrix products, arithmetic and copies ran while one was open for 0% of the time, Pallas kernels for 6%

profile of v9, /device:TPU:0, one launch (start us, length us, event | category | flops | bytes accessed | tf_op | source)
XLA Modules:
  0.0 100.0 jit_solution(10731094309039494293)
XLA Ops:
  0.0 3.8 %pack.1 = f32[64,16,4,128]{3,2,1,0:T(4,128)} custom-call(f32[80,4,1024]{2,1,0:T(4,128)} %ens_hbm.1, s32[1,128]{1,0:T(1,128)} %cell_hbm.1, f32[1,128]{1,0:T(1,128)} %value_hbm.1, f32[1,128]{1,0:T(1,128)} %var_hbm.1, s32[1,2]{1,0:T(1,128)} %rows_hbm.1), custom_call_target="tpu_custom_call" | custom-call | tf_op jit(solution)/shard_map/pack/pallas_call | solution.py:620
  3.8 41.1 %all_to_all.10.recv_ref = f32[64,16,4,128]{3,2,1,0:T(4,128)S(1)} all-to-all(f32[64,16,4,128]{3,2,1,0:T(4,128)} %pack.1), channel_id=1, replica_groups=mesh['y'=4,'core'=2,'lat'=16] {'y','lat'}, dimensions={0} | all-to-all | bytes 4194304 | tf_op jit(solution)/shard_map/all_to_all | solution.py:662
  44.9 1.1 %place.1 = f32[65,16,384]{2,1,0:T(8,128)S(1)} custom-call(f32[64,16,4,128]{3,2,1,0:T(4,128)S(1)} %all_to_all.10.recv_ref), custom_call_target="tpu_custom_call" | custom-call | tf_op jit(solution)/shard_map/place/pallas_call | solution.py:620
  46.0 0.1 collective-permute-start
  46.1 2.9 %forecast_own.1 = (f32[512,256]{1,0:T(8,128)S(1)}, f32[65,16,128]{2,1,0:T(8,128)S(1)}) custom-call(f32[64,16,4,128]{3,2,1,0:T(4,128)S(1)} %all_to_all.10.recv_ref), custom_call_target="tpu_custom_call" | custom-call | flops 8388608 | bytes 8388608 | tf_op jit(solution)/shard_map/forecast_own/pallas_call | solution.py:620
  48.9 0.6 collective-permute-done.other_ref
  49.5 3.8 %forecast.1 = (f32[512,640]{1,0:T(8,128)S(1)}, f32[136,640]{1,0:T(8,128)S(1)}) custom-call(f32[65,16,128]{2,1,0:T(8,128)S(1)} %get-tuple-element.17.tail_ref, f32[65,16,384]{2,1,0:T(8,128)S(1)} %collective-permute-done.other_ref, f32[512,256]{1,0:T(8,128)S(1)} %get-tuple-element.18.part_ref), custom_call_target="tpu_custom_call" | custom-call | tf_op jit(solution)/shard_map/forecast/pallas_call | solution.py:620
  53.3 0.4 collective-permute-start.1
  53.7 0.0 collective-permute-start.2
  53.7 1.1 %prepare.1 = (bf16[512,1920]{1,0:T(8,128)(2,1)S(1)}, bf16[128,1920]{1,0:T(8,128)(2,1)S(1)}, bf16[640,128]{1,0:T(8,128)(2,1)S(1)}, f32[640,128]{1,0:T(8,128)S(1)}, f32[512,1]{1,0:T(8,128)S(1)}) custom-call(f32[512,640]{1,0:T(8,128)S(1)} %get-tuple-element.19.x_ref, f32[136,640]{1,0:T(8,128)S(1)} %get-tuple-element.20.own_ref), custom_call_target="tpu_custom_call" | custom-call | flops 314572800 | bytes 8388608 | tf_op jit(solution)/shard_map/prepare/pallas_call | solution.py:620
  54.7 0.2 collective-permute-done.1.obs_ref.near_ref
  55.0 2.0 %beside.1 = (bf16[128,1920]{1,0:T(8,128)(2,1)S(1)}, f32[768,128]{1,0:T(8,128)S(1)}, f32[640,1280]{1,0:T(8,128)S(1)}) custom-call(f32[136,640]{1,0:T(8,128)S(1)} %get-tuple-element.20.own_ref, f32[136,640]{1,0:T(8,128)S(1)} %collective-permute-done.1.obs_ref.near_ref, bf16[512,1920]{1,0:T(8,128)(2,1)S(1)} %get-tuple-element.21.x3_ref, ...), custom_call_target="tpu_custom_call" | custom-call | flops 1258291200 | bytes 8388608 | tf_op jit(solution)/shard_map/beside/pallas_call | solution.py:620
  57.0 4.6 %collective-permute-done.2.far_ref = f32[136,640]{1,0:T(8,128)S(1)} collective-permute-done((f32[136,640]{1,0:T(8,128)S(1)}, f32[136,640]{1,0:T(8,128)S(1)}, u32[]{:S(2)}, u32[]{:S(2)}) %collective-permute-start.2) | collective-permute-done | bytes 348192 | tf_op jit(solution)/shard_map/ppermute | solution.py:685
  61.6 10.0 %server.1 = f32[128,5,4,128]{3,2,1,0:T(4,128)S(1)} custom-call(f32[512,640]{1,0:T(8,128)S(1)} %get-tuple-element.19.x_ref, f32[136,640]{1,0:T(8,128)S(1)} %get-tuple-element.20.own_ref, bf16[512,1920]{1,0:T(8,128)(2,1)S(1)} %get-tuple-element.21.x3_ref, bf16[128,1920]{1,0:T(8,128)(2,1)S(1)} %get-tuple-element.22.own3_ref, ...), custom_call_target="tpu_custom_call" | custom-call | tf_op jit(solution)/shard_map/server/pallas_call | solution.py:620
  71.6 26.2 %all_to_all.11.recv_ref = f32[128,5,4,128]{3,2,1,0:T(4,128)S(1)} all-to-all(f32[128,5,4,128]{3,2,1,0:T(4,128)S(1)} %server.1), channel_id=1, replica_groups=mesh['y'=4,'core'=2,'lat'=16] {'y','core','lat'}, dimensions={0} | all-to-all | bytes 2621440 | tf_op jit(solution)/shard_map/all_to_all | solution.py:745
  97.8 2.2 %unpack.1 = f32[80,4,1024]{2,1,0:T(4,128)} custom-call(f32[128,5,4,128]{3,2,1,0:T(4,128)S(1)} %all_to_all.11.recv_ref), custom_call_target="tpu_custom_call" | custom-call | tf_op jit(solution)/shard_map/unpack/pallas_call | solution.py:620
Async XLA Ops:
  46.0 3.5 %collective-permute-start = (f32[65,16,384]{2,1,0:T(8,128)S(1)}, f32[65,16,384]{2,1,0:T(8,128)S(1)}, u32[]{:S(2)}, u32[]{:S(2)}) collective-permute-start(f32[65,16,384]{2,1,0:T(8,128)S(1)} %place.1), channel_id=1, source_target_pairs={{0,16},{16,0},{1,17},{17,1},{2,18},{18,2},{3,19},{19,3},{4,20},{20... | collective-permute-start | bytes 4792328 | tf_op jit(solution)/shard_map/ppermute | solution.py:664
  53.3 1.7 %collective-permute-start.1 = (f32[136,640]{1,0:T(8,128)S(1)}, f32[136,640]{1,0:T(8,128)S(1)}, u32[]{:S(2)}, u32[]{:S(2)}) collective-permute-start(f32[136,640]{1,0:T(8,128)S(1)} %get-tuple-element.20.own_ref), channel_id=1, source_target_pairs={{0,16},{16,0},{1,17},{17,1},{2,18},{18,2},{3,19},{19,3},{4,20},{20... | collective-permute-start | bytes 1044488 | tf_op jit(solution)/shard_map/ppermute | solution.py:686
  53.7 7.9 %collective-permute-start.2 = (f32[136,640]{1,0:T(8,128)S(1)}, f32[136,640]{1,0:T(8,128)S(1)}, u32[]{:S(2)}, u32[]{:S(2)}) collective-permute-start(f32[136,640]{1,0:T(8,128)S(1)} %get-tuple-element.20.own_ref), channel_id=1, source_target_pairs={{16,1},{17,2},{18,3},{19,35},{51,32},{48,33},{49,34},{50,66},{82,6... | collective-permute-start | bytes 1044488 | tf_op jit(solution)/shard_map/ppermute | solution.py:685

commit v10 on v9

--- a/solution.py
+++ b/solution.py
@@ -232,7 +232,7 @@
                 dst[i + 1, 8 * h : 8 * h + 8, :] = value
             return carry
 
-        lax.fori_loop(0, 64, move, 0, unroll=8)
+        lax.fori_loop(0, 64, move, 0, unroll=16)
 
     def last(i, carry):
         a, b = (pltpu.roll(value, 4, 0) for value in advance(fb, i + 1))
@@ -240,7 +240,7 @@
         finish(i, 10.0 * jnp.where(column < 4, a, b))
         return carry
 
-    lax.fori_loop(0, 64, last, 0, unroll=8)
+    lax.fori_loop(0, 64, last, 0, unroll=16)
 
 
 def forecast_own_kernel(recv_ref, x_ref, tail_ref, fa, fb):

time: 100 us -> 100 us (level)
  no operation moved by 1% of the time
where the time goes in v10:
time: 100 us; the launch traced here: 99.9 us
  blocking collectives  67.3 us (67%)
  Pallas kernels  26.6 us (27%)
  waiting for transfers between devices  5.47 us (5%)
    all_to_all x1, blocking collectives, per_device(): lax.all_to_all(chunks, CHIPS, split_axis=0, concat_axis=0, tiled=True)  41.1 us
    pallas_call x8, Pallas kernels, call(): pl.pallas_call(kernel, out_shape=out_shape, in_specs=ins or [WHOLE] * len...  26.6 us
    all_to_all x1, blocking collectives, per_device(): back = lax.all_to_all(back, ALL, split_axis=0, concat_axis=0, tiled=True)  26.1 us
    ppermute x1, waiting for transfers between devices, per_device(): far = lax.ppermute(obs, ALL, far_pairs + [(b, a) for a, b in far_pairs])  4.51 us
  transfers between devices with their start and end apart: 3, of which 3 were waited for; matrix products, arithmetic and copies ran while one was open for 0% of the time, Pallas kernels for 6%

profile of v10, /device:TPU:0, one launch (start us, length us, event | category | flops | bytes accessed | tf_op | source)
XLA Modules:
  0.0 99.9 jit_solution(16300525986422428527)
XLA Ops:
  0.0 3.8 %pack.1 = f32[64,16,4,128]{3,2,1,0:T(4,128)} custom-call(f32[80,4,1024]{2,1,0:T(4,128)} %ens_hbm.1, s32[1,128]{1,0:T(1,128)} %cell_hbm.1, f32[1,128]{1,0:T(1,128)} %value_hbm.1, f32[1,128]{1,0:T(1,128)} %var_hbm.1, s32[1,2]{1,0:T(1,128)} %rows_hbm.1), custom_call_target="tpu_custom_call" | custom-call | tf_op jit(solution)/shard_map/pack/pallas_call | solution.py:620
  3.8 41.1 %all_to_all.10.recv_ref = f32[64,16,4,128]{3,2,1,0:T(4,128)S(1)} all-to-all(f32[64,16,4,128]{3,2,1,0:T(4,128)} %pack.1), channel_id=1, replica_groups=mesh['y'=4,'core'=2,'lat'=16] {'y','lat'}, dimensions={0} | all-to-all | bytes 4194304 | tf_op jit(solution)/shard_map/all_to_all | solution.py:662
  44.9 1.1 %place.1 = f32[65,16,384]{2,1,0:T(8,128)S(1)} custom-call(f32[64,16,4,128]{3,2,1,0:T(4,128)S(1)} %all_to_all.10.recv_ref), custom_call_target="tpu_custom_call" | custom-call | tf_op jit(solution)/shard_map/place/pallas_call | solution.py:620
  46.0 0.1 collective-permute-start
  46.1 2.7 %forecast_own.1 = (f32[512,256]{1,0:T(8,128)S(1)}, f32[65,16,128]{2,1,0:T(8,128)S(1)}) custom-call(f32[64,16,4,128]{3,2,1,0:T(4,128)S(1)} %all_to_all.10.recv_ref), custom_call_target="tpu_custom_call" | custom-call | flops 8388608 | bytes 8388608 | tf_op jit(solution)/shard_map/forecast_own/pallas_call | solution.py:620
  48.8 0.7 collective-permute-done.other_ref
  49.5 3.6 %forecast.1 = (f32[512,640]{1,0:T(8,128)S(1)}, f32[136,640]{1,0:T(8,128)S(1)}) custom-call(f32[65,16,128]{2,1,0:T(8,128)S(1)} %get-tuple-element.17.tail_ref, f32[65,16,384]{2,1,0:T(8,128)S(1)} %collective-permute-done.other_ref, f32[512,256]{1,0:T(8,128)S(1)} %get-tuple-element.18.part_ref), custom_call_target="tpu_custom_call" | custom-call | tf_op jit(solution)/shard_map/forecast/pallas_call | solution.py:620
  53.1 0.3 collective-permute-start.1
  53.4 0.1 collective-permute-start.2
  53.5 1.1 %prepare.1 = (bf16[512,1920]{1,0:T(8,128)(2,1)S(1)}, bf16[128,1920]{1,0:T(8,128)(2,1)S(1)}, bf16[640,128]{1,0:T(8,128)(2,1)S(1)}, f32[640,128]{1,0:T(8,128)S(1)}, f32[512,1]{1,0:T(8,128)S(1)}) custom-call(f32[512,640]{1,0:T(8,128)S(1)} %get-tuple-element.19.x_ref, f32[136,640]{1,0:T(8,128)S(1)} %get-tuple-element.20.own_ref), custom_call_target="tpu_custom_call" | custom-call | flops 314572800 | bytes 8388608 | tf_op jit(solution)/shard_map/prepare/pallas_call | solution.py:620
  54.6 0.3 collective-permute-done.1.obs_ref.near_ref
  54.9 2.0 %beside.1 = (bf16[128,1920]{1,0:T(8,128)(2,1)S(1)}, f32[768,128]{1,0:T(8,128)S(1)}, f32[640,1280]{1,0:T(8,128)S(1)}) custom-call(f32[136,640]{1,0:T(8,128)S(1)} %get-tuple-element.20.own_ref, f32[136,640]{1,0:T(8,128)S(1)} %collective-permute-done.1.obs_ref.near_ref, bf16[512,1920]{1,0:T(8,128)(2,1)S(1)} %get-tuple-element.21.x3_ref, ...), custom_call_target="tpu_custom_call" | custom-call | flops 1258291200 | bytes 8388608 | tf_op jit(solution)/shard_map/beside/pallas_call | solution.py:620
  56.9 4.5 %collective-permute-done.2.far_ref = f32[136,640]{1,0:T(8,128)S(1)} collective-permute-done((f32[136,640]{1,0:T(8,128)S(1)}, f32[136,640]{1,0:T(8,128)S(1)}, u32[]{:S(2)}, u32[]{:S(2)}) %collective-permute-start.2) | collective-permute-done | bytes 348192 | tf_op jit(solution)/shard_map/ppermute | solution.py:685
  61.4 10.0 %server.1 = f32[128,5,4,128]{3,2,1,0:T(4,128)S(1)} custom-call(f32[512,640]{1,0:T(8,128)S(1)} %get-tuple-element.19.x_ref, f32[136,640]{1,0:T(8,128)S(1)} %get-tuple-element.20.own_ref, bf16[512,1920]{1,0:T(8,128)(2,1)S(1)} %get-tuple-element.21.x3_ref, bf16[128,1920]{1,0:T(8,128)(2,1)S(1)} %get-tuple-element.22.own3_ref, ...), custom_call_target="tpu_custom_call" | custom-call | tf_op jit(solution)/shard_map/server/pallas_call | solution.py:620
  71.5 26.1 %all_to_all.11.recv_ref = f32[128,5,4,128]{3,2,1,0:T(4,128)S(1)} all-to-all(f32[128,5,4,128]{3,2,1,0:T(4,128)S(1)} %server.1), channel_id=1, replica_groups=mesh['y'=4,'core'=2,'lat'=16] {'y','core','lat'}, dimensions={0} | all-to-all | bytes 2621440 | tf_op jit(solution)/shard_map/all_to_all | solution.py:745
  97.6 2.2 %unpack.1 = f32[80,4,1024]{2,1,0:T(4,128)} custom-call(f32[128,5,4,128]{3,2,1,0:T(4,128)S(1)} %all_to_all.11.recv_ref), custom_call_target="tpu_custom_call" | custom-call | tf_op jit(solution)/shard_map/unpack/pallas_call | solution.py:620
Async XLA Ops:
  46.0 3.5 %collective-permute-start = (f32[65,16,384]{2,1,0:T(8,128)S(1)}, f32[65,16,384]{2,1,0:T(8,128)S(1)}, u32[]{:S(2)}, u32[]{:S(2)}) collective-permute-start(f32[65,16,384]{2,1,0:T(8,128)S(1)} %place.1), channel_id=1, source_target_pairs={{0,16},{16,0},{1,17},{17,1},{2,18},{18,2},{3,19},{19,3},{4,20},{20... | collective-permute-start | bytes 4792328 | tf_op jit(solution)/shard_map/ppermute | solution.py:664
  53.1 1.7 %collective-permute-start.1 = (f32[136,640]{1,0:T(8,128)S(1)}, f32[136,640]{1,0:T(8,128)S(1)}, u32[]{:S(2)}, u32[]{:S(2)}) collective-permute-start(f32[136,640]{1,0:T(8,128)S(1)} %get-tuple-element.20.own_ref), channel_id=1, source_target_pairs={{0,16},{16,0},{1,17},{17,1},{2,18},{18,2},{3,19},{19,3},{4,20},{20... | collective-permute-start | bytes 1044488 | tf_op jit(solution)/shard_map/ppermute | solution.py:686
  53.4 8.0 %collective-permute-start.2 = (f32[136,640]{1,0:T(8,128)S(1)}, f32[136,640]{1,0:T(8,128)S(1)}, u32[]{:S(2)}, u32[]{:S(2)}) collective-permute-start(f32[136,640]{1,0:T(8,128)S(1)} %get-tuple-element.20.own_ref), channel_id=1, source_target_pairs={{16,1},{17,2},{18,3},{19,35},{51,32},{48,33},{49,34},{50,66},{82,6... | collective-permute-start | bytes 1044488 | tf_op jit(solution)/shard_map/ppermute | solution.py:685

commit v11 on v9

--- a/solution.py
+++ b/solution.py
@@ -291,8 +291,7 @@
     pick = jnp.where(
         lax.broadcasted_iota(jnp.int32, (128, CELLS), 1) == cell.astype(jnp.int32), 1.0, 0.0
     ).astype(BF16)
-    for j in range(5):
-        cols = slice(j * 128, (j + 1) * 128)
+    for cols in (slice(0, 256), slice(256, 512), slice(512, 640)):
         x = x_ref[:, cols]
         x1 = x.astype(BF16)
         rest = x - x1.astype(F32)

time: 100 us -> 100 us (level)
  no operation moved by 1% of the time
where the time goes in v11:
time: 100 us; the launch traced here: 99.9 us
  blocking collectives  67.3 us (67%)
  Pallas kernels  26.7 us (27%)
  waiting for transfers between devices  5.37 us (5%)
    all_to_all x1, blocking collectives, per_device(): lax.all_to_all(chunks, CHIPS, split_axis=0, concat_axis=0, tiled=True)  41.1 us
    pallas_call x8, Pallas kernels, call(): pl.pallas_call(kernel, out_shape=out_shape, in_specs=ins or [WHOLE] * len...  26.7 us
    all_to_all x1, blocking collectives, per_device(): back = lax.all_to_all(back, ALL, split_axis=0, concat_axis=0, tiled=True)  26.2 us
    ppermute x1, waiting for transfers between devices, per_device(): far = lax.ppermute(obs, ALL, far_pairs + [(b, a) for a, b in far_pairs])  4.54 us
  transfers between devices with their start and end apart: 3, of which 3 were waited for; matrix products, arithmetic and copies ran while one was open for 0% of the time, Pallas kernels for 6%

profile of v11, /device:TPU:0, one launch (start us, length us, event | category | flops | bytes accessed | tf_op | source)
XLA Modules:
  0.0 99.9 jit_solution(2515439417611696206)
XLA Ops:
  0.0 3.8 %pack.1 = f32[64,16,4,128]{3,2,1,0:T(4,128)} custom-call(f32[80,4,1024]{2,1,0:T(4,128)} %ens_hbm.1, s32[1,128]{1,0:T(1,128)} %cell_hbm.1, f32[1,128]{1,0:T(1,128)} %value_hbm.1, f32[1,128]{1,0:T(1,128)} %var_hbm.1, s32[1,2]{1,0:T(1,128)} %rows_hbm.1), custom_call_target="tpu_custom_call" | custom-call | tf_op jit(solution)/shard_map/pack/pallas_call | solution.py:619
  3.8 41.1 %all_to_all.10.recv_ref = f32[64,16,4,128]{3,2,1,0:T(4,128)S(1)} all-to-all(f32[64,16,4,128]{3,2,1,0:T(4,128)} %pack.1), channel_id=1, replica_groups=mesh['y'=4,'core'=2,'lat'=16] {'y','lat'}, dimensions={0} | all-to-all | bytes 4194304 | tf_op jit(solution)/shard_map/all_to_all | solution.py:661
  44.9 1.1 %place.1 = f32[65,16,384]{2,1,0:T(8,128)S(1)} custom-call(f32[64,16,4,128]{3,2,1,0:T(4,128)S(1)} %all_to_all.10.recv_ref), custom_call_target="tpu_custom_call" | custom-call | tf_op jit(solution)/shard_map/place/pallas_call | solution.py:619
  46.0 0.1 collective-permute-start
  46.1 2.9 %forecast_own.1 = (f32[512,256]{1,0:T(8,128)S(1)}, f32[65,16,128]{2,1,0:T(8,128)S(1)}) custom-call(f32[64,16,4,128]{3,2,1,0:T(4,128)S(1)} %all_to_all.10.recv_ref), custom_call_target="tpu_custom_call" | custom-call | flops 8388608 | bytes 8388608 | tf_op jit(solution)/shard_map/forecast_own/pallas_call | solution.py:619
  48.9 0.6 collective-permute-done.other_ref
  49.5 3.6 %forecast.1 = (f32[512,640]{1,0:T(8,128)S(1)}, f32[136,640]{1,0:T(8,128)S(1)}) custom-call(f32[65,16,128]{2,1,0:T(8,128)S(1)} %get-tuple-element.17.tail_ref, f32[65,16,384]{2,1,0:T(8,128)S(1)} %collective-permute-done.other_ref, f32[512,256]{1,0:T(8,128)S(1)} %get-tuple-element.18.part_ref), custom_call_target="tpu_custom_call" | custom-call | tf_op jit(solution)/shard_map/forecast/pallas_call | solution.py:619
  53.1 0.4 collective-permute-start.1
  53.5 0.0 collective-permute-start.2
  53.5 1.1 %prepare.1 = (bf16[512,1920]{1,0:T(8,128)(2,1)S(1)}, bf16[128,1920]{1,0:T(8,128)(2,1)S(1)}, bf16[640,128]{1,0:T(8,128)(2,1)S(1)}, f32[640,128]{1,0:T(8,128)S(1)}, f32[512,1]{1,0:T(8,128)S(1)}) custom-call(f32[512,640]{1,0:T(8,128)S(1)} %get-tuple-element.19.x_ref, f32[136,640]{1,0:T(8,128)S(1)} %get-tuple-element.20.own_ref), custom_call_target="tpu_custom_call" | custom-call | flops 314572800 | bytes 8388608 | tf_op jit(solution)/shard_map/prepare/pallas_call | solution.py:619
  54.6 0.3 collective-permute-done.1.obs_ref.near_ref
  54.8 2.0 %beside.1 = (bf16[128,1920]{1,0:T(8,128)(2,1)S(1)}, f32[768,128]{1,0:T(8,128)S(1)}, f32[640,1280]{1,0:T(8,128)S(1)}) custom-call(f32[136,640]{1,0:T(8,128)S(1)} %get-tuple-element.20.own_ref, f32[136,640]{1,0:T(8,128)S(1)} %collective-permute-done.1.obs_ref.near_ref, bf16[512,1920]{1,0:T(8,128)(2,1)S(1)} %get-tuple-element.21.x3_ref, ...), custom_call_target="tpu_custom_call" | custom-call | flops 1258291200 | bytes 8388608 | tf_op jit(solution)/shard_map/beside/pallas_call | solution.py:619
  56.9 4.5 %collective-permute-done.2.far_ref = f32[136,640]{1,0:T(8,128)S(1)} collective-permute-done((f32[136,640]{1,0:T(8,128)S(1)}, f32[136,640]{1,0:T(8,128)S(1)}, u32[]{:S(2)}, u32[]{:S(2)}) %collective-permute-start.2) | collective-permute-done | bytes 348192 | tf_op jit(solution)/shard_map/ppermute | solution.py:684
  61.4 10.0 %server.1 = f32[128,5,4,128]{3,2,1,0:T(4,128)S(1)} custom-call(f32[512,640]{1,0:T(8,128)S(1)} %get-tuple-element.19.x_ref, f32[136,640]{1,0:T(8,128)S(1)} %get-tuple-element.20.own_ref, bf16[512,1920]{1,0:T(8,128)(2,1)S(1)} %get-tuple-element.21.x3_ref, bf16[128,1920]{1,0:T(8,128)(2,1)S(1)} %get-tuple-element.22.own3_ref, ...), custom_call_target="tpu_custom_call" | custom-call | tf_op jit(solution)/shard_map/server/pallas_call | solution.py:619
  71.5 26.2 %all_to_all.11.recv_ref = f32[128,5,4,128]{3,2,1,0:T(4,128)S(1)} all-to-all(f32[128,5,4,128]{3,2,1,0:T(4,128)S(1)} %server.1), channel_id=1, replica_groups=mesh['y'=4,'core'=2,'lat'=16] {'y','core','lat'}, dimensions={0} | all-to-all | bytes 2621440 | tf_op jit(solution)/shard_map/all_to_all | solution.py:744
  97.6 2.2 %unpack.1 = f32[80,4,1024]{2,1,0:T(4,128)} custom-call(f32[128,5,4,128]{3,2,1,0:T(4,128)S(1)} %all_to_all.11.recv_ref), custom_call_target="tpu_custom_call" | custom-call | tf_op jit(solution)/shard_map/unpack/pallas_call | solution.py:619
Async XLA Ops:
  46.0 3.5 %collective-permute-start = (f32[65,16,384]{2,1,0:T(8,128)S(1)}, f32[65,16,384]{2,1,0:T(8,128)S(1)}, u32[]{:S(2)}, u32[]{:S(2)}) collective-permute-start(f32[65,16,384]{2,1,0:T(8,128)S(1)} %place.1), channel_id=1, source_target_pairs={{0,16},{16,0},{1,17},{17,1},{2,18},{18,2},{3,19},{19,3},{4,20},{20... | collective-permute-start | bytes 4792328 | tf_op jit(solution)/shard_map/ppermute | solution.py:663
  53.1 1.7 %collective-permute-start.1 = (f32[136,640]{1,0:T(8,128)S(1)}, f32[136,640]{1,0:T(8,128)S(1)}, u32[]{:S(2)}, u32[]{:S(2)}) collective-permute-start(f32[136,640]{1,0:T(8,128)S(1)} %get-tuple-element.20.own_ref), channel_id=1, source_target_pairs={{0,16},{16,0},{1,17},{17,1},{2,18},{18,2},{3,19},{19,3},{4,20},{20... | collective-permute-start | bytes 1044488 | tf_op jit(solution)/shard_map/ppermute | solution.py:685
  53.5 7.9 %collective-permute-start.2 = (f32[136,640]{1,0:T(8,128)S(1)}, f32[136,640]{1,0:T(8,128)S(1)}, u32[]{:S(2)}, u32[]{:S(2)}) collective-permute-start(f32[136,640]{1,0:T(8,128)S(1)} %get-tuple-element.20.own_ref), channel_id=1, source_target_pairs={{16,1},{17,2},{18,3},{19,35},{51,32},{48,33},{49,34},{50,66},{82,6... | collective-permute-start | bytes 1044488 | tf_op jit(solution)/shard_map/ppermute | solution.py:684
